TPU v7x, 32 devices: a whole 2x2x4 slice. The times are simulated.
32 devices in a mesh: dp: 4 (over y, x), expert: 8 (over z, core).
Axes of the slice: x: 2, y: 2, z: 4, core: 2. Of those that a mesh axis runs over, the one named last changes fastest.
Arguments:
- tokens: bfloat16 [32768, 768], P(('dp', 'expert')), may hold values from -6 to 6
- cotangent: bfloat16 [32768, 768], P(('dp', 'expert')), may hold values from -6 to 6
- seg_start: int32 [32768], P(('dp', 'expert')), may hold values from 0 to 1023, as said below
- dispatch_slot: int32 [32768], P(('dp', 'expert')), may hold values from 0 to 2048, as said below
- ln1_gain: float32 [768], replicated, may hold values from 0.25 to 1.75
- ln1_shift: float32 [768], replicated, may hold values from -3 to 3
- w_qkv: bfloat16 [768, 2304], replicated, may hold values from -0.21875 to 0.21875
- w_attn_out: bfloat16 [768, 768], replicated, may hold values from -0.875 to 0.875
- ln2_gain: float32 [768], replicated, may hold values from 0.25 to 1.75
- ln2_shift: float32 [768], replicated, may hold values from -3 to 3
- w_in: bfloat16 [2, 768, 3072], replicated, may hold values from -0.21875 to 0.21875
- w_out: bfloat16 [2, 3072, 768], replicated, may hold values from -0.109375 to 0.109375
Outputs:
- result_out: bfloat16 [32768, 768], P(('dp', 'expert'))
- grad_tokens: float32 [32768, 768], P(('dp', 'expert'))
- grad_ln1_gain: float32 [768], replicated
- grad_ln1_shift: float32 [768], replicated
- grad_w_qkv: float32 [768, 2304], replicated
- grad_w_attn_out: float32 [768, 768], replicated
- grad_ln2_gain: float32 [768], replicated
- grad_ln2_shift: float32 [768], replicated
- grad_w_in: float32 [2, 768, 3072], P(None, None, 'expert')
- grad_w_out: float32 [2, 3072, 768], P(None, 'expert')
- expert_counts: int32 [2], replicated
Inputs may be any that keep to these rules, and one draw needn't show every extreme that they name: A row is an image row or a caption row. An image row's first 985 slots hold 5 images of 197 patches each, its other slots are padding, each padding token a segment of its own; a caption row is filled with captions. A token attends only to tokens of its own row with the same seg_start. `dispatch_slot`: slot s sends the token to the device at expert index s // 256 of its dp index, at place s % 256. Image tokens go to expert indices below 4, caption tokens to the others; no two tokens of one device share a slot; padding tokens, and only they, have s = 2048.
All inputs are finite; a program needn't handle non-finite values.
Results may differ from a plain program's by a relative error of at most 0.012.
Values may be sent and summed in bfloat16 or wider, within the bound.
No kernel may reach another device: no remote copies, remote signals or barrier semaphores. Data moves between devices by JAX's collectives and lax.ppermute only.
A program may use at most 320 MiB of HBM per device.

v0:
```python
import functools
import math

import jax
import jax.numpy as jnp
from jax import lax
from jax.experimental import pallas as pl
from jax.experimental.pallas import tpu as pltpu
from jax.sharding import Mesh, PartitionSpec as P

HEADS = 12
DH = 64
LEN = 1024
NEG = -1e30
EPS = 1e-05
PAIR = 128
LOG2E = math.log2(math.e)
bf16 = jnp.bfloat16
f32 = jnp.float32
VMEM_BYTES = 22 << 20
COST = {"early": 1e11, "late": 1.3e9, "none": 0.0, "tail": 1e11}
PHASE = ["early"]


def near(v):
    return pltpu.with_memory_space_constraint(v, pltpu.VMEM)


def far(v):
    return pltpu.with_memory_space_constraint(v, pltpu.HBM)


def work(us):
    return pl.CostEstimate(flops=int(us * COST[PHASE[0]]), bytes_accessed=1 << 20, transcendentals=0)


def dot_nn(a, b):
    return lax.dot_general(a, b, (((1,), (0,)), ((), ())), preferred_element_type=f32)


def dot_nt(a, b):
    return lax.dot_general(a, b, (((1,), (1,)), ((), ())), preferred_element_type=f32)


def dot_tn(a, b):
    return lax.dot_general(a, b, (((0,), (0,)), ((), ())), preferred_element_type=f32)


def window(lo_ref, i, t, win, seg_col_ref):
    base=lo_ref[0,i]+t*win
    start=pl.multiple_of(jnp.minimum(base,LEN-win),16)
    seg_k=seg_col_ref[pl.ds(start,win),:]
    pos=start+lax.broadcasted_iota(jnp.int32,(win,PAIR),0)
    return start, jnp.where(pos>=base,seg_k,jnp.full_like(seg_k,-1))

def fwd_kernel(qb, win, lo_ref, q_ref, k_ref, v_ref, seg_col_ref, seg_row_ref, o_ref, ot_ref, lse_ref):
    c=LOG2E/math.sqrt(DH)
    def block(i,_):
        r0=pl.multiple_of(i*qb,qb)
        q=q_ref[pl.ds(r0,qb),:]
        low=lax.broadcasted_iota(jnp.int32,(qb,PAIR),1)<DH
        zero=jnp.zeros_like(q)
        qs=(jnp.where(low,q,zero),jnp.where(low,zero,q))
        seg_q=seg_row_ref[:,pl.ds(r0,qb)]
        def win_step(t,carry):
            start,seg_k=window(lo_ref,i,t,win,seg_col_ref)
            ok=jnp.concatenate([seg_k]*(qb//PAIR),axis=1)==seg_q
            kw=k_ref[pl.ds(start,win),:]
            out=[]
            for h in range(2):
                m,l,acc=carry[h]
                s=jnp.where(ok,dot_nt(kw,qs[h])*c,NEG)
                mn=jnp.maximum(m,jnp.max(s,axis=0,keepdims=True))
                al=jnp.exp2(m-mn)
                p=jnp.exp2(s-mn)
                l=l*al+jnp.sum(p,axis=0,keepdims=True)
                vtw=v_ref[pl.ds(start,win),:].T[h*DH:(h+1)*DH]
                acc=acc*al+dot_nn(vtw,p.astype(bf16))
                out.append((mn,l,acc))
            return tuple(out)
        init=(jnp.full((1,qb),NEG,f32),jnp.zeros((1,qb),f32),jnp.zeros((DH,qb),f32))
        res=lax.fori_loop(0,lo_ref[1,i],win_step,(init,init))
        ot=jnp.concatenate([a/l for m,l,a in res],axis=0).astype(bf16)
        ot_ref[:,pl.ds(r0,qb)]=ot
        o_ref[pl.ds(r0,qb),:]=ot.T
        lse_ref[0,:,pl.ds(r0,qb)]=jnp.concatenate([m+jnp.log2(l) for m,l,a in res],axis=0)
        return 0
    single=lo_ref[2,0]==1
    @pl.when(single)
    def _():
        low=lax.broadcasted_iota(jnp.int32,(qb,PAIR),1)<DH
        def scores(i,h):
            q=q_ref[i*qb:(i+1)*qb,:]
            zero=jnp.zeros_like(q)
            qh=jnp.where(low,q,zero) if h==0 else jnp.where(low,zero,q)
            start=pl.multiple_of(lo_ref[0,i],16)
            ok=jnp.concatenate([seg_col_ref[pl.ds(start,win),:]]*(qb//PAIR),axis=1)==seg_row_ref[:,i*qb:(i+1)*qb]
            return jnp.where(ok,dot_nt(k_ref[pl.ds(start,win),:],qh)*c,NEG)
        units=[(i,h) for i in range(LEN//qb) for h in range(2)]
        ahead=3
        queue=[scores(*u) for u in units[:ahead]]
        done={}
        for n,(i,h) in enumerate(units):
            s=queue.pop(0)
            m=jnp.max(s,axis=0,keepdims=True)
            if n+ahead<len(units): queue.append(scores(*units[n+ahead]))
            p=jnp.exp2(s-m)
            l=jnp.sum(p,axis=0,keepdims=True)
            if h==0:
                vt=v_ref[pl.ds(pl.multiple_of(lo_ref[0,i],16),win),:].T
            acc=dot_nn(vt[h*DH:(h+1)*DH],p.astype(bf16))
            done[h]=(acc/l,m+jnp.log2(l))
            if h==1:
                ot=jnp.concatenate([done[0][0],done[1][0]],axis=0).astype(bf16)
                ot_ref[:,i*qb:(i+1)*qb]=ot
                o_ref[i*qb:(i+1)*qb,:]=ot.T
                lse_ref[0,:,i*qb:(i+1)*qb]=jnp.concatenate([done[0][1],done[1][1]],axis=0)
    @pl.when(jnp.logical_not(single))
    def _():
        lax.fori_loop(0,LEN//qb,block,0)

def attn_fwd(qkv, meta, seg_col, seg_row, qb=256, win=512):
    nh=HEADS//2
    return pl.pallas_call(
        functools.partial(fwd_kernel,qb,win),
        out_shape=(pltpu.VMEM((LEN,HEADS*DH),bf16),pltpu.HBM((HEADS*DH,LEN),bf16),
                   jax.ShapeDtypeStruct((nh,2,LEN),f32)),
        grid_spec=pltpu.PrefetchScalarGridSpec(num_scalar_prefetch=1,grid=(nh,),
            in_specs=[pl.BlockSpec((LEN,PAIR),lambda h,*_:(0,h)),
                      pl.BlockSpec((LEN,PAIR),lambda h,*_:(0,nh+h)),
                      pl.BlockSpec((LEN,PAIR),lambda h,*_:(0,2*nh+h)),
                      pl.BlockSpec((LEN,PAIR),lambda h,*_:(0,0)),
                      pl.BlockSpec((1,LEN),lambda h,*_:(0,0))],
            out_specs=[pl.BlockSpec((LEN,PAIR),lambda h,*_:(0,h)),
                       pl.BlockSpec((PAIR,LEN),lambda h,*_:(h,0)),
                       pl.BlockSpec((1,2,LEN),lambda h,*_:(h,0,0))],
            ),
        compiler_params=pltpu.CompilerParams(vmem_limit_bytes=VMEM_BYTES),
        cost_estimate=work(14.0),
        name="attn_fwd",
    )(meta,*[far(qkv)]*3,seg_col,seg_row)

def bwd_kernel(qb, win, lo_ref, q_ref, k_ref, v_ref, dm_ref, ot_ref, lse_ref, seg_col_ref, seg_row_ref, out_ref, dka, dva):
    dka[...]=jnp.zeros_like(dka); dva[...]=jnp.zeros_like(dva)
    c=LOG2E/math.sqrt(DH); scale=1.0/math.sqrt(DH)
    def block(i,_):
        r0=pl.multiple_of(i*qb,qb)
        q=q_ref[pl.ds(r0,qb),:]; dm=dm_ref[pl.ds(r0,qb),:]
        low=lax.broadcasted_iota(jnp.int32,(qb,PAIR),1)<DH
        zero=jnp.zeros_like(q)
        qs=(jnp.where(low,q,zero),jnp.where(low,zero,q))
        dms=(jnp.where(low,dm,zero),jnp.where(low,zero,dm))
        seg_q=seg_row_ref[:,pl.ds(r0,qb)]
        prod=dm.T.astype(f32)*ot_ref[:,pl.ds(r0,qb)].astype(f32)
        delta=[jnp.sum(prod[h*DH:(h+1)*DH],axis=0,keepdims=True) for h in range(2)]
        lse=[lse_ref[0,h:h+1,pl.ds(r0,qb)] for h in range(2)]
        def win_step(t,carry):
            start,seg_k=window(lo_ref,i,t,win,seg_col_ref)
            ok=jnp.concatenate([seg_k]*(qb//PAIR),axis=1)==seg_q
            kw=k_ref[pl.ds(start,win),:]; vw=v_ref[pl.ds(start,win),:]
            out=[]
            dk=dka[pl.ds(start,win),:]; dv=dva[pl.ds(start,win),:]
            for h in range(2):
                s=dot_nt(kw,qs[h])
                p=jnp.where(ok,jnp.exp2(s*c-lse[h]),0.0)
                dp=dot_nt(vw,dms[h])
                ds=(p*(dp-delta[h])).astype(bf16)
                dv=dv+dot_nn(p.astype(bf16),dms[h])
                dk=dk+dot_nn(ds,qs[h])
                out.append(carry[h]+dot_nn(kw.T[h*DH:(h+1)*DH],ds))
            dka[pl.ds(start,win),:]=dk; dva[pl.ds(start,win),:]=dv
            return tuple(out)
        init=jnp.zeros((DH,qb),f32)
        res=lax.fori_loop(0,lo_ref[1,i],win_step,(init,init))
        out_ref[0,pl.ds(r0,qb),:]=(jnp.concatenate(res,axis=0)*scale).T.astype(bf16)
        return 0
    single=lo_ref[2,0]==1
    @pl.when(single)
    def _():
        low=lax.broadcasted_iota(jnp.int32,(qb,PAIR),1)<DH
        def half(x,h):
            zero=jnp.zeros_like(x)
            return jnp.where(low,x,zero) if h==0 else jnp.where(low,zero,x)
        def products(i,h):
            start=pl.multiple_of(lo_ref[0,i],16)
            qh=half(q_ref[i*qb:(i+1)*qb,:],h); dmh=half(dm_ref[i*qb:(i+1)*qb,:],h)
            return dot_nt(k_ref[pl.ds(start,win),:],qh),dot_nt(v_ref[pl.ds(start,win),:],dmh),qh,dmh
        units=[(i,h) for i in range(LEN//qb) for h in range(2)]
        ahead=2
        queue=[products(*u) for u in units[:ahead]]
        dqs={}
        for n,(i,h) in enumerate(units):
            s,dp,qh,dmh=queue.pop(0)
            if n+ahead<len(units): queue.append(products(*units[n+ahead]))
            start=pl.multiple_of(lo_ref[0,i],16)
            rows=slice(i*qb,(i+1)*qb)
            if h==0:
                kt=k_ref[pl.ds(start,win),:].T
                prod=dm_ref[rows,:].T.astype(f32)*ot_ref[:,rows].astype(f32)
                ok=jnp.concatenate([seg_col_ref[pl.ds(start,win),:]]*(qb//PAIR),axis=1)==seg_row_ref[:,rows]
            delta=jnp.sum(prod[h*DH:(h+1)*DH],axis=0,keepdims=True)
            p=jnp.where(ok,jnp.exp2(s*c-lse_ref[0,h:h+1,rows]),0.0)
            ds=(p*(dp-delta)).astype(bf16)
            dva[pl.ds(start,win),:]+=dot_nn(p.astype(bf16),dmh)
            dka[pl.ds(start,win),:]+=dot_nn(ds,qh)
            dqs[h]=dot_nn(kt[h*DH:(h+1)*DH],ds)
            if h==1:
                out_ref[0,rows,:]=(jnp.concatenate([dqs[0],dqs[1]],axis=0)*scale).T.astype(bf16)
    @pl.when(jnp.logical_not(single))
    def _():
        lax.fori_loop(0,LEN//qb,block,0)
    out_ref[1]=(dka[...]*scale).astype(bf16)
    out_ref[2]=dva[...].astype(bf16)

def attn_bwd(qkv, dmixed, mixed_t, lse, meta, seg_col, seg_row, qb=256, win=512, h0=0, nh=6):
    np_=HEADS//2
    col=lambda off: pl.BlockSpec((LEN,PAIR),lambda h,*_:(0,off+h0+h))
    return pl.pallas_call(
        functools.partial(bwd_kernel,qb,win),
        out_shape=pltpu.VMEM((3,LEN,nh*PAIR),bf16),
        grid_spec=pltpu.PrefetchScalarGridSpec(num_scalar_prefetch=1,grid=(nh,),
            in_specs=[col(0),col(np_),col(2*np_),col(0),pl.BlockSpec((PAIR,LEN),lambda h,*_:(h0+h,0)),
                      pl.BlockSpec((1,2,LEN),lambda h,*_:(h0+h,0,0)),
                      pl.BlockSpec((LEN,PAIR),lambda h,*_:(0,0)),
                      pl.BlockSpec((1,LEN),lambda h,*_:(0,0))],
            out_specs=pl.BlockSpec((3,LEN,PAIR),lambda h,*_:(0,0,h)),
            scratch_shapes=[pltpu.VMEM((LEN,PAIR),f32),pltpu.VMEM((LEN,PAIR),f32)]),
        compiler_params=pltpu.CompilerParams(vmem_limit_bytes=VMEM_BYTES),
        cost_estimate=work(3.7 * nh),
        name="attn_bwd",
    )(meta,*[far(qkv)]*3,far(dmixed),far(mixed_t),lse,seg_col,seg_row)

ROWS = 256


def full(*shape):
    return pl.BlockSpec(shape, lambda *_: (0,) * len(shape))


def once(*shape):
    return pl.BlockSpec(shape, lambda *_: (0,) * len(shape), pipeline_mode=pl.Buffered(1))


def resident():
    return pl.BlockSpec(memory_space=pltpu.VMEM)


def rows_of(width):
    return pl.BlockSpec((ROWS, width), lambda i, *_: (i, 0))


def normalise(x):
    centred = x - jnp.mean(x, axis=-1, keepdims=True)
    rstd = lax.rsqrt(jnp.mean(centred * centred, axis=-1, keepdims=True) + EPS)
    return centred * rstd, rstd


def norm_back(u, gain, n, rstd):
    ug = u * gain
    return rstd * (
        ug - jnp.mean(ug, axis=-1, keepdims=True) - n * jnp.mean(ug * n, axis=-1, keepdims=True)
    )


def params():
    return pltpu.CompilerParams(vmem_limit_bytes=VMEM_BYTES)


def qkv_kernel(x_ref, gain_ref, shift_ref, w_ref, h1_ref, qkv_ref):
    n, _ = normalise(x_ref[...].astype(f32))
    h1 = (n * gain_ref[...][None] + shift_ref[...][None]).astype(bf16)
    h1_ref[...] = h1.T
    qkv_ref[...] = dot_nn(h1, w_ref[...]).astype(bf16)


def ln_qkv(tokens, gain, shift, w_qkv):
    t, d = tokens.shape
    return pl.pallas_call(
        qkv_kernel,
        grid=(t // ROWS,),
        in_specs=[rows_of(d), full(d), full(d), once(d, 3 * d)],
        out_specs=[pl.BlockSpec((d, ROWS), lambda i: (0, i)), rows_of(3 * d)],
        out_shape=(
            pltpu.HBM((d, t), bf16),
            pltpu.HBM((t, 3 * d), bf16),
        ),
        compiler_params=params(),
        cost_estimate=work(8.0),
        name="ln_qkv",
    )(far(tokens), gain, shift, far(w_qkv))


def prelude_kernel(n_slots, seg_ref, slot_ref, meta_ref, info_ref, seg_col_ref, seg_row_ref, valid_ref):
    seg = seg_ref[...]
    slot = slot_ref[...]
    per, lanes = seg.shape
    blocks = meta_ref.shape[1]
    rows = per // blocks
    pos = lax.broadcasted_iota(jnp.int32, seg.shape, 0) * lanes + lax.broadcasted_iota(
        jnp.int32, seg.shape, 1
    )
    most = 0
    for i in range(blocks):
        part = seg[i * rows:(i + 1) * rows]
        hit = jnp.logical_and(seg >= jnp.min(part), seg <= jnp.max(part))
        first = jnp.min(jnp.where(hit, pos, LEN))
        last = jnp.max(jnp.where(hit, pos + 1, 0))
        lo = jnp.minimum(first // 16 * 16, LEN - WIN)
        count = (last - lo + WIN - 1) // WIN
        meta_ref[0, i] = lo
        meta_ref[1, i] = count
        most = jnp.maximum(most, count)
    for i in range(blocks):
        meta_ref[2, i] = (most == 1).astype(jnp.int32)
    second = jnp.logical_and(slot >= n_slots // 2, slot < n_slots).astype(jnp.int32)
    first = (slot < n_slots // 2).astype(jnp.int32)
    info_ref[0] = jnp.max(second)
    info_ref[1] = jnp.sum(first)
    info_ref[2] = jnp.sum(second)
    seg = seg.astype(f32)
    valid = (slot < n_slots).astype(f32)
    for i in range(per):
        at = slice(i * lanes, (i + 1) * lanes)
        seg_row_ref[:, at] = seg[i:i + 1]
        seg_col_ref[at, :] = jnp.broadcast_to(seg[i:i + 1], (lanes, lanes)).T
        valid_ref[at, :] = jnp.broadcast_to(valid[i:i + 1], (lanes, lanes)).T


def prelude(seg_start, dispatch_slot, n_slots):
    t = seg_start.shape[0]
    smem = pl.BlockSpec(memory_space=pltpu.SMEM)
    vmem = pl.BlockSpec(memory_space=pltpu.VMEM)
    return pl.pallas_call(
        functools.partial(prelude_kernel, n_slots),
        in_specs=[vmem, vmem],
        out_specs=[smem, smem, vmem, vmem, vmem],
        out_shape=(
            jax.ShapeDtypeStruct((3, LEN // QBLOCK), jnp.int32),
            jax.ShapeDtypeStruct((3,), jnp.int32),
            jax.ShapeDtypeStruct((t, PAIR), f32),
            jax.ShapeDtypeStruct((1, t), f32),
            jax.ShapeDtypeStruct((t, PAIR), f32),
        ),
        cost_estimate=work(2.0),
        name="prelude",
    )(seg_start.reshape(t // PAIR, PAIR), dispatch_slot.reshape(t // PAIR, PAIR))


def proj_kernel(x_ref, mixed_ref, cot_ref, valid_ref, w_ref, gain_ref, shift_ref,
                resid_ref, h2_ref, cotm_ref):
    resid = x_ref[...].astype(f32) + dot_nn(mixed_ref[...], w_ref[...])
    resid_ref[...] = resid
    n, _ = normalise(resid)
    routed = jnp.concatenate([valid_ref[...]] * (resid.shape[1] // PAIR), axis=1) > 0.5
    h2 = n * gain_ref[...][None] + shift_ref[...][None]
    h2_ref[...] = jnp.where(routed, h2, 0.0).astype(bf16)
    cotm_ref[...] = jnp.where(routed, cot_ref[...].astype(f32), 0.0).astype(bf16)


def proj_ln(tokens, mixed, cotangent, valid, w_attn_out, gain, shift):
    t, d = tokens.shape
    return pl.pallas_call(
        proj_kernel,
        grid=(t // ROWS,),
        in_specs=[rows_of(d), rows_of(d), rows_of(d), rows_of(PAIR), full(d, d), full(d), full(d)],
        out_specs=[rows_of(d), rows_of(d), rows_of(d)],
        out_shape=(
            pltpu.HBM((t, d), f32),
            pltpu.VMEM((t, d), bf16),
            pltpu.VMEM((t, d), bf16),
        ),
        compiler_params=params(),
        cost_estimate=work(7.0),
        name="proj_ln",
    )(far(tokens), near(mixed), far(cotangent), valid, far(w_attn_out), gain, shift)


def gelu_parts(v):
    half = 0.5 * (1.0 + lax.erf(v * math.sqrt(0.5)))
    bell = jnp.exp(-0.5 * v * v) * (1.0 / math.sqrt(2.0 * math.pi))
    return v * half, half + v * bell


TOKENS_STEP = 256


def expert_kernel(axis, which_ref, place_ref, h2_ref, cot_ref, wina_ref, winb_ref, wouta_ref, woutb_ref,
                  hid_ref, dpre_ref, *out_refs):
    win = jnp.concatenate([wina_ref[0], winb_ref[0]], axis=1)
    wout = jnp.concatenate([wouta_ref[0], woutb_ref[0]], axis=0)
    hiddens, d_pres = [], []
    for at in range(0, h2_ref.shape[0], TOKENS_STEP):
        rows = slice(at, at + TOKENS_STEP)
        hidden, slope = gelu_parts(dot_nn(h2_ref[rows, :], win))
        hidden = hidden.astype(bf16)
        d_pre = (dot_nt(cot_ref[rows, :], wout) * slope).astype(bf16)
        hid_ref[rows, :] = hidden
        dpre_ref[rows, :] = d_pre
        hiddens.append(hidden)
        d_pres.append(d_pre)
    g_in = dot_tn(jnp.concatenate(d_pres, axis=0), h2_ref[...]).astype(bf16)
    g_out = dot_tn(jnp.concatenate(hiddens, axis=0), cot_ref[...]).astype(bf16)
    unit = wina_ref.shape[2]
    if axis is None:
        e = which_ref[0]
        for core in range(2):
            for j, g in enumerate((g_in, g_out)):
                part = g[core * unit:(core + 1) * unit]
                n_dp = out_refs[0].shape[1]
                step = unit // n_dp
                for to in range(n_dp):
                    piece = part[to * step:(to + 1) * step]
                    out_refs[0][core, to, e, j] = piece
                    out_refs[0][core, to, 1 - e, j] = jnp.zeros_like(piece)
    else:
        hold = out_refs[4]
        hold[0] = g_in
        hold[1] = g_out
        half = unit // 2
        for k in range(4):
            core, side = place_ref[0] ^ (k & 1), place_ref[axis] ^ (k >> 1)
            at = pl.multiple_of(core * unit + side * half, half)
            for j in range(2):
                out_refs[k][0, j] = hold[j, pl.ds(at, half), :]


def expert_part(which, place, h2, cot, w_in, w_out, p, axis, unit, n_z, n_dp=1):
    t, d = h2.shape
    parts = w_in.shape[2] // (unit * n_z * 2)

    def column(core):
        return pl.BlockSpec((1, d, unit), lambda z, w, _: (w[0], 0, parts * (2 * z + core) + p))

    def row(core):
        return pl.BlockSpec((1, unit, d), lambda z, w, _: (w[0], parts * (2 * z + core) + p, 0))

    if axis is None:
        step = unit // n_dp
        shapes = [pltpu.HBM((2 * n_z, n_dp, 2, 2, step, d), bf16)]
        specs = [pl.BlockSpec((2, n_dp, 2, 2, step, d), lambda z, *_: (z, 0, 0, 0, 0, 0))]
        scratch = []
    else:
        shapes = [pltpu.HBM((n_z, 2, unit // 2, d), bf16)] * 4
        specs = [pl.BlockSpec((1, 2, unit // 2, d), lambda z, *_: (z, 0, 0, 0))] * 4
        scratch = [pltpu.VMEM((2, 2 * unit, d), bf16)]
    act = (t, 2 * n_z * unit)
    act_spec = pl.BlockSpec((t, 2 * unit), lambda z, *_: (0, z))
    return pl.pallas_call(
        functools.partial(expert_kernel, axis),
        grid_spec=pltpu.PrefetchScalarGridSpec(
            num_scalar_prefetch=2,
            grid=(n_z,),
            in_specs=[resident(), resident(), column(0), column(1), row(0), row(1)],
            out_specs=[act_spec, act_spec] + specs,
            scratch_shapes=scratch,
        ),
        out_shape=[pltpu.HBM(act, bf16), pltpu.HBM(act, bf16)] + shapes,
        compiler_params=params(),
        cost_estimate=work(33.0 / parts),
        name="expert_part",
    )(which, place, near(h2), near(cot), *[far(w_in)] * 2, *[far(w_out)] * 2)


def in_order(refs, unit):
    blocks = refs[0].shape[1] // unit
    return jnp.concatenate(
        [r[:, b * unit:(b + 1) * unit] for b in range(blocks) for r in refs], axis=1
    )


def post_kernel(n, unit, which_ref, *refs):
    dpre_refs, rest = refs[:n], refs[n:]
    win_ref, resid_ref, cot_ref, w_ref, gain_ref, dres_ref, dbr_ref, dmix_ref, gvec_ref = rest
    u = dot_nt(in_order(dpre_refs, unit), win_ref[0]).astype(bf16).astype(f32)
    nrm, rstd = normalise(resid_ref[...])
    d_resid = cot_ref[...].astype(f32) + norm_back(u, gain_ref[...][None], nrm, rstd)
    dres_ref[...] = d_resid
    d_branch = d_resid.astype(bf16)
    dbr_ref[...] = d_branch
    dmix_ref[...] = dot_nt(d_branch, w_ref[...]).astype(bf16)
    gg = jnp.sum(u * nrm, axis=0, keepdims=True)
    gs = jnp.sum(u, axis=0, keepdims=True)
    step = pl.program_id(0)

    @pl.when(step == 0)
    def _():
        gvec_ref[0:1, :] = gg
        gvec_ref[1:2, :] = gs

    @pl.when(step > 0)
    def _():
        gvec_ref[0:1, :] += gg
        gvec_ref[1:2, :] += gs


def post_ffn(which, d_pres, w_in, resid, cotangent, w_attn_out, gain, unit):
    t, d = resid.shape
    n = len(d_pres)
    ff = w_in.shape[2]
    return pl.pallas_call(
        functools.partial(post_kernel, n, unit),
        grid_spec=pltpu.PrefetchScalarGridSpec(
            num_scalar_prefetch=1,
            grid=(t // ROWS,),
            in_specs=[rows_of(ff // n)] * n
            + [pl.BlockSpec((1, d, ff), lambda i, w: (w[0], 0, 0), pipeline_mode=pl.Buffered(1))]
            + [rows_of(d)] * 2
            + [full(d, d), full(d)],
            out_specs=[rows_of(d)] * 3 + [full(2, d)],
        ),
        out_shape=(
            pltpu.HBM((t, d), f32),
            pltpu.HBM((t, d), bf16),
            pltpu.HBM((t, d), bf16),
            jax.ShapeDtypeStruct((2, d), f32),
        ),
        compiler_params=params(),
        cost_estimate=work(10.0),
        name="post_ffn",
    )(which, *[far(v) for v in d_pres], far(w_in), far(resid), far(cotangent), far(w_attn_out), gain)


def result_kernel(n, unit, which_ref, *refs):
    wout_ref, resid_ref, out_ref = refs[n:]
    ffn = dot_nn(in_order(refs[:n], unit), wout_ref[0]).astype(bf16).astype(f32)
    out_ref[...] = (resid_ref[...] + ffn).astype(bf16)


def result_of(which, hiddens, w_out, resid, unit):
    t, d = resid.shape
    n = len(hiddens)
    ff = w_out.shape[1]
    return pl.pallas_call(
        functools.partial(result_kernel, n, unit),
        grid_spec=pltpu.PrefetchScalarGridSpec(
            num_scalar_prefetch=1,
            grid=(t // ROWS,),
            in_specs=[rows_of(ff // n)] * n
            + [pl.BlockSpec((1, ff, d), lambda i, w: (w[0], 0, 0), pipeline_mode=pl.Buffered(1)), rows_of(d)],
            out_specs=rows_of(d),
        ),
        out_shape=pltpu.HBM((t, d), bf16),
        compiler_params=params(),
        cost_estimate=work(8.0),
        name="result_of",
    )(which, *[far(v) for v in hiddens], far(w_out), far(resid))


def weight_kernel(c_ref, *refs):
    extra = len(refs) == 6
    h1_ref, d_ref = refs[:2]
    other_ref, mine_ref = refs[-2:]
    half = other_ref.shape[0]
    mine_at = pl.multiple_of(c_ref[0] * half, half)
    other_at = pl.multiple_of(half - c_ref[0] * half, half)

    def products(left_ref, right):
        other_ref[...] = dot_nn(left_ref[pl.ds(other_at, half), :], right).astype(bf16)
        mine_ref[...] = dot_nn(left_ref[pl.ds(mine_at, half), :], right).astype(bf16)

    if not extra:
        products(h1_ref, d_ref[0])
        return

    @pl.when(pl.program_id(0) < 3)
    def _():
        products(h1_ref, d_ref[0])

    @pl.when(pl.program_id(0) >= 3)
    def _():
        products(refs[2], refs[3][...])


def weight_grads(core, h1_t, d_qkv, more=()):
    d, t = h1_t.shape
    half, width = d // 2, d_qkv.shape[2]
    blocks = 3
    specs = [full(d, t), pl.BlockSpec((1, t, width), lambda i, c: (jnp.minimum(i, 2), 0, 0))]
    if more:
        specs += [full(d, t), pl.BlockSpec((t, width), lambda i, c: (0, jnp.maximum(i - 3, 0)))]
        blocks += more[1].shape[1] // width
    shape = pltpu.HBM((half, blocks * width), bf16)
    return pl.pallas_call(
        weight_kernel,
        grid_spec=pltpu.PrefetchScalarGridSpec(
            num_scalar_prefetch=1,
            grid=(blocks,),
            in_specs=specs,
            out_specs=[pl.BlockSpec((half, width), lambda i, c: (0, i))] * 2,
        ),
        out_shape=(shape, shape),
        compiler_params=params(),
        cost_estimate=work(1.2 * blocks * width / half),
        name="weight_grads",
    )(core, far(h1_t), near(d_qkv), *[far(v) for v in more])


def input_kernel(groups, *refs):
    ins, (x_ref, dres_ref, w_ref, gain_ref, gtok_ref, gvec_ref) = refs[:groups], refs[groups:]
    side = jnp.concatenate([r[j] for j in range(3) for r in ins], axis=1)
    u = dot_nt(side, w_ref[...])
    n, rstd = normalise(x_ref[...].astype(f32))
    gtok_ref[...] = dres_ref[...] + norm_back(u, gain_ref[...][None], n, rstd)
    gg = jnp.sum(u * n, axis=0, keepdims=True)
    gs = jnp.sum(u, axis=0, keepdims=True)
    first = pl.program_id(0) == 0

    @pl.when(first)
    def _():
        gvec_ref[0:1, :] = gg
        gvec_ref[1:2, :] = gs

    @pl.when(jnp.logical_not(first))
    def _():
        gvec_ref[0:1, :] += gg
        gvec_ref[1:2, :] += gs


def input_grad(parts, tokens, d_resid, w_qkv, gain):
    t, d = tokens.shape
    return pl.pallas_call(
        functools.partial(input_kernel, len(parts)),
        grid=(t // ROWS,),
        in_specs=[pl.BlockSpec((3, ROWS, p.shape[2]), lambda i: (0, i, 0)) for p in parts]
        + [rows_of(d), rows_of(d), once(d, 3 * d), full(d)],
        out_specs=[rows_of(d), full(2, d)],
        out_shape=(
            pltpu.HBM((t, d), f32),
            jax.ShapeDtypeStruct((2, d), f32),
        ),
        compiler_params=params(),
        cost_estimate=work(10.0),
        name="input_grad",
    )(*[far(p) for p in parts], far(tokens), far(d_resid), far(w_qkv), gain)


def sum_kernel(axis, place_ref, voice_ref, a_ref, b_ref, c_ref, d_ref, keep_ref, send_ref):
    me = place_ref[3]
    bit = place_ref[3 - axis]
    step = keep_ref.shape[3]
    for j in range(2):
        for out_ref, mine in ((keep_ref, bit), (send_ref, 1 - bit)):
            at = pl.multiple_of(mine * step, step)
            sides = [None, None]
            for k, ref in enumerate((a_ref, b_ref, c_ref, d_ref)):
                term = ref[0, j, pl.ds(at, step), :].astype(f32)
                second = voice_ref[me ^ ((k & 1) | ((k >> 1) << axis))] == 1
                for e in range(2):
                    part = jnp.where(second, term if e else 0.0, 0.0 if e else term)
                    sides[e] = part if sides[e] is None else sides[e] + part
            for e in range(2):
                out_ref[0, e, j] = sides[e].astype(bf16)


def sum_sides(axis, place, voice, got):
    n_z, two, rows, d = got[0].shape
    spec = pl.BlockSpec((1, two, rows, d), lambda z, *_: (z, 0, 0, 0))
    out = pl.BlockSpec((1, 2, two, rows // 2, d), lambda z, *_: (z, 0, 0, 0, 0))
    shape = jax.ShapeDtypeStruct((n_z, 2, two, rows // 2, d), bf16)
    return pl.pallas_call(
        functools.partial(sum_kernel, axis),
        grid_spec=pltpu.PrefetchScalarGridSpec(
            num_scalar_prefetch=2,
            grid=(n_z,),
            in_specs=[spec] * 4,
            out_specs=[out, out],
        ),
        out_shape=(shape, shape),
        compiler_params=params(),
        cost_estimate=work(3.0),
        name="sum_sides",
    )(place, voice, *[near(v) for v in got])


def finish_kernel(axes, place_ref, tally_ref, *refs):
    blocks, (gin_ref, gout_ref, counts_ref, hold_ref) = refs[:-4], refs[-4:]
    spots = [(ref, k) for ref in blocks for k in range(ref.shape[1])]
    d = gin_ref.shape[1]
    lane = lax.broadcasted_iota(jnp.int32, (1, d), 1)
    counts = [jnp.sum(jnp.where(lane == 128 + e, tally_ref[...], 0.0)) for e in range(2)]
    for e in range(2):
        counts_ref[e] = counts[e].astype(jnp.int32)
    unit = hold_ref.shape[0]
    step = unit // 4
    for p, ((ref, part), axis) in enumerate(zip(spots, axes)):
        for e in range(2):
            factor = jnp.full((1, d), counts[0] + counts[1], f32) / (2.0 * counts[e])
            for j in range(2):
                for k in range(4):
                    to = 2 * (k & 1) + (k >> 1) if axis == X else k
                    rows = slice(to * step, (to + 1) * step)
                    hold_ref[rows, :] = ref[k, part, e, j].astype(f32) * factor
                where = slice(p * unit, (p + 1) * unit)
                if j == 0:
                    gin_ref[e, :, where] = hold_ref[...].T
                else:
                    gout_ref[e, where, :] = hold_ref[...]


def finish_experts(axes, place, tally, blocks):
    step, d = blocks[0].shape[-2:]
    n = len(axes)
    smem = pl.BlockSpec(memory_space=pltpu.SMEM)
    return pl.pallas_call(
        functools.partial(finish_kernel, axes),
        in_specs=[smem] + [resident()] * (1 + len(blocks)),
        out_specs=[resident(), resident(), smem],
        out_shape=(
            jax.ShapeDtypeStruct((2, d, n * 4 * step), f32),
            jax.ShapeDtypeStruct((2, n * 4 * step, d), f32),
            jax.ShapeDtypeStruct((2,), jnp.int32),
        ),
        scratch_shapes=[pltpu.VMEM((4 * step, d), f32)],
        compiler_params=params(),
        cost_estimate=work(4.0),
        name="finish_experts",
    )(place, tally, *[near(v) for v in blocks])


def join_kernel(widths, place_ref, *refs):
    n = len(widths)
    gw_ref, gwo_ref, vec_ref = refs[2 * n:]
    d = gwo_ref.shape[2]
    rows = gwo_ref.shape[1]
    rel = pl.program_id(0) ^ (place_ref[3] >> 1)
    at = place_ref[3] >> 1
    vec = refs[2 * n - 2][at, rows:, :d].astype(f32) + refs[2 * n - 1][at, rows:, :d].astype(f32)
    vec_ref[...] = vec[:8]
    before = 0
    for k, width in enumerate(widths):
        for half, ref in ((place_ref[0], refs[2 * k]), (1 - place_ref[0], refs[2 * k + 1])):
            for third in range(3):
                at, src = third * d + before, third * width
                gw_ref[half, :, at:at + width] = ref[rel, :rows, src:src + width].astype(f32)
            if k == 0:
                gwo_ref[half] = ref[rel, :rows, 3 * width:].astype(f32)
        before += width


def join_weights(place, sums, d):
    step = d // 8
    extra = [d] + [0] * (len(sums) - 1)
    widths = [(s[0].shape[2] - x) // 3 for s, x in zip(sums, extra)]
    flat = [v for pair in sums for v in pair]
    gw, gwo, vec = pl.pallas_call(
        functools.partial(join_kernel, widths),
        grid_spec=pltpu.PrefetchScalarGridSpec(
            num_scalar_prefetch=1,
            grid=(4,),
            in_specs=[resident()] * len(flat),
            out_specs=[
                pl.BlockSpec((2, step, 3 * d), lambda i, *_: (0, i, 0)),
                pl.BlockSpec((2, step, d), lambda i, *_: (0, i, 0)),
                full(8, d),
            ],
        ),
        out_shape=(
            jax.ShapeDtypeStruct((2, d // 2, 3 * d), f32),
            jax.ShapeDtypeStruct((2, d // 2, d), f32),
            jax.ShapeDtypeStruct((8, d), f32),
        ),
        compiler_params=params(),
        cost_estimate=work(5.0),
        name="join_weights",
    )(place, *[near(v) for v in flat])
    return gw.reshape(d, 3 * d), gwo.reshape(d, d), vec


X, Y = 1, 2
NEAR = [(0, 1), (1, 0), (2, 3), (3, 2)]
FAR = [(0, 3), (3, 0), (1, 2), (2, 1)]


def swap_core(v):
    return lax.ppermute(v, "core", [(0, 1), (1, 0)])


def swap(v, axis):
    return lax.ppermute(v, "dp", [(i, i ^ axis) for i in range(4)])


def swap_both(v, axis):
    return lax.ppermute(v, ("dp", "core"), [(i, i ^ (1 | (axis << 1))) for i in range(8)])


def along_z(v, pairs):
    return lax.ppermute(v, "z", pairs)


def tie(v, *after):
    return lax.optimization_barrier((v,) + after)[0] if after else v


def small_kernel(fn, *refs):
    out_ref = refs[-1]
    out_ref[...] = fn(*[r[...] for r in refs[:-1]]).astype(out_ref.dtype)


def small(fn, *args, space=pltpu.VMEM, name="small"):
    shape = jax.eval_shape(fn, *args)
    return pl.pallas_call(
        functools.partial(small_kernel, fn),
        in_specs=[resident()] * len(args),
        out_specs=resident(),
        out_shape=pltpu.VMEM(shape.shape, args[0].dtype),
        compiler_params=params(),
        cost_estimate=work(1.0),
        name=name,
    )(*[near(v) for v in args])


def add_f32(a, b):
    return a.astype(f32) + b.astype(f32)


def add(a, b):
    return small(add_f32, a, b, name="add")


def merge_kernel(mine_ref, away_ref, first_ref, second_ref, out_ref):
    n, rows, width = out_ref.shape
    rows -= 16
    d = first_ref.shape[1]
    for k in range(n):
        at = slice(k * rows, (k + 1) * rows)
        out_ref[k, :rows] = (mine_ref[at, :].astype(f32) + away_ref[at, :].astype(f32)).astype(bf16)
        out_ref[k, rows:] = jnp.zeros((16, width), bf16)
    small = jnp.concatenate([first_ref[...], second_ref[...], jnp.zeros((12, d), f32)], axis=0)
    out_ref[0, rows:, :d] = small.astype(bf16)


def merge_small(mine, away, first, second):
    half, width = mine.shape
    return pl.pallas_call(
        merge_kernel,
        in_specs=[resident()] * 4,
        out_specs=resident(),
        out_shape=pltpu.VMEM((4, half // 4 + 16, width), bf16),
        compiler_params=params(),
        cost_estimate=work(1.0),
        name="merge_small",
    )(near(mine), near(away), first, second)


def split_kernel(axis, place_ref, *refs):
    keep_ref, send_ref = refs[-2:]
    bit = place_ref[axis]
    for out_ref, at in ((keep_ref, bit), (send_ref, 1 - bit)):
        v = refs[0][at]
        for r in refs[1:-2]:
            v = v.astype(f32) + r[at].astype(f32)
        out_ref[...] = v.astype(bf16)


def split(place, axis, *v):
    shape = pltpu.VMEM(v[0].shape[1:], bf16)
    return pl.pallas_call(
        functools.partial(split_kernel, axis),
        in_specs=[pl.BlockSpec(memory_space=pltpu.SMEM)] + [resident()] * len(v),
        out_specs=[resident()] * 2,
        out_shape=(shape, shape),
        compiler_params=params(),
        cost_estimate=work(1.0),
        name="split",
    )(place, *[near(x) for x in v])


def total(v):
    return small(lambda x: sum(x[k].astype(f32) for k in range(x.shape[0])), v, name="total")


def stack(*v):
    return small(lambda *x: jnp.stack(x), *v, name="stack")


class Line:
    def __init__(self):
        self.last = ()

    def __call__(self, step, first, *rest):
        out = step(tie(first, *self.last), *rest)
        self.last = (jax.tree.leaves(out)[0],)
        return out


UNIT = 128
QBLOCK = 256
WIN = 512
GROUPS = (3, 3)


def tuned(tokens, cotangent, seg_start, dispatch_slot, ln1_gain, ln1_shift, w_qkv, w_attn_out,
          ln2_gain, ln2_shift, w_in, w_out):
    tok_count, d = tokens.shape
    n_z = lax.axis_size("z")
    n_slots = 2 * n_z * (2 * tok_count // (2 * n_z))
    core, dp = lax.axis_index("core"), lax.axis_index("dp")
    bits = {X: dp & 1, Y: dp >> 1}
    place = jnp.stack([core, bits[X], bits[Y], dp * 2 + core]).astype(jnp.int32)
    line = Line()
    PHASE[0] = "early"

    def around(v):
        return [v, swap(v, X), swap(v, Y), swap(v, X | Y)]

    def exchange(v):
        return lax.all_to_all(v, "dp", split_axis=0, concat_axis=0, tiled=True)

    def merge(a, b):
        return small(add_f32, a, b, name="merge").reshape(4, -1, a.shape[1])

    meta, info, seg_col, seg_row, valid = prelude(seg_start, dispatch_slot, n_slots)
    lane = lax.broadcasted_iota(jnp.int32, (1, d), 1)
    voice = jnp.where(lane == place[3], info[0], 0)
    voice = jnp.where(lane == 128, info[1], jnp.where(lane == 129, info[2], voice)).astype(f32)
    away = swap_core(voice)
    h1_t, qkv = line(ln_qkv, tokens, ln1_gain, ln1_shift, w_qkv)
    voice = line(add, voice, away)
    away = swap(voice, X)
    mixed, mixed_t, lse = line(
        lambda v: attn_fwd(v, meta, seg_col, seg_row, QBLOCK, WIN), qkv
    )
    voice = line(add, voice, away)
    away = swap(voice, Y)
    resid, h2, cotm = line(
        lambda v: proj_ln(tokens, v, cotangent, valid, w_attn_out, ln2_gain, ln2_shift), mixed
    )
    tally = line(add, voice, away)
    voice = tally[0, :8].astype(jnp.int32)
    away_t = along_z(tally, NEAR)

    def expert(p, axis):
        return line(
            lambda v: expert_part(info, place, v, cotm, w_in, w_out, p, axis, UNIT, n_z, 4), h2
        )

    def plane(pieces, axis):
        return [pieces[0], swap_core(pieces[1]), swap(pieces[2], axis), swap_both(pieces[3], axis)]

    hid_b, dpre_b, *out_b = expert(1, X)
    got_b = plane(out_b, X)
    tally = line(add, tally, away_t)
    away_t = along_z(tally, FAR)
    hid_a, dpre_a, out_a = expert(0, None)
    tally = line(add, tally, away_t)
    own_a = lax.psum_scatter(out_a, ("z", "core"), scatter_dimension=0, tiled=True)
    hid_c, dpre_c, *out_c = expert(2, Y)
    got_c = plane(out_c, Y)
    d_resid, d_branch, d_mixed, gvec2 = line(
        lambda v: post_ffn(
            info, (dpre_a, v, dpre_c), w_in, resid, cotangent, w_attn_out, ln2_gain, UNIT
        ),
        dpre_b,
    )

    def sides(got, axis):
        return line(lambda v: sum_sides(axis, place, voice, (got[0], got[1], got[2], v)), got[3])

    def bwd(at, nh):
        return line(
            lambda v: attn_bwd(qkv, v, mixed_t, lse, meta, seg_col, seg_row, QBLOCK, WIN, at, nh),
            d_mixed,
        )

    def scatter_z(v):
        return lax.psum_scatter(v, "z", scatter_dimension=0, tiled=True)[0]

    one, two = GROUPS
    keep_b, send_b = sides(got_b, X)
    away_b = swap(send_b, Y)
    d_qkv_1 = bwd(0, one)
    other_1, mine_1 = line(lambda v: weight_grads(place, v, d_qkv_1, (mixed_t, d_branch)), h1_t)
    away_1 = swap_core(other_1)
    keep_c, send_c = sides(got_c, Y)
    away_c = swap(send_c, X)
    both_b = line(add, keep_b, away_b)
    half_b = scatter_z(both_b)
    keep_a, send_a = line(lambda v: split(place, Y, v.reshape((2, 2) + v.shape[1:])), own_a[0])
    away_a = swap(send_a, Y)
    all_1 = exchange(line(merge, mine_1, away_1))
    d_qkv_2 = bwd(one, two)
    PHASE[0] = "late"
    PHASE[0] = "early"
    other_2, mine_2 = line(lambda v: weight_grads(place, v, d_qkv_2), h1_t)
    away_2 = swap_core(other_2)
    PHASE[0] = "late"
    both_c = line(add, keep_c, away_c)
    half_c = scatter_z(both_c)
    keep_a, send_a = line(lambda a, b: split(place, X, a, b), keep_a, away_a)
    away_a = swap(send_a, X)
    piece_1 = line(total, all_1)
    away_1 = along_z(piece_1, NEAR)

    def copies(*v):
        return small(lambda *x: jnp.stack([jnp.stack(x)] * 4), *v, name="copies")

    half_a = line(add, keep_a, away_a)
    all_ab = exchange(line(copies, half_a, half_b))
    grad_tokens, gvec1 = line(
        lambda v: input_grad((d_qkv_1, d_qkv_2), v, d_resid, w_qkv, ln1_gain), tokens
    )
    all_2 = exchange(line(lambda a, b: merge_small(a, b, gvec1, gvec2), tie(mine_2, all_ab), away_2))
    piece_1 = line(add, piece_1, away_1)
    away_1 = along_z(piece_1, FAR)
    result_out = line(lambda v: result_of(info, (hid_a, hid_b, hid_c), w_out, v, UNIT), resid)
    piece_2 = line(total, all_2)
    away_2 = along_z(piece_2, NEAR)
    all_c = exchange(line(copies, half_c))
    PHASE[0] = "tail"
    piece_2 = line(add, piece_2, away_2)
    away_2 = along_z(piece_2, FAR)
    piece_1 = line(add, piece_1, away_1)
    around_1 = around(piece_1)
    piece_2 = line(add, piece_2, away_2)
    around_2 = around(piece_2)
    grad_w_in, grad_w_out, all_counts = line(
        lambda v: finish_experts((Y, X, Y), place, tie(tally, piece_2), (all_ab, v)), all_c
    )
    whole_1 = line(stack, *around_1)
    other_1 = swap_core(whole_1)
    whole_2 = line(stack, *around_2)
    other_2 = swap_core(whole_2)
    grad_wqkv, grad_wo, vectors = join_weights(
        place, ((tie(whole_1, *line.last), other_1), (whole_2, other_2)), d
    )
    PHASE[0] = "early"
    return (
        result_out, grad_tokens, vectors[0], vectors[1], grad_wqkv, grad_wo, vectors[2], vectors[3],
        grad_w_in, grad_w_out, all_counts,
    )


def general(tokens, cotangent, seg_start, dispatch_slot, ln1_gain, ln1_shift, w_qkv, w_attn_out,
            ln2_gain, ln2_shift, w_in, w_out):
    tok_count, d = tokens.shape
    n_expert = lax.axis_size("expert")
    n_slots = n_expert * (2 * tok_count // n_expert)
    everywhere = ("dp", "expert")
    first_half = jnp.zeros((1,), jnp.int32)
    meta, info, seg_col, seg_row, valid = prelude(seg_start, dispatch_slot, n_slots)
    h1_t, qkv = ln_qkv(tokens, ln1_gain, ln1_shift, w_qkv)
    mixed, mixed_t, lse = attn_fwd(qkv, meta, seg_col, seg_row, QBLOCK, WIN)
    resid, h2, cotm = proj_ln(tokens, mixed, cotangent, valid, w_attn_out, ln2_gain, ln2_shift)
    blocks = w_in.shape[2] // (UNIT * 2)
    hidden, d_pre, grads = expert_part(
        info, first_half, h2, cotm, w_in, w_out, 0, None, UNIT, blocks
    )
    grads = jnp.transpose(grads[:, 0], (1, 2, 0, 3, 4)).reshape(2, 2, 2 * blocks * UNIT, d)
    grads = lax.psum_scatter(grads, "expert", scatter_dimension=2, tiled=True)
    grads = lax.psum(grads, "dp").astype(f32)
    d_resid, d_branch, d_mixed, gvec2 = post_ffn(
        info, (d_pre,), w_in, resid, cotangent, w_attn_out, ln2_gain, UNIT
    )
    result_out = result_of(info, (hidden,), w_out, resid, UNIT)
    d_qkv = attn_bwd(qkv, d_mixed, mixed_t, lse, meta, seg_col, seg_row, QBLOCK, WIN)
    bottom, top = weight_grads(first_half, h1_t, d_qkv, (mixed_t, d_branch))
    grad_tokens, gvec1 = input_grad((d_qkv,), tokens, d_resid, w_qkv, ln1_gain)
    weights = lax.psum(jnp.concatenate([top, bottom], axis=0), everywhere).astype(f32)
    grad_wqkv, grad_wo = weights[:, : 3 * d], weights[:, 3 * d:]
    counts, gvec1, gvec2 = lax.psum((info[1:].astype(f32), gvec1, gvec2), everywhere)
    factor = (jnp.sum(counts) / (2.0 * counts))[:, None, None]
    return (
        result_out, grad_tokens, gvec1[0], gvec1[1], grad_wqkv, grad_wo,
        gvec2[0], gvec2[1], jnp.transpose(grads[:, 0], (0, 2, 1)) * factor, grads[:, 1] * factor,
        counts.astype(jnp.int32),
    )


def solution(mesh):
    n_dp, n_expert = mesh.shape["dp"], mesh.shape["expert"]
    if (n_dp, n_expert) == (4, 8):
        mesh = Mesh(mesh.devices.reshape(n_dp, n_expert // 2, 2), ("dp", "z", "core"))
        body, expert = tuned, ("z", "core")
    else:
        body, expert = general, ("expert",)
    everywhere = ("dp",) + expert
    rows = P(everywhere, None)
    flat = P(everywhere)
    rep = P()
    return jax.shard_map(
        body,
        mesh=mesh,
        in_specs=(rows, rows, flat, flat) + (rep,) * 8,
        out_specs=(rows, rows) + (rep,) * 6 + (P(None, None, expert), P(None, expert, None), rep),
        check_vma=False,
    )
```

profile of v0, /device:TPU:9, one launch (start us, length us, event | category | flops | bytes accessed | tf_op | source)
XLA Modules:
  0.0 301.9 jit_solution(15350574891792011112)
XLA Ops:
  7.3 2.8 prelude.1
  10.0 1.4 fusion.2
  11.4 2.5 fusion.refs_0_
  14.6 8.5 %ln_qkv.1 = (bf16[768,1024]{1,0:T(8,128)(2,1)}, bf16[1024,2304]{1,0:T(8,128)(2,1)}) custom-call(bf16[1024,768]{1,0:T(8,128)(2,1)} %refs_2_, f32[768]{0:T(1024)S(1)} %copy-done.14, f32[768]{0:T(1024)S(1)} %copy-done.10, bf16[768,2304]{1,0:T(8,128)(2,1)} %refs_4_.1), custom_call_target="tpu_custom_call" | custom-call | flops 799999983616 | bytes 1048576 | tf_op jit(solution)/shard_map/ln_qkv/pallas_call | solution.py:278
  23.2 1.3 add.35.refs_0_
  24.5 1.2 collective-permute-start.1
  25.7 13.7 %attn_fwd.1 = (bf16[1024,768]{1,0:T(8,128)(2,1)S(1)}, bf16[768,1024]{1,0:T(8,128)(2,1)}, f32[6,2,1024]{2,1,0:T(2,128)S(1)}) custom-call(s32[3,4]{1,0:T(4,128)S(1)} %copy-done.28, bf16[1024,2304]{1,0:T(8,128)(2,1)} %get-tuple-element.107.q_ref.k_ref.v_ref, bf16[1024,2304]{1,0:T(8,128)(2,1)} %get-tuple-element.107.q_ref.k_ref.v_ref, ...), custom_call_target="tpu_custom_call" | custom-call | flops 1399999954944 | bytes 1048576 | tf_op jit(solution)/shard_map/attn_fwd/pallas_call | solution.py:124
  39.4 1.3 add.36.refs_0_
  40.8 1.1 collective-permute-start.2
  41.9 5.8 %proj_ln.1 = (f32[1024,768]{1,0:T(8,128)}, bf16[1024,768]{1,0:T(8,128)(2,1)S(1)}, bf16[1024,768]{1,0:T(8,128)(2,1)S(1)}) custom-call(bf16[1024,768]{1,0:T(8,128)(2,1)} %refs_2_, bf16[1024,768]{1,0:T(8,128)(2,1)S(1)} %get-tuple-element.112.mixed_ref, bf16[1024,768]{1,0:T(8,128)(2,1)} %refs_5_.2, f32[1024,128]{1,0:T(8,128)S(1)} %copy-done.23, ...), custom_call_target="tpu_custom_call" | custom-call | flops 699999977472 | bytes 1048576 | tf_op jit(solution)/shard_map/proj_ln/pallas_call | solution.py:362
  47.7 1.3 add.37.refs_0_
  49.3 10.9 %expert_part.3 = (bf16[1024,1024]{1,0:T(8,128)(2,1)}, bf16[1024,1024]{1,0:T(8,128)(2,1)}, bf16[4,2,64,768]{3,2,1,0:T(8,128)(2,1)}, bf16[4,2,64,768]{3,2,1,0:T(8,...) custom-call(s32[3]{0:T(128)S(1)} %copy-done.1, s32[4]{0:T(128)S(1)} %pad_add_fusion.place_ref.c_ref, ...), custom_call_target="tpu_custom_call" | custom-call | flops 1100000002048 | bytes 1048576 | tf_op jit(solution)/shard_map/expert_part/pallas_call | solution.py:448
  61.7 1.4 collective-permute-start.7
  63.1 1.3 add.38.refs_0_
  64.4 2.4 collective-permute-start.4
  66.8 11.2 %expert_part.4 = (bf16[1024,1024]{1,0:T(8,128)(2,1)}, bf16[1024,1024]{1,0:T(8,128)(2,1)}, bf16[8,4,2,2,32,768]{5,4,3,2,1,0:T(8,128)(2,1)}) custom-call(s32[3]{0:T(128)S(1)} %copy-done.1, s32[4]{0:T(128)S(1)} %pad_add_fusion.place_ref.c_ref, bf16[1024,768]{1,0:T(8,128)(2,1)S(1)} %get-tuple-element.124.h2_ref, ...), custom_call_target="tpu_custom_call" | custom-call | flops 1100000002048 | bytes 1048576 | tf_op jit(solution)/shard_map/expert_part/pallas_call | solution.py:448
  79.0 10.9 %expert_part.5 = (bf16[1024,1024]{1,0:T(8,128)(2,1)}, bf16[1024,1024]{1,0:T(8,128)(2,1)}, bf16[4,2,64,768]{3,2,1,0:T(8,128)(2,1)}, bf16[4,2,64,768]{3,2,1,0:T(8,...) custom-call(s32[3]{0:T(128)S(1)} %copy-done.1, s32[4]{0:T(128)S(1)} %pad_add_fusion.place_ref.c_ref, ...), custom_call_target="tpu_custom_call" | custom-call | flops 1100000002048 | bytes 1048576 | tf_op jit(solution)/shard_map/expert_part/pallas_call | solution.py:448
  90.8 16.4 %post_ffn.1 = (f32[1024,768]{1,0:T(8,128)}, bf16[1024,768]{1,0:T(8,128)(2,1)}, bf16[1024,768]{1,0:T(8,128)(2,1)}, f32[2,768]{1,0:T(2,128)S(1)}) custom-call(s32[3]{0:T(128)S(1)} %copy-done.1, bf16[1024,1024]{1,0:T(8,128)(2,1)} %get-tuple-element.126.refs_0_, bf16[1024,1024]{1,0:T(8,128)(2,1)} %get-tuple-element.128.refs_1_, ...), custom_call_target="tpu_custom_call" | custom-call | flops 999999995904 | bytes 1048576 | tf_op jit(solution)/shard_map/post_ffn/pallas_call | solution.py:500
  107.2 1.4 collective-permute-start.10
  108.6 4.5 %sum_sides.2 = (bf16[4,2,2,32,768]{4,3,2,1,0:T(8,128)(2,1)S(1)}, bf16[4,2,2,32,768]{4,3,2,1,0:T(8,128)(2,1)}) custom-call(s32[4]{0:T(128)S(1)} %pad_add_fusion.place_ref.c_ref, s32[8]{0:T(128)S(1)} %fusion.1.voice_ref, bf16[4,2,64,768]{3,2,1,0:T(8,128)(2,1)S(1)} %copy-done.24, bf16[4,2,64,768]{3,2,1,0:T(8,128)(2,1)} %collective-permute-done.5.b_ref, ...), custom_call_target="tpu_custom_call" | custom-call | flops 299999985664 | bytes 1048576 | tf_op jit(solution)/shard_map/sum_sides/pallas_call | solution.py:660
  113.5 11.8 %attn_bwd.2.refs_1_.refs_0_ = bf16[3,1024,384]{2,1,0:T(8,128)(2,1)S(1)} custom-call(s32[3,4]{1,0:T(4,128)S(1)} %copy-done.29, bf16[1024,2304]{1,0:T(8,128)(2,1)} %get-tuple-element.107.q_ref.k_ref.v_ref, bf16[1024,2304]{1,0:T(8,128)(2,1)} %get-tuple-element.107.q_ref.k_ref.v_ref, bf16[1024,2304]{1,0:T(8,128)(2,1)} %get-tuple-element.107.q_ref.k_ref.v_ref, ...), custom_call_target="tpu_custom_call" | custom-call | flops 1110000009216 | bytes 1048576 | tf_op jit(solution)/shard_map/attn_bwd/pallas_call | solution.py:218
  125.4 9.5 %weight_grads.2 = (bf16[384,1920]{1,0:T(8,128)(2,1)}, bf16[384,1920]{1,0:T(8,128)(2,1)}) custom-call(s32[4]{0:T(128)S(1)} %pad_add_fusion.place_ref.c_ref, bf16[768,1024]{1,0:T(8,128)(2,1)} %get-tuple-element.158.refs_0_, bf16[3,1024,384]{2,1,0:T(8,128)(2,1)S(1)} %attn_bwd.2.refs_1_.refs_0_, bf16[768,1024]{1,0:T(8,128)(2,1)} %get-tuple-element.139.ot_ref.refs_2_, ...), custom_call_target="tpu_custom_call" | custom-call | flops 599999971328 | bytes 1048576 | tf_op jit(solution)/shard_map/weight_grads/pallas_call | solution.py:583
  135.2 4.5 %sum_sides.3 = (bf16[4,2,2,32,768]{4,3,2,1,0:T(8,128)(2,1)S(1)}, bf16[4,2,2,32,768]{4,3,2,1,0:T(8,128)(2,1)}) custom-call(s32[4]{0:T(128)S(1)} %pad_add_fusion.place_ref.c_ref, s32[8]{0:T(128)S(1)} %fusion.1.voice_ref, bf16[4,2,64,768]{3,2,1,0:T(8,128)(2,1)S(1)} %copy-done.25, bf16[4,2,64,768]{3,2,1,0:T(8,128)(2,1)} %collective-permute-done.8.b_ref, ...), custom_call_target="tpu_custom_call" | custom-call | flops 299999985664 | bytes 1048576 | tf_op jit(solution)/shard_map/sum_sides/pallas_call | solution.py:660
  139.7 4.2 %collective-permute-done.11.refs_1_ = bf16[4,2,2,32,768]{4,3,2,1,0:T(8,128)(2,1)} collective-permute-done((bf16[4,2,2,32,768]{4,3,2,1,0:T(8,128)(2,1)}, bf16[4,2,2,32,768]{4,3,2,1,0:T(8,128)(2,1)}, u32[]{:S(2)}, u32[]{:S(2)}) %collective-permute-start.11) | collective-permute-done | bytes 786464 | tf_op jit(solution)/shard_map/ppermute | solution.py:779
  143.9 2.2 add.40
  146.2 1.1 copy-done.5
  147.4 1.3 split.2
  148.7 2.8 merge.1
  151.5 4.5 %all-to-all-start = ((bf16[4,96,1920]{2,1,0:T(8,128)(2,1)}), bf16[4,96,1920]{2,1,0:T(8,128)(2,1)}, u32[]{:S(2)}, u32[]{:S(2)}) async-start(bf16[4,96,1920]{2,1,0:T(8,128)(2,1)} %bitcast.12), calls=%async_computation.1 | async-start | bytes 2949120 | tf_op jit(solution)/shard_map/all_to_all | solution.py:907
  156.3 1.1 collective-permute-start.14
  157.5 11.8 %attn_bwd.3.refs_1_ = bf16[3,1024,384]{2,1,0:T(8,128)(2,1)S(1)} custom-call(s32[3,4]{1,0:T(4,128)S(1)} %copy-done.29, bf16[1024,2304]{1,0:T(8,128)(2,1)} %get-tuple-element.107.q_ref.k_ref.v_ref, bf16[1024,2304]{1,0:T(8,128)(2,1)} %get-tuple-element.107.q_ref.k_ref.v_ref, bf16[1024,2304]{1,0:T(8,128)(2,1)} %get-tuple-element.107.q_ref.k_ref.v_ref, ...), custom_call_target="tpu_custom_call" | custom-call | flops 1110000009216 | bytes 1048576 | tf_op jit(solution)/shard_map/attn_bwd/pallas_call | solution.py:218
  169.3 5.9 %weight_grads.3 = (bf16[384,1152]{1,0:T(8,128)(2,1)}, bf16[384,1152]{1,0:T(8,128)(2,1)}) custom-call(s32[4]{0:T(128)S(1)} %pad_add_fusion.place_ref.c_ref, bf16[768,1024]{1,0:T(8,128)(2,1)} %get-tuple-element.158.refs_0_, bf16[3,1024,384]{2,1,0:T(8,128)(2,1)S(1)} %attn_bwd.3.refs_1_), custom_call_target="tpu_custom_call" | custom-call | flops 359999995904 | bytes 1048576 | tf_op jit(solution)/shard_map/weight_grads/pallas_call | solution.py:583
  175.2 2.2 add.41
  177.5 4.7 %collective-permute-done.14.refs_1_ = bf16[2,2,2,32,768]{4,3,2,1,0:T(8,128)(2,1)} collective-permute-done((bf16[2,2,2,32,768]{4,3,2,1,0:T(8,128)(2,1)}, bf16[2,2,2,32,768]{4,3,2,1,0:T(8,128)(2,1)}, u32[]{:S(2)}, u32[]{:S(2)}) %collective-permute-start.14) | collective-permute-done | bytes 393248 | tf_op jit(solution)/shard_map/ppermute | solution.py:779
  182.2 1.1 split.3
  183.3 1.2 collective-permute-start.15
  184.5 1.8 collective-permute-start.16
  186.3 1.6 total.2.refs_0_
  187.9 1.1 collective-permute-start.17
  190.0 1.2 copies.2
  191.3 3.7 %all-to-all-start.1 = ((bf16[4,2,2,2,32,768]{5,4,3,2,1,0:T(8,128)(2,1)}), bf16[4,2,2,2,32,768]{5,4,3,2,1,0:T(8,128)(2,1)S(1)}, u32[]{:S(2)}, u32[]{:S(2)}) async-start(bf16[4,2,2,2,32,768]{5,4,3,2,1,0:T(8,128)(2,1)} %copies.2), calls=%async_computation.3 | async-start | bytes 3145728 | tf_op jit(solution)/shard_map/all_to_all | solution.py:907
  195.0 9.8 %input_grad.1 = (f32[1024,768]{1,0:T(8,128)}, f32[2,768]{1,0:T(2,128)S(1)}) custom-call(bf16[3,1024,384]{2,1,0:T(8,128)(2,1)} %copy-done.17, bf16[3,1024,384]{2,1,0:T(8,128)(2,1)} %copy-done.18, bf16[1024,768]{1,0:T(8,128)(2,1)} %refs_2_, f32[1024,768]{1,0:T(8,128)} %get-tuple-element.135.refs_3_, bf16[768,2304]{1,0:T(8,128)(2,1)} %refs_4_.1, f32[768]{0:T(1024)S(1)} %copy-done.15), custom_call_target="tpu_custom_call" | custom-call | flops 12999999488 | bytes 1048576 | tf_op jit(solution)/shard_map/input_grad/pallas_call | solution.py:621
  204.8 8.8 %all-to-all-done.1.refs_0_ = bf16[4,2,2,2,32,768]{5,4,3,2,1,0:T(8,128)(2,1)S(1)} async-done(((bf16[4,2,2,2,32,768]{5,4,3,2,1,0:T(8,128)(2,1)}), bf16[4,2,2,2,32,768]{5,4,3,2,1,0:T(8,128)(2,1)S(1)}, u32[]{:S(2)}, u32[]{:S(2)}) %all-to-all-start.1) | async-done | bytes 1572896 | tf_op jit(solution)/shard_map/all_to_all | solution.py:907
  213.6 1.2 copy-done.16
  216.0 3.5 %all-to-all-start.2 = ((bf16[4,112,1152]{2,1,0:T(8,128)(2,1)}), bf16[4,112,1152]{2,1,0:T(8,128)(2,1)S(1)}, u32[]{:S(2)}, u32[]{:S(2)}) async-start(bf16[4,112,1152]{2,1,0:T(8,128)(2,1)} %copy-done), calls=%async_computation.4 | async-start | bytes 2064384 | tf_op jit(solution)/shard_map/all_to_all | solution.py:907
  220.4 10.6 %result_of.1 = bf16[1024,768]{1,0:T(8,128)(2,1)} custom-call(s32[3]{0:T(128)S(1)} %copy-done.2, bf16[1024,1024]{1,0:T(8,128)(2,1)} %get-tuple-element.122.refs_0_, bf16[1024,1024]{1,0:T(8,128)(2,1)} %get-tuple-element.119.refs_1_, bf16[1024,1024]{1,0:T(8,128)(2,1)} %get-tuple-element.125.refs_2_, bf16[2,3072,768]{2,1,0:T(8,128)(2,1)} %refs_3_.3, ...), custom_call_target="tpu_custom_call" | custom-call | flops 10400000000 | bytes 1048576 | tf_op jit(solution)/shard_map/result_of/pallas_call | solution.py:533
  231.0 1.4 all-to-all-done.2.refs_0_
  235.1 4.2 %all-to-all-start.3 = ((bf16[4,1,2,2,32,768]{5,4,3,2,1,0:T(8,128)(2,1)}), bf16[4,1,2,2,32,768]{5,4,3,2,1,0:T(8,128)(2,1)}, u32[]{:S(2)}, u32[]{:S(2)}) async-start(bf16[4,1,2,2,32,768]{5,4,3,2,1,0:T(8,128)(2,1)} %copies.3), calls=%async_computation.6 | async-start | bytes 1572864 | tf_op jit(solution)/shard_map/all_to_all | solution.py:907
  239.4 1.3 collective-permute-start.20
  240.7 14.0 %collective-permute-done.19.refs_1_ = bf16[96,1920]{1,0:T(8,128)(2,1)S(1)} collective-permute-done((bf16[96,1920]{1,0:T(8,128)(2,1)S(1)}, bf16[96,1920]{1,0:T(8,128)(2,1)S(1)}, u32[]{:S(2)}, u32[]{:S(2)}) %collective-permute-start.19) | collective-permute-done | bytes 368672 | tf_op jit(solution)/shard_map/ppermute | solution.py:787
  255.5 1.3 collective-permute-start.23
  256.9 1.3 collective-permute-start.21
  258.2 2.1 collective-permute-done.20.refs_1_
  261.0 1.3 collective-permute-start.26
  262.3 3.9 %finish_experts.1 = (f32[2,768,384]{2,1,0:T(8,128)}, f32[2,384,768]{2,1,0:T(8,128)}, s32[2]{0:T(128)}) custom-call(s32[4]{0:T(128)S(1)} %copy-done.4, f32[1,768]{1,0:T(1,128)S(1)} %add.39.tally_ref, bf16[4,2,2,2,32,768]{5,4,3,2,1,0:T(8,128)(2,1)S(1)} %all-to-all-done.1.refs_0_, bf16[4,1,2,2,32,768]{5,4,3,2,1,0:T(8,128)(2,1)} %all-to-all-done.3.refs_1_), custom_call_target="tpu_custom_call" | custom-call | flops 399999991808 | bytes 1048576 | tf_op jit(solution)/shard_map/finish_experts/pallas_call | solution.py:704
  266.2 1.4 collective-permute-start.24
  267.6 8.4 %collective-permute-done.22.refs_2_ = bf16[96,1920]{1,0:T(8,128)(2,1)} collective-permute-done((bf16[96,1920]{1,0:T(8,128)(2,1)}, bf16[96,1920]{1,0:T(8,128)(2,1)}, u32[]{:S(2)}, u32[]{:S(2)}) %collective-permute-start.22) | collective-permute-done | bytes 368672 | tf_op jit(solution)/shard_map/ppermute | solution.py:779
  276.1 1.4 stack.22.refs_0_
  277.5 4.4 %collective-permute-start.27 = (bf16[4,96,1920]{2,1,0:T(8,128)(2,1)S(1)}, bf16[4,96,1920]{2,1,0:T(8,128)(2,1)S(1)}, u32[]{:S(2)}, u32[]{:S(2)}) collective-permute-start(bf16[4,96,1920]{2,1,0:T(8,128)(2,1)S(1)} %stack.22.refs_0_), channel_id=1, source_target_pairs={{0,1},{1,0},{2,3},{3,2},{4,5},{5,4},{6,7},{7,6},{8,9},{9,8},{10,11... | collective-permute-start | bytes 4423688 | tf_op jit(solution)/shard_map/ppermute | solution.py:775
  281.9 2.5 collective-permute-done.25.refs_2_
  284.4 1.3 stack.23.refs_2_
  285.6 2.4 collective-permute-start.28
  288.1 2.3 collective-permute-done.28.refs_3_
  290.3 4.4 %join_weights.1 = (f32[2,384,2304]{2,1,0:T(8,128)}, f32[2,384,768]{2,1,0:T(8,128)}, f32[8,768]{1,0:T(8,128)S(1)}) custom-call(s32[4]{0:T(128)S(1)} %copy-done.4, bf16[4,96,1920]{2,1,0:T(8,128)(2,1)S(1)} %stack.22.refs_0_, bf16[4,96,1920]{2,1,0:T(8,128)(2,1)S(1)} %collective-permute-done.27.refs_1_, bf16[4,112,1152]{2,1,0:T(8,128)(2,1)S(1)} %stack.23.refs_2_, ...), custom_call_target="tpu_custom_call" | custom-call | flops 499999997952 | bytes 1048576 | tf_op jit(solution)/shard_map/join_weights/pallas_call | solution.py:745
  (116 shorter events, 13.9 us)
Async XLA Ops:
  7.2 139.0 %reduce-scatter.4.cloned.1.call-start = ((), (), s32[]{:S(2)}) async-start(), calls=%async_computation.7 | async-start | bytes 7077888 | tf_op jit(solution)/shard_map/reduce_scatter | solution.py:946
  7.2 7.4 %copy-start.10 = (f32[768]{0:T(1024)S(1)}, f32[768]{0:T(1024)}, u32[]{:S(2)}) copy-start(f32[768]{0:T(1024)} %shift_ref.2) | copy-start | bytes 9220
  7.2 7.4 %copy-start.14 = (f32[768]{0:T(1024)S(1)}, f32[768]{0:T(1024)}, u32[]{:S(2)}) copy-start(f32[768]{0:T(1024)} %refs_5_.3) | copy-start | bytes 9220
  13.9 9.2 %collective-permute-start = (f32[1,768]{1,0:T(1,128)}, f32[1,768]{1,0:T(1,128)}, u32[]{:S(2)}, u32[]{:S(2)}) collective-permute-start(f32[1,768]{1,0:T(1,128)} %fusion.refs_0_), channel_id=1, source_target_pairs={{0,1},{1,0},{2,3},{3,2},{4,5},{5,4},{6,7},{7,6},{8,9},{9,8},{10,11... | collective-permute-start | bytes 9224 | tf_op jit(solution)/shard_map/ppermute | solution.py:775
  23.1 159.1 %copy-start.3 = (s32[4]{0:T(128)}, s32[4]{0:T(128)S(1)}, u32[]{:S(2)}) copy-start(s32[4]{0:T(128)S(1)} %pad_add_fusion.place_ref.c_ref) | copy-start | bytes 52
  23.1 2.6 copy-start.20
  23.1 2.6 copy-start.26
  23.1 2.6 copy-start.28
  24.5 14.9 %collective-permute-start.1 = (f32[1,768]{1,0:T(1,128)}, f32[1,768]{1,0:T(1,128)}, u32[]{:S(2)}, u32[]{:S(2)}) collective-permute-start(f32[1,768]{1,0:T(1,128)} %add.35.refs_0_), channel_id=1, source_target_pairs={{0,8},{8,0},{16,24},{24,16},{1,9},{9,1},{17,25},{25,17},{2,10},{10... | collective-permute-start | bytes 9224 | tf_op jit(solution)/shard_map/ppermute | solution.py:779
  39.4 2.4 copy-start.11
  39.4 2.4 copy-start.12
  39.4 2.4 copy-start.23
  40.8 6.9 %collective-permute-start.2 = (f32[1,768]{1,0:T(1,128)}, f32[1,768]{1,0:T(1,128)}, u32[]{:S(2)}, u32[]{:S(2)}) collective-permute-start(f32[1,768]{1,0:T(1,128)} %add.36.refs_0_), channel_id=1, source_target_pairs={{0,16},{8,24},{16,0},{24,8},{1,17},{9,25},{17,1},{25,9},{2,18},{10... | collective-permute-start | bytes 9224 | tf_op jit(solution)/shard_map/ppermute | solution.py:779
  47.6 1.7 copy-start.1
  48.9 14.2 %collective-permute-start.3 = (f32[1,768]{1,0:T(1,128)}, f32[1,768]{1,0:T(1,128)}, u32[]{:S(2)}, u32[]{:S(2)}) collective-permute-start(f32[1,768]{1,0:T(1,128)} %add.37.refs_0_), channel_id=1, source_target_pairs={{0,2},{2,0},{4,6},{6,4},{1,3},{3,1},{5,7},{7,5},{8,10},{10,8},{12,... | collective-permute-start | bytes 9224 | tf_op jit(solution)/shard_map/ppermute | solution.py:787
  60.8 47.7 %collective-permute-start.5 = (bf16[4,2,64,768]{3,2,1,0:T(8,128)(2,1)}, bf16[4,2,64,768]{3,2,1,0:T(8,128)(2,1)}, u32[]{:S(2)}, u32[]{:S(2)}) collective-permute-start(bf16[4,2,64,768]{3,2,1,0:T(8,128)(2,1)} %get-tuple-element.132), channel_id=1, source_target_pairs={{0,1},{1,0},{2,3},{3,2},{4,5},{5,4},{6,7},{7,6},{8,9},{9,8},{10,11... | collective-permute-start | bytes 2359304 | tf_op jit(solution)/shard_map/ppermute | solution.py:775
  61.5 47.1 %collective-permute-start.6 = (bf16[4,2,64,768]{3,2,1,0:T(8,128)(2,1)}, bf16[4,2,64,768]{3,2,1,0:T(8,128)(2,1)}, u32[]{:S(2)}, u32[]{:S(2)}) collective-permute-start(bf16[4,2,64,768]{3,2,1,0:T(8,128)(2,1)} %get-tuple-element.133), channel_id=1, source_target_pairs={{0,8},{8,0},{16,24},{24,16},{1,9},{9,1},{17,25},{25,17},{2,10},{10... | collective-permute-start | bytes 2359304 | tf_op jit(solution)/shard_map/ppermute | solution.py:779
  61.7 45.4 %collective-permute-start.7 = (bf16[4,2,64,768]{3,2,1,0:T(8,128)(2,1)}, bf16[4,2,64,768]{3,2,1,0:T(8,128)(2,1)}, u32[]{:S(2)}, u32[]{:S(2)}) collective-permute-start(bf16[4,2,64,768]{3,2,1,0:T(8,128)(2,1)} %get-tuple-element.134), channel_id=1, source_target_pairs={{0,9},{1,8},{8,1},{9,0},{16,25},{17,24},{24,17},{25,16},{2,11},{3,... | collective-permute-start | bytes 2359304 | tf_op jit(solution)/shard_map/ppermute | solution.py:783
  64.4 13.9 %collective-permute-start.4 = (f32[1,768]{1,0:T(1,128)}, f32[1,768]{1,0:T(1,128)}, u32[]{:S(2)}, u32[]{:S(2)}) collective-permute-start(f32[1,768]{1,0:T(1,128)} %add.38.refs_0_), channel_id=1, source_target_pairs={{0,6},{6,0},{2,4},{4,2},{1,7},{7,1},{3,5},{5,3},{8,14},{14,8},{10,... | collective-permute-start | bytes 9224 | tf_op jit(solution)/shard_map/ppermute | solution.py:787
  78.1 111.0 %reduce-scatter.6.cloned.1.call-start = ((), (), s32[]{:S(2)}) async-start(), calls=%async_computation.8 | async-start | bytes 983040 | tf_op jit(solution)/shard_map/reduce_scatter | solution.py:966
  79.0 11.8 %copy-start.13 = (f32[768]{0:T(1024)S(1)}, f32[768]{0:T(1024)}, u32[]{:S(2)}) copy-start(f32[768]{0:T(1024)} %refs_7_.1) | copy-start | bytes 9220
  89.9 45.3 %collective-permute-start.8 = (bf16[4,2,64,768]{3,2,1,0:T(8,128)(2,1)}, bf16[4,2,64,768]{3,2,1,0:T(8,128)(2,1)}, u32[]{:S(2)}, u32[]{:S(2)}) collective-permute-start(bf16[4,2,64,768]{3,2,1,0:T(8,128)(2,1)} %get-tuple-element.146), channel_id=1, source_target_pairs={{0,1},{1,0},{2,3},{3,2},{4,5},{5,4},{6,7},{7,6},{8,9},{9,8},{10,11... | collective-permute-start | bytes 2359304 | tf_op jit(solution)/shard_map/ppermute | solution.py:775
  90.4 44.8 %collective-permute-start.9 = (bf16[4,2,64,768]{3,2,1,0:T(8,128)(2,1)}, bf16[4,2,64,768]{3,2,1,0:T(8,128)(2,1)}, u32[]{:S(2)}, u32[]{:S(2)}) collective-permute-start(bf16[4,2,64,768]{3,2,1,0:T(8,128)(2,1)} %get-tuple-element.147), channel_id=1, source_target_pairs={{0,16},{8,24},{16,0},{24,8},{1,17},{9,25},{17,1},{25,9},{2,18},{10... | collective-permute-start | bytes 2359304 | tf_op jit(solution)/shard_map/ppermute | solution.py:779
  90.8 17.7 %copy-start.24 = (bf16[4,2,64,768]{3,2,1,0:T(8,128)(2,1)S(1)}, bf16[4,2,64,768]{3,2,1,0:T(8,128)(2,1)}, u32[]{:S(2)}) copy-start(bf16[4,2,64,768]{3,2,1,0:T(8,128)(2,1)} %get-tuple-element.131.a_ref) | copy-start | bytes 2359300
  107.2 28.0 %collective-permute-start.10 = (bf16[4,2,64,768]{3,2,1,0:T(8,128)(2,1)}, bf16[4,2,64,768]{3,2,1,0:T(8,128)(2,1)}, u32[]{:S(2)}, u32[]{:S(2)}) collective-permute-start(bf16[4,2,64,768]{3,2,1,0:T(8,128)(2,1)} %get-tuple-element.148), channel_id=1, source_target_pairs={{0,17},{1,16},{8,25},{9,24},{16,1},{17,0},{24,9},{25,8},{2,19},{3,... | collective-permute-start | bytes 2359304 | tf_op jit(solution)/shard_map/ppermute | solution.py:783
  108.6 4.9 %copy-start.21 = (f32[1024,128]{1,0:T(8,128)S(1)}, f32[1024,128]{1,0:T(8,128)}, u32[]{:S(2)}) copy-start(f32[1024,128]{1,0:T(8,128)} %get-tuple-element.108.seg_col_ref) | copy-start | bytes 1572868
  108.6 4.9 %copy-start.27 = (f32[1,1024]{1,0:T(1,128)S(1)}, f32[1,1024]{1,0:T(1,128)}, u32[]{:S(2)}) copy-start(f32[1,1024]{1,0:T(1,128)} %get-tuple-element.109.seg_row_ref) | copy-start | bytes 12292
  108.6 4.9 %copy-start.29 = (s32[3,4]{1,0:T(4,128)S(1)}, s32[3,4]{1,0:T(4,128)}, u32[]{:S(2)}) copy-start(s32[3,4]{1,0:T(4,128)} %get-tuple-element.103.lo_ref) | copy-start | bytes 148
  113.1 30.8 %collective-permute-start.11 = (bf16[4,2,2,32,768]{4,3,2,1,0:T(8,128)(2,1)}, bf16[4,2,2,32,768]{4,3,2,1,0:T(8,128)(2,1)}, u32[]{:S(2)}, u32[]{:S(2)}) collective-permute-start(bf16[4,2,2,32,768]{4,3,2,1,0:T(8,128)(2,1)} %get-tuple-element.153), channel_id=1, source_target_pairs={{0,16},{8,24},{16,0},{24,8},{1,17},{9,25},{17,1},{25,9},{2,18},{10... | collective-permute-start | bytes 2359304 | tf_op jit(solution)/shard_map/ppermute | solution.py:779
  125.3 9.5 %copy-start.17 = (bf16[3,1024,384]{2,1,0:T(8,128)(2,1)}, bf16[3,1024,384]{2,1,0:T(8,128)(2,1)S(1)}, u32[]{:S(2)}) copy-start(bf16[3,1024,384]{2,1,0:T(8,128)(2,1)S(1)} %attn_bwd.2.refs_1_.refs_0_) | copy-start | bytes 7077892
  125.3 9.8 %copy-start.25 = (bf16[4,2,64,768]{3,2,1,0:T(8,128)(2,1)S(1)}, bf16[4,2,64,768]{3,2,1,0:T(8,128)(2,1)}, u32[]{:S(2)}) copy-start(bf16[4,2,64,768]{3,2,1,0:T(8,128)(2,1)} %get-tuple-element.145.a_ref) | copy-start | bytes 2359300
  134.8 13.9 %collective-permute-start.12 = (bf16[384,1920]{1,0:T(8,128)(2,1)}, bf16[384,1920]{1,0:T(8,128)(2,1)}, u32[]{:S(2)}, u32[]{:S(2)}) collective-permute-start(bf16[384,1920]{1,0:T(8,128)(2,1)} %get-tuple-element.149), channel_id=1, source_target_pairs={{0,1},{1,0},{2,3},{3,2},{4,5},{5,4},{6,7},{7,6},{8,9},{9,8},{10,11... | collective-permute-start | bytes 4423688 | tf_op jit(solution)/shard_map/ppermute | solution.py:775
  139.7 35.6 %collective-permute-start.13 = (bf16[4,2,2,32,768]{4,3,2,1,0:T(8,128)(2,1)}, bf16[4,2,2,32,768]{4,3,2,1,0:T(8,128)(2,1)}, u32[]{:S(2)}, u32[]{:S(2)}) collective-permute-start(bf16[4,2,2,32,768]{4,3,2,1,0:T(8,128)(2,1)} %get-tuple-element.161), channel_id=1, source_target_pairs={{0,8},{8,0},{16,24},{24,16},{1,9},{9,1},{17,25},{25,17},{2,10},{10... | collective-permute-start | bytes 2359304 | tf_op jit(solution)/shard_map/ppermute | solution.py:779
  146.2 1.1 copy-start.5
  147.3 1.4 copy-start.19
  151.5 5.9 %copy-start.22 = (f32[1024,128]{1,0:T(8,128)S(1)}, f32[1024,128]{1,0:T(8,128)}, u32[]{:S(2)}) copy-start(f32[1024,128]{1,0:T(8,128)} %get-tuple-element.108.seg_col_ref) | copy-start | bytes 1572868
  151.5 34.8 %all-to-all-start = ((bf16[4,96,1920]{2,1,0:T(8,128)(2,1)}), bf16[4,96,1920]{2,1,0:T(8,128)(2,1)}, u32[]{:S(2)}, u32[]{:S(2)}) async-start(bf16[4,96,1920]{2,1,0:T(8,128)(2,1)} %bitcast.12), calls=%async_computation.1 | async-start | bytes 2949120 | tf_op jit(solution)/shard_map/all_to_all | solution.py:907
  156.0 77.2 %reduce-scatter.8.cloned.1.call-start = ((), (), s32[]{:S(2)}) async-start(), calls=%async_computation.9 | async-start | bytes 983040 | tf_op jit(solution)/shard_map/reduce_scatter | solution.py:966
  156.3 25.9 %collective-permute-start.14 = (bf16[2,2,2,32,768]{4,3,2,1,0:T(8,128)(2,1)}, bf16[2,2,2,32,768]{4,3,2,1,0:T(8,128)(2,1)}, u32[]{:S(2)}, u32[]{:S(2)}) collective-permute-start(bf16[2,2,2,32,768]{4,3,2,1,0:T(8,128)(2,1)} %get-tuple-element.163), channel_id=1, source_target_pairs={{0,16},{8,24},{16,0},{24,8},{1,17},{9,25},{17,1},{25,9},{2,18},{10... | collective-permute-start | bytes 1179656 | tf_op jit(solution)/shard_map/ppermute | solution.py:779
  169.3 5.9 %copy-start.18 = (bf16[3,1024,384]{2,1,0:T(8,128)(2,1)}, bf16[3,1024,384]{2,1,0:T(8,128)(2,1)S(1)}, u32[]{:S(2)}) copy-start(bf16[3,1024,384]{2,1,0:T(8,128)(2,1)S(1)} %attn_bwd.3.refs_1_) | copy-start | bytes 7077892
  183.3 5.7 %collective-permute-start.15 = (bf16[2,2,32,768]{3,2,1,0:T(8,128)(2,1)S(1)}, bf16[2,2,32,768]{3,2,1,0:T(8,128)(2,1)S(1)}, u32[]{:S(2)}, u32[]{:S(2)}) collective-permute-start(bf16[2,2,32,768]{3,2,1,0:T(8,128)(2,1)S(1)} %get-tuple-element.168), channel_id=1, source_target_pairs={{0,8},{8,0},{16,24},{24,16},{1,9},{9,1},{17,25},{25,17},{2,10},{10... | collective-permute-start | bytes 589832 | tf_op jit(solution)/shard_map/ppermute | solution.py:779
  184.5 29.2 %collective-permute-start.16 = (bf16[384,1152]{1,0:T(8,128)(2,1)}, bf16[384,1152]{1,0:T(8,128)(2,1)S(1)}, u32[]{:S(2)}, u32[]{:S(2)}) collective-permute-start(bf16[384,1152]{1,0:T(8,128)(2,1)} %get-tuple-element.159), channel_id=1, source_target_pairs={{0,1},{1,0},{2,3},{3,2},{4,5},{5,4},{6,7},{7,6},{8,9},{9,8},{10,11... | collective-permute-start | bytes 2654216 | tf_op jit(solution)/shard_map/ppermute | solution.py:775
  187.9 31.7 %collective-permute-start.17 = (bf16[96,1920]{1,0:T(8,128)(2,1)S(1)}, bf16[96,1920]{1,0:T(8,128)(2,1)S(1)}, u32[]{:S(2)}, u32[]{:S(2)}) collective-permute-start(bf16[96,1920]{1,0:T(8,128)(2,1)S(1)} %total.2.refs_0_), channel_id=1, source_target_pairs={{0,2},{2,0},{4,6},{6,4},{1,3},{3,1},{5,7},{7,5},{8,10},{10,8},{12,... | collective-permute-start | bytes 1105928 | tf_op jit(solution)/shard_map/ppermute | solution.py:787
  189.1 0.9 copy-start.8
  191.3 3.7 %copy-start.15 = (f32[768]{0:T(1024)S(1)}, f32[768]{0:T(1024)}, u32[]{:S(2)}) copy-start(f32[768]{0:T(1024)} %refs_5_.3) | copy-start | bytes 9220
  191.3 22.4 %all-to-all-start.1 = ((bf16[4,2,2,2,32,768]{5,4,3,2,1,0:T(8,128)(2,1)}), bf16[4,2,2,2,32,768]{5,4,3,2,1,0:T(8,128)(2,1)S(1)}, u32[]{:S(2)}, u32[]{:S(2)}) async-start(bf16[4,2,2,2,32,768]{5,4,3,2,1,0:T(8,128)(2,1)} %copies.2), calls=%async_computation.3 | async-start | bytes 3145728 | tf_op jit(solution)/shard_map/all_to_all | solution.py:907
  213.6 1.2 copy-start.16
  215.0 1.0 copy-start
  216.0 16.4 %all-to-all-start.2 = ((bf16[4,112,1152]{2,1,0:T(8,128)(2,1)}), bf16[4,112,1152]{2,1,0:T(8,128)(2,1)S(1)}, u32[]{:S(2)}, u32[]{:S(2)}) async-start(bf16[4,112,1152]{2,1,0:T(8,128)(2,1)} %copy-done), calls=%async_computation.4 | async-start | bytes 2064384 | tf_op jit(solution)/shard_map/all_to_all | solution.py:907
  231.0 2.0 copy-start.7
  232.5 6.8 %collective-permute-start.18 = (bf16[112,1152]{1,0:T(8,128)(2,1)S(1)}, bf16[112,1152]{1,0:T(8,128)(2,1)S(1)}, u32[]{:S(2)}, u32[]{:S(2)}) collective-permute-start(bf16[112,1152]{1,0:T(8,128)(2,1)S(1)} %total.3.refs_0_), channel_id=1, source_target_pairs={{0,2},{2,0},{4,6},{6,4},{1,3},{3,1},{5,7},{7,5},{8,10},{10,8},{12,... | collective-permute-start | bytes 774152 | tf_op jit(solution)/shard_map/ppermute | solution.py:787
  233.0 21.7 %collective-permute-start.19 = (bf16[96,1920]{1,0:T(8,128)(2,1)S(1)}, bf16[96,1920]{1,0:T(8,128)(2,1)S(1)}, u32[]{:S(2)}, u32[]{:S(2)}) collective-permute-start(bf16[96,1920]{1,0:T(8,128)(2,1)S(1)} %copy-done.7), channel_id=1, source_target_pairs={{0,6},{6,0},{2,4},{4,2},{1,7},{7,1},{3,5},{5,3},{8,14},{14,8},{10,... | collective-permute-start | bytes 1105928 | tf_op jit(solution)/shard_map/ppermute | solution.py:787
  233.2 0.9 copy-start.9
  235.1 27.3 %all-to-all-start.3 = ((bf16[4,1,2,2,32,768]{5,4,3,2,1,0:T(8,128)(2,1)}), bf16[4,1,2,2,32,768]{5,4,3,2,1,0:T(8,128)(2,1)}, u32[]{:S(2)}, u32[]{:S(2)}) async-start(bf16[4,1,2,2,32,768]{5,4,3,2,1,0:T(8,128)(2,1)} %copies.3), calls=%async_computation.6 | async-start | bytes 1572864 | tf_op jit(solution)/shard_map/all_to_all | solution.py:907
  239.4 20.9 %collective-permute-start.20 = (bf16[112,1152]{1,0:T(8,128)(2,1)S(1)}, bf16[112,1152]{1,0:T(8,128)(2,1)S(1)}, u32[]{:S(2)}, u32[]{:S(2)}) collective-permute-start(bf16[112,1152]{1,0:T(8,128)(2,1)S(1)} %add.44.refs_0_), channel_id=1, source_target_pairs={{0,6},{6,0},{2,4},{4,2},{1,7},{7,1},{3,5},{5,3},{8,14},{14,8},{10,... | collective-permute-start | bytes 774152 | tf_op jit(solution)/shard_map/ppermute | solution.py:787
  255.5 6.8 %copy-start.4 = (s32[4]{0:T(128)S(1)}, s32[4]{0:T(128)}, u32[]{:S(2)}) copy-start(s32[4]{0:T(128)} %copy-done.3) | copy-start | bytes 52
  255.5 10.7 %collective-permute-start.23 = (bf16[96,1920]{1,0:T(8,128)(2,1)}, bf16[96,1920]{1,0:T(8,128)(2,1)}, u32[]{:S(2)}, u32[]{:S(2)}) collective-permute-start(bf16[96,1920]{1,0:T(8,128)(2,1)} %add.45.refs_0_), channel_id=1, source_target_pairs={{0,24},{8,16},{16,8},{24,0},{1,25},{9,17},{17,9},{25,1},{2,26},{10... | collective-permute-start | bytes 1105928 | tf_op jit(solution)/shard_map/ppermute | solution.py:779
  256.8 19.3 %collective-permute-start.22 = (bf16[96,1920]{1,0:T(8,128)(2,1)}, bf16[96,1920]{1,0:T(8,128)(2,1)}, u32[]{:S(2)}, u32[]{:S(2)}) collective-permute-start(bf16[96,1920]{1,0:T(8,128)(2,1)} %add.45.refs_0_), channel_id=1, source_target_pairs={{0,16},{8,24},{16,0},{24,8},{1,17},{9,25},{17,1},{25,9},{2,18},{10... | collective-permute-start | bytes 1105928 | tf_op jit(solution)/shard_map/ppermute | solution.py:779
  256.9 19.2 %collective-permute-start.21 = (bf16[96,1920]{1,0:T(8,128)(2,1)}, bf16[96,1920]{1,0:T(8,128)(2,1)}, u32[]{:S(2)}, u32[]{:S(2)}) collective-permute-start(bf16[96,1920]{1,0:T(8,128)(2,1)} %add.45.refs_0_), channel_id=1, source_target_pairs={{0,8},{8,0},{16,24},{24,16},{1,9},{9,1},{17,25},{25,17},{2,10},{10... | collective-permute-start | bytes 1105928 | tf_op jit(solution)/shard_map/ppermute | solution.py:779
  261.0 20.9 %collective-permute-start.26 = (bf16[112,1152]{1,0:T(8,128)(2,1)}, bf16[112,1152]{1,0:T(8,128)(2,1)}, u32[]{:S(2)}, u32[]{:S(2)}) collective-permute-start(bf16[112,1152]{1,0:T(8,128)(2,1)} %add.46.refs_0_), channel_id=1, source_target_pairs={{0,24},{8,16},{16,8},{24,0},{1,25},{9,17},{17,9},{25,1},{2,26},{10... | collective-permute-start | bytes 774152 | tf_op jit(solution)/shard_map/ppermute | solution.py:779
  262.3 22.1 %collective-permute-start.25 = (bf16[112,1152]{1,0:T(8,128)(2,1)}, bf16[112,1152]{1,0:T(8,128)(2,1)}, u32[]{:S(2)}, u32[]{:S(2)}) collective-permute-start(bf16[112,1152]{1,0:T(8,128)(2,1)} %add.46.refs_0_), channel_id=1, source_target_pairs={{0,16},{8,24},{16,0},{24,8},{1,17},{9,25},{17,1},{25,9},{2,18},{10... | collective-permute-start | bytes 774152 | tf_op jit(solution)/shard_map/ppermute | solution.py:779
  266.2 18.1 %collective-permute-start.24 = (bf16[112,1152]{1,0:T(8,128)(2,1)}, bf16[112,1152]{1,0:T(8,128)(2,1)S(1)}, u32[]{:S(2)}, u32[]{:S(2)}) collective-permute-start(bf16[112,1152]{1,0:T(8,128)(2,1)} %add.46.refs_0_), channel_id=1, source_target_pairs={{0,8},{8,0},{16,24},{24,16},{1,9},{9,1},{17,25},{25,17},{2,10},{10... | collective-permute-start | bytes 774152 | tf_op jit(solution)/shard_map/ppermute | solution.py:779
  277.5 12.8 %collective-permute-start.27 = (bf16[4,96,1920]{2,1,0:T(8,128)(2,1)S(1)}, bf16[4,96,1920]{2,1,0:T(8,128)(2,1)S(1)}, u32[]{:S(2)}, u32[]{:S(2)}) collective-permute-start(bf16[4,96,1920]{2,1,0:T(8,128)(2,1)S(1)} %stack.22.refs_0_), channel_id=1, source_target_pairs={{0,1},{1,0},{2,3},{3,2},{4,5},{5,4},{6,7},{7,6},{8,9},{9,8},{10,11... | collective-permute-start | bytes 4423688 | tf_op jit(solution)/shard_map/ppermute | solution.py:775
  285.6 4.7 %collective-permute-start.28 = (bf16[4,112,1152]{2,1,0:T(8,128)(2,1)S(1)}, bf16[4,112,1152]{2,1,0:T(8,128)(2,1)S(1)}, u32[]{:S(2)}, u32[]{:S(2)}) collective-permute-start(bf16[4,112,1152]{2,1,0:T(8,128)(2,1)S(1)} %stack.23.refs_2_), channel_id=1, source_target_pairs={{0,1},{1,0},{2,3},{3,2},{4,5},{5,4},{6,7},{7,6},{8,9},{9,8},{10,11... | collective-permute-start | bytes 3096584 | tf_op jit(solution)/shard_map/ppermute | solution.py:775
  (2 other events, 1.6 us)
Sparse Core Ops, SparseCore 0:
  78.2 66.4 reduce-scatter.3
  147.0 20.6 reduce-scatter.5
  186.4 25.1 reduce-scatter.7
where the time goes:
time: 304 us; the launch traced here: 302 us
  Pallas kernels  181 us (60%)
  waiting for transfers between devices  48.5 us (16%)
  starting transfers between devices  47 us (15%)
  between operations  14.1 us (5%)
  local copies, waits for them, and re-layouts  7.94 us (3%)
  other arithmetic  3.26 us (1%)
    pallas_call x3, Pallas kernels, expert_part(): pl.pallas_call(functools.partial(expert_kernel, axis), grid_spec=pltpu.Pr...  33 us
    pallas_call x2, Pallas kernels, attn_bwd(): pl.pallas_call(functools.partial(bwd_kernel, qb, win), out_shape=pltpu.VM...  23.7 us
    pallas_call x19, Pallas kernels, small(): pl.pallas_call(functools.partial(small_kernel, fn), in_specs=[resident()]...  21.6 us
    ppermute x14, waiting for transfers between devices, swap(): return lax.ppermute(v, 'dp', [(i, i ^ axis) for i in range(4)])  19.8 us
    pallas_call x1, Pallas kernels, post_ffn(): pl.pallas_call(functools.partial(post_kernel, n, unit), grid_spec=pltpu.P...  16.4 us
    ppermute x6, waiting for transfers between devices, along_z(): return lax.ppermute(v, 'z', pairs)  16.1 us
    all_to_all x4, starting transfers between devices, exchange(): return lax.all_to_all(v, 'dp', split_axis=0, concat_axis=0, tiled=True)  15.9 us
    pallas_call x2, Pallas kernels, weight_grads(): pl.pallas_call(weight_kernel, grid_spec=pltpu.PrefetchScalarGridSpec(num_...  15.4 us
  transfers between devices with their start and end apart: 36, of which 9 were waited for; matrix products, arithmetic and copies ran while one was open for 0% of the time, Pallas kernels for 56%

commit v1 on v0

--- a/solution.py
+++ b/solution.py
@@ -18,7 +18,7 @@
 bf16 = jnp.bfloat16
 f32 = jnp.float32
 VMEM_BYTES = 22 << 20
-COST = {"early": 1e11, "late": 1.3e9, "none": 0.0, "tail": 1e11}
+COST = {"early": 1e11, "late": 1.2e9, "none": 0.0, "tail": 1e11}
 PHASE = ["early"]
 
 
@@ -290,7 +290,8 @@
     )(far(tokens), gain, shift, far(w_qkv))
 
 
-def prelude_kernel(n_slots, seg_ref, slot_ref, meta_ref, info_ref, seg_col_ref, seg_row_ref, valid_ref):
+def prelude_kernel(n_slots, place_ref, seg_ref, slot_ref, meta_ref, info_ref, seg_col_ref, seg_row_ref,
+                   valid_ref, voice_ref):
     seg = seg_ref[...]
     slot = slot_ref[...]
     per, lanes = seg.shape
@@ -317,6 +318,10 @@
     info_ref[0] = jnp.max(second)
     info_ref[1] = jnp.sum(first)
     info_ref[2] = jnp.sum(second)
+    lane = lax.broadcasted_iota(jnp.int32, voice_ref.shape, 1)
+    voice = jnp.where(lane == place_ref[3], jnp.max(second).astype(f32), 0.0)
+    voice = jnp.where(lane == 128, jnp.sum(first).astype(f32), voice)
+    voice_ref[...] = jnp.where(lane == 129, jnp.sum(second).astype(f32), voice)
     seg = seg.astype(f32)
     valid = (slot < n_slots).astype(f32)
     for i in range(per):
@@ -326,24 +331,25 @@
         valid_ref[at, :] = jnp.broadcast_to(valid[i:i + 1], (lanes, lanes)).T
 
 
-def prelude(seg_start, dispatch_slot, n_slots):
+def prelude(place, seg_start, dispatch_slot, n_slots):
     t = seg_start.shape[0]
     smem = pl.BlockSpec(memory_space=pltpu.SMEM)
     vmem = pl.BlockSpec(memory_space=pltpu.VMEM)
     return pl.pallas_call(
         functools.partial(prelude_kernel, n_slots),
-        in_specs=[vmem, vmem],
-        out_specs=[smem, smem, vmem, vmem, vmem],
+        in_specs=[smem, vmem, vmem],
+        out_specs=[smem, smem, vmem, vmem, vmem, vmem],
         out_shape=(
             jax.ShapeDtypeStruct((3, LEN // QBLOCK), jnp.int32),
             jax.ShapeDtypeStruct((3,), jnp.int32),
             jax.ShapeDtypeStruct((t, PAIR), f32),
             jax.ShapeDtypeStruct((1, t), f32),
             jax.ShapeDtypeStruct((t, PAIR), f32),
+            jax.ShapeDtypeStruct((1, 2 * PAIR), f32),
         ),
         cost_estimate=work(2.0),
         name="prelude",
-    )(seg_start.reshape(t // PAIR, PAIR), dispatch_slot.reshape(t // PAIR, PAIR))
+    )(place, seg_start.reshape(t // PAIR, PAIR), dispatch_slot.reshape(t // PAIR, PAIR))
 
 
 def proj_kernel(x_ref, mixed_ref, cot_ref, valid_ref, w_ref, gain_ref, shift_ref,
@@ -676,7 +682,7 @@
     blocks, (gin_ref, gout_ref, counts_ref, hold_ref) = refs[:-4], refs[-4:]
     spots = [(ref, k) for ref in blocks for k in range(ref.shape[1])]
     d = gin_ref.shape[1]
-    lane = lax.broadcasted_iota(jnp.int32, (1, d), 1)
+    lane = lax.broadcasted_iota(jnp.int32, tally_ref.shape, 1)
     counts = [jnp.sum(jnp.where(lane == 128 + e, tally_ref[...], 0.0)) for e in range(2)]
     for e in range(2):
         counts_ref[e] = counts[e].astype(jnp.int32)
@@ -909,10 +915,7 @@
     def merge(a, b):
         return small(add_f32, a, b, name="merge").reshape(4, -1, a.shape[1])
 
-    meta, info, seg_col, seg_row, valid = prelude(seg_start, dispatch_slot, n_slots)
-    lane = lax.broadcasted_iota(jnp.int32, (1, d), 1)
-    voice = jnp.where(lane == place[3], info[0], 0)
-    voice = jnp.where(lane == 128, info[1], jnp.where(lane == 129, info[2], voice)).astype(f32)
+    meta, info, seg_col, seg_row, valid, voice = prelude(place, seg_start, dispatch_slot, n_slots)
     away = swap_core(voice)
     h1_t, qkv = line(ln_qkv, tokens, ln1_gain, ln1_shift, w_qkv)
     voice = line(add, voice, away)
@@ -927,7 +930,6 @@
     )
     tally = line(add, voice, away)
     voice = tally[0, :8].astype(jnp.int32)
-    away_t = along_z(tally, NEAR)
 
     def expert(p, axis):
         return line(
@@ -939,10 +941,7 @@
 
     hid_b, dpre_b, *out_b = expert(1, X)
     got_b = plane(out_b, X)
-    tally = line(add, tally, away_t)
-    away_t = along_z(tally, FAR)
     hid_a, dpre_a, out_a = expert(0, None)
-    tally = line(add, tally, away_t)
     own_a = lax.psum_scatter(out_a, ("z", "core"), scatter_dimension=0, tiled=True)
     hid_c, dpre_c, *out_c = expert(2, Y)
     got_c = plane(out_c, Y)
@@ -994,30 +993,33 @@
     def copies(*v):
         return small(lambda *x: jnp.stack([jnp.stack(x)] * 4), *v, name="copies")
 
-    half_a = line(add, keep_a, away_a)
-    all_ab = exchange(line(copies, half_a, half_b))
+    away_t = along_z(tie(tally, mine_2), NEAR)
     grad_tokens, gvec1 = line(
         lambda v: input_grad((d_qkv_1, d_qkv_2), v, d_resid, w_qkv, ln1_gain), tokens
     )
-    all_2 = exchange(line(lambda a, b: merge_small(a, b, gvec1, gvec2), tie(mine_2, all_ab), away_2))
+    all_2 = exchange(line(lambda a, b: merge_small(a, b, gvec1, gvec2), mine_2, away_2))
     piece_1 = line(add, piece_1, away_1)
     away_1 = along_z(piece_1, FAR)
+    tally = line(add, tally, away_t)
+    away_t = along_z(tally, FAR)
+    half_a = line(add, keep_a, away_a)
     result_out = line(lambda v: result_of(info, (hid_a, hid_b, hid_c), w_out, v, UNIT), resid)
     piece_2 = line(total, all_2)
     away_2 = along_z(piece_2, NEAR)
-    all_c = exchange(line(copies, half_c))
     PHASE[0] = "tail"
+    all_e = exchange(line(copies, half_a, half_b, half_c))
     piece_2 = line(add, piece_2, away_2)
     away_2 = along_z(piece_2, FAR)
     piece_1 = line(add, piece_1, away_1)
     around_1 = around(piece_1)
     piece_2 = line(add, piece_2, away_2)
     around_2 = around(piece_2)
-    grad_w_in, grad_w_out, all_counts = line(
-        lambda v: finish_experts((Y, X, Y), place, tie(tally, piece_2), (all_ab, v)), all_c
-    )
     whole_1 = line(stack, *around_1)
     other_1 = swap_core(whole_1)
+    tally = line(add, tally, away_t)
+    grad_w_in, grad_w_out, all_counts = line(
+        lambda v: finish_experts((Y, X, Y), place, tie(tally, piece_2), (v,)), all_e
+    )
     whole_2 = line(stack, *around_2)
     other_2 = swap_core(whole_2)
     grad_wqkv, grad_wo, vectors = join_weights(
@@ -1037,7 +1039,9 @@
     n_slots = n_expert * (2 * tok_count // n_expert)
     everywhere = ("dp", "expert")
     first_half = jnp.zeros((1,), jnp.int32)
-    meta, info, seg_col, seg_row, valid = prelude(seg_start, dispatch_slot, n_slots)
+    meta, info, seg_col, seg_row, valid, _ = prelude(
+        jnp.zeros((4,), jnp.int32), seg_start, dispatch_slot, n_slots
+    )
     h1_t, qkv = ln_qkv(tokens, ln1_gain, ln1_shift, w_qkv)
     mixed, mixed_t, lse = attn_fwd(qkv, meta, seg_col, seg_row, QBLOCK, WIN)
     resid, h2, cotm = proj_ln(tokens, mixed, cotangent, valid, w_attn_out, ln2_gain, ln2_shift)

time: 304 us -> 300 us (0.987)
  local copies, waits for them, and re-layouts: 7.94 us -> 3.77 us
  starting transfers between devices: 47 us -> 50.4 us
  waiting for transfers between devices: 48.5 us -> 45.1 us
    ppermute x14, waiting for transfers between devices: 19.8 us -> 31.9 us  [swap(): return lax.ppermute(v, 'dp', [(i, i ^ axis) for i in range(4)])]
    all_to_all x4 -> x3, waiting for transfers between devices: 10.2 us -> 0.01 us  [exchange(): return lax.all_to_all(v, 'dp', split_axis=0, concat_axis=0, tiled=True)]
    ppermute x6, waiting for transfers between devices: 16.1 us -> 10.3 us  [along_z(): return lax.ppermute(v, 'z', pairs)]
    ppermute x6, starting transfers between devices: 5.94 us -> 9.99 us  [along_z(): return lax.ppermute(v, 'z', pairs)]
    all_to_all x4 -> x3, starting transfers between devices: 15.9 us -> 12.4 us  [exchange(): return lax.all_to_all(v, 'dp', split_axis=0, concat_axis=0, tiled=True)]
    pallas_call x19 -> x18, Pallas kernels: 21.6 us -> 20.5 us  [small(): pl.pallas_call(functools.partial(small_kernel, fn), in_specs=[resident()]...]
  transfers between devices with their start and end apart: 36 -> 35, of which waited for: 9 -> 8; matrix products, arithmetic and copies ran while one was open for 0% -> 0% of each run, Pallas kernels for 56% -> 54%
where the time goes in v1:
time: 300 us; the launch traced here: 297 us
  Pallas kernels  183 us (61%)
  starting transfers between devices  50.4 us (17%)
  waiting for transfers between devices  45.1 us (15%)
  between operations  14.2 us (5%)
  local copies, waits for them, and re-layouts  3.77 us (1%)
    pallas_call x3, Pallas kernels, expert_part(): pl.pallas_call(functools.partial(expert_kernel, axis), grid_spec=pltpu.Pr...  33 us
    ppermute x14, waiting for transfers between devices, swap(): return lax.ppermute(v, 'dp', [(i, i ^ axis) for i in range(4)])  31.9 us
    pallas_call x2, Pallas kernels, attn_bwd(): pl.pallas_call(functools.partial(bwd_kernel, qb, win), out_shape=pltpu.VM...  23.5 us
    pallas_call x18, Pallas kernels, small(): pl.pallas_call(functools.partial(small_kernel, fn), in_specs=[resident()]...  20.5 us
    pallas_call x1, Pallas kernels, post_ffn(): pl.pallas_call(functools.partial(post_kernel, n, unit), grid_spec=pltpu.P...  16.4 us
    pallas_call x2, Pallas kernels, weight_grads(): pl.pallas_call(weight_kernel, grid_spec=pltpu.PrefetchScalarGridSpec(num_...  15.5 us
    pallas_call x1, Pallas kernels, attn_fwd(): pl.pallas_call(functools.partial(fwd_kernel, qb, win), out_shape=(pltpu.V...  13.8 us
    ppermute x7, starting transfers between devices, swap_core(): return lax.ppermute(v, 'core', [(0, 1), (1, 0)])  12.8 us
  transfers between devices with their start and end apart: 35, of which 8 were waited for; matrix products, arithmetic and copies ran while one was open for 0% of the time, Pallas kernels for 54%

profile of v1, /device:TPU:9, one launch (start us, length us, event | category | flops | bytes accessed | tf_op | source)
XLA Modules:
  0.0 297.5 jit_solution(1974772320373333078)
XLA Ops:
  7.8 2.9 prelude.1
  10.7 0.7 collective-permute-start
  11.5 8.4 %ln_qkv.1 = (bf16[768,1024]{1,0:T(8,128)(2,1)}, bf16[1024,2304]{1,0:T(8,128)(2,1)}) custom-call(bf16[1024,768]{1,0:T(8,128)(2,1)} %refs_2_, f32[768]{0:T(1024)S(1)} %copy-done.9, f32[768]{0:T(1024)S(1)} %copy-done.5, bf16[768,2304]{1,0:T(8,128)(2,1)} %refs_4_.1), custom_call_target="tpu_custom_call" | custom-call | flops 799999983616 | bytes 1048576 | tf_op jit(solution)/shard_map/ln_qkv/pallas_call | solution.py:278
  19.9 1.2 add.35.refs_0_
  21.2 1.2 collective-permute-start.1
  22.4 13.8 %attn_fwd.1 = (bf16[1024,768]{1,0:T(8,128)(2,1)S(1)}, bf16[768,1024]{1,0:T(8,128)(2,1)}, f32[6,2,1024]{2,1,0:T(2,128)S(1)}) custom-call(s32[3,4]{1,0:T(4,128)S(1)} %copy-done.29, bf16[1024,2304]{1,0:T(8,128)(2,1)} %get-tuple-element.109.q_ref.k_ref.v_ref, bf16[1024,2304]{1,0:T(8,128)(2,1)} %get-tuple-element.109.q_ref.k_ref.v_ref, ...), custom_call_target="tpu_custom_call" | custom-call | flops 1399999954944 | bytes 1048576 | tf_op jit(solution)/shard_map/attn_fwd/pallas_call | solution.py:124
  36.2 1.3 add.36.refs_0_
  37.5 1.2 collective-permute-start.2
  38.7 5.8 %proj_ln.1 = (f32[1024,768]{1,0:T(8,128)}, bf16[1024,768]{1,0:T(8,128)(2,1)S(1)}, bf16[1024,768]{1,0:T(8,128)(2,1)S(1)}) custom-call(bf16[1024,768]{1,0:T(8,128)(2,1)} %refs_2_, bf16[1024,768]{1,0:T(8,128)(2,1)S(1)} %get-tuple-element.114.mixed_ref, bf16[1024,768]{1,0:T(8,128)(2,1)} %refs_5_.2, f32[1024,128]{1,0:T(8,128)S(1)} %copy-done.24, ...), custom_call_target="tpu_custom_call" | custom-call | flops 699999977472 | bytes 1048576 | tf_op jit(solution)/shard_map/proj_ln/pallas_call | solution.py:368
  44.5 0.7 add.37.refs_0_
  45.3 10.9 %expert_part.3 = (bf16[1024,1024]{1,0:T(8,128)(2,1)}, bf16[1024,1024]{1,0:T(8,128)(2,1)}, bf16[4,2,64,768]{3,2,1,0:T(8,128)(2,1)}, bf16[4,2,64,768]{3,2,1,0:T(8,...) custom-call(s32[3]{0:T(128)S(1)} %copy-done.20, s32[4]{0:T(128)S(1)} %copy-done, ...), custom_call_target="tpu_custom_call" | custom-call | flops 1100000002048 | bytes 1048576 | tf_op jit(solution)/shard_map/expert_part/pallas_call | solution.py:454
  56.1 0.6 collective-permute-start.3
  57.0 1.4 collective-permute-start.5
  58.5 11.2 %expert_part.4 = (bf16[1024,1024]{1,0:T(8,128)(2,1)}, bf16[1024,1024]{1,0:T(8,128)(2,1)}, bf16[8,4,2,2,32,768]{5,4,3,2,1,0:T(8,128)(2,1)}) custom-call(s32[3]{0:T(128)S(1)} %copy-done.20, s32[4]{0:T(128)S(1)} %copy-done, bf16[1024,768]{1,0:T(8,128)(2,1)S(1)} %get-tuple-element.124.h2_ref, bf16[1024,768]{1,0:T(8,128)(2,1)S(1)} %get-tuple-element.120.cot_ref, ...), custom_call_target="tpu_custom_call" | custom-call | flops 1100000002048 | bytes 1048576 | tf_op jit(solution)/shard_map/expert_part/pallas_call | solution.py:454
  70.0 10.9 %expert_part.5 = (bf16[1024,1024]{1,0:T(8,128)(2,1)}, bf16[1024,1024]{1,0:T(8,128)(2,1)}, bf16[4,2,64,768]{3,2,1,0:T(8,128)(2,1)}, bf16[4,2,64,768]{3,2,1,0:T(8,...) custom-call(s32[3]{0:T(128)S(1)} %copy-done.20, s32[4]{0:T(128)S(1)} %copy-done, ...), custom_call_target="tpu_custom_call" | custom-call | flops 1100000002048 | bytes 1048576 | tf_op jit(solution)/shard_map/expert_part/pallas_call | solution.py:454
  81.3 16.4 %post_ffn.1 = (f32[1024,768]{1,0:T(8,128)}, bf16[1024,768]{1,0:T(8,128)(2,1)}, bf16[1024,768]{1,0:T(8,128)(2,1)}, f32[2,768]{1,0:T(2,128)S(1)}) custom-call(s32[3]{0:T(128)S(1)} %copy-done.20, bf16[1024,1024]{1,0:T(8,128)(2,1)} %get-tuple-element.131.refs_0_, bf16[1024,1024]{1,0:T(8,128)(2,1)} %get-tuple-element.133.refs_1_, ...), custom_call_target="tpu_custom_call" | custom-call | flops 999999995904 | bytes 1048576 | tf_op jit(solution)/shard_map/post_ffn/pallas_call | solution.py:506
  97.7 1.8 collective-permute-start.8
  99.5 4.5 %sum_sides.2 = (bf16[4,2,2,32,768]{4,3,2,1,0:T(8,128)(2,1)S(1)}, bf16[4,2,2,32,768]{4,3,2,1,0:T(8,128)(2,1)}) custom-call(s32[4]{0:T(128)S(1)} %copy-done, s32[8]{0:T(128)S(1)} %fusion.voice_ref, bf16[4,2,64,768]{3,2,1,0:T(8,128)(2,1)S(1)} %copy-done.26, bf16[4,2,64,768]{3,2,1,0:T(8,128)(2,1)} %collective-permute-done.3.b_ref, ...), custom_call_target="tpu_custom_call" | custom-call | flops 299999985664 | bytes 1048576 | tf_op jit(solution)/shard_map/sum_sides/pallas_call | solution.py:666
  104.3 11.8 %attn_bwd.2.refs_1_.refs_0_ = bf16[3,1024,384]{2,1,0:T(8,128)(2,1)S(1)} custom-call(s32[3,4]{1,0:T(4,128)S(1)} %copy-done.30, bf16[1024,2304]{1,0:T(8,128)(2,1)} %get-tuple-element.109.q_ref.k_ref.v_ref, bf16[1024,2304]{1,0:T(8,128)(2,1)} %get-tuple-element.109.q_ref.k_ref.v_ref, bf16[1024,2304]{1,0:T(8,128)(2,1)} %get-tuple-element.109.q_ref.k_ref.v_ref, ...), custom_call_target="tpu_custom_call" | custom-call | flops 1110000009216 | bytes 1048576 | tf_op jit(solution)/shard_map/attn_bwd/pallas_call | solution.py:218
  116.1 9.5 %weight_grads.2 = (bf16[384,1920]{1,0:T(8,128)(2,1)}, bf16[384,1920]{1,0:T(8,128)(2,1)}) custom-call(s32[4]{0:T(128)S(1)} %copy-done, bf16[768,1024]{1,0:T(8,128)(2,1)} %get-tuple-element.158.refs_0_, bf16[3,1024,384]{2,1,0:T(8,128)(2,1)S(1)} %attn_bwd.2.refs_1_.refs_0_, bf16[768,1024]{1,0:T(8,128)(2,1)} %get-tuple-element.144.ot_ref.refs_2_, ...), custom_call_target="tpu_custom_call" | custom-call | flops 599999971328 | bytes 1048576 | tf_op jit(solution)/shard_map/weight_grads/pallas_call | solution.py:589
  125.7 4.5 %sum_sides.3 = (bf16[4,2,2,32,768]{4,3,2,1,0:T(8,128)(2,1)S(1)}, bf16[4,2,2,32,768]{4,3,2,1,0:T(8,128)(2,1)}) custom-call(s32[4]{0:T(128)S(1)} %copy-done, s32[8]{0:T(128)S(1)} %copy-done.15, bf16[4,2,64,768]{3,2,1,0:T(8,128)(2,1)S(1)} %copy-done.25, bf16[4,2,64,768]{3,2,1,0:T(8,128)(2,1)} %collective-permute-done.6.b_ref, ...), custom_call_target="tpu_custom_call" | custom-call | flops 299999985664 | bytes 1048576 | tf_op jit(solution)/shard_map/sum_sides/pallas_call | solution.py:666
  130.5 4.3 %collective-permute-done.9.refs_1_ = bf16[4,2,2,32,768]{4,3,2,1,0:T(8,128)(2,1)} collective-permute-done((bf16[4,2,2,32,768]{4,3,2,1,0:T(8,128)(2,1)}, bf16[4,2,2,32,768]{4,3,2,1,0:T(8,128)(2,1)}, u32[]{:S(2)}, u32[]{:S(2)}) %collective-permute-start.9) | collective-permute-done | bytes 786464 | tf_op jit(solution)/shard_map/ppermute | solution.py:785
  134.9 2.2 add.38
  137.3 1.1 copy-done.2
  138.4 1.3 split.2
  139.8 2.8 merge.1
  142.6 4.3 %all-to-all-start = ((bf16[4,96,1920]{2,1,0:T(8,128)(2,1)}), bf16[4,96,1920]{2,1,0:T(8,128)(2,1)}, u32[]{:S(2)}, u32[]{:S(2)}) async-start(bf16[4,96,1920]{2,1,0:T(8,128)(2,1)} %bitcast.9), calls=%async_computation.1 | async-start | bytes 2949120 | tf_op jit(solution)/shard_map/all_to_all | solution.py:913
  147.2 1.3 collective-permute-start.12
  148.5 11.8 %attn_bwd.3.refs_1_ = bf16[3,1024,384]{2,1,0:T(8,128)(2,1)S(1)} custom-call(s32[3,4]{1,0:T(4,128)S(1)} %copy-done.30, bf16[1024,2304]{1,0:T(8,128)(2,1)} %get-tuple-element.109.q_ref.k_ref.v_ref, bf16[1024,2304]{1,0:T(8,128)(2,1)} %get-tuple-element.109.q_ref.k_ref.v_ref, bf16[1024,2304]{1,0:T(8,128)(2,1)} %get-tuple-element.109.q_ref.k_ref.v_ref, ...), custom_call_target="tpu_custom_call" | custom-call | flops 1110000009216 | bytes 1048576 | tf_op jit(solution)/shard_map/attn_bwd/pallas_call | solution.py:218
  160.3 6.0 %weight_grads.3 = (bf16[384,1152]{1,0:T(8,128)(2,1)}, bf16[384,1152]{1,0:T(8,128)(2,1)}) custom-call(s32[4]{0:T(128)S(1)} %copy-done, bf16[768,1024]{1,0:T(8,128)(2,1)} %get-tuple-element.158.refs_0_, bf16[3,1024,384]{2,1,0:T(8,128)(2,1)S(1)} %attn_bwd.3.refs_1_), custom_call_target="tpu_custom_call" | custom-call | flops 359999995904 | bytes 1048576 | tf_op jit(solution)/shard_map/weight_grads/pallas_call | solution.py:589
  166.3 0.7 collective-permute-start.13
  167.0 2.2 add.39
  169.2 2.1 collective-permute-start.15
  171.3 2.1 collective-permute-done.12.refs_1_
  173.4 1.1 split.3
  174.5 1.3 collective-permute-start.16
  175.7 1.6 total.2.refs_0_
  177.4 9.9 %input_grad.1 = (f32[1024,768]{1,0:T(8,128)}, f32[2,768]{1,0:T(2,128)S(1)}) custom-call(bf16[3,1024,384]{2,1,0:T(8,128)(2,1)} %copy-done.17, bf16[3,1024,384]{2,1,0:T(8,128)(2,1)} %copy-done.18, bf16[1024,768]{1,0:T(8,128)(2,1)} %refs_2_, f32[1024,768]{1,0:T(8,128)} %get-tuple-element.135.refs_3_, bf16[768,2304]{1,0:T(8,128)(2,1)} %refs_4_.1, f32[768]{0:T(1024)S(1)} %copy-done.10), custom_call_target="tpu_custom_call" | custom-call | flops 12000000000 | bytes 1048576 | tf_op jit(solution)/shard_map/input_grad/pallas_call | solution.py:627
  187.4 1.2 merge_small.1
  188.6 3.5 %all-to-all-start.1 = ((bf16[4,112,1152]{2,1,0:T(8,128)(2,1)}), bf16[4,112,1152]{2,1,0:T(8,128)(2,1)S(1)}, u32[]{:S(2)}, u32[]{:S(2)}) async-start(bf16[4,112,1152]{2,1,0:T(8,128)(2,1)} %merge_small.1), calls=%async_computation.2 | async-start | bytes 2064384 | tf_op jit(solution)/shard_map/all_to_all | solution.py:913
  192.1 2.1 collective-permute-done.14.refs_1_
  194.2 0.8 add.40.refs_0_
  195.6 2.1 collective-permute-start.23
  197.8 10.6 %result_of.1 = bf16[1024,768]{1,0:T(8,128)(2,1)} custom-call(s32[3]{0:T(128)S(1)} %copy-done.21, bf16[1024,1024]{1,0:T(8,128)(2,1)} %get-tuple-element.123.refs_0_, bf16[1024,1024]{1,0:T(8,128)(2,1)} %get-tuple-element.121.refs_1_, bf16[1024,1024]{1,0:T(8,128)(2,1)} %get-tuple-element.125.refs_2_, bf16[2,3072,768]{2,1,0:T(8,128)(2,1)} %refs_3_.3, ...), custom_call_target="tpu_custom_call" | custom-call | flops 9600000000 | bytes 1048576 | tf_op jit(solution)/shard_map/result_of/pallas_call | solution.py:539
  208.5 3.8 %collective-permute-start.17 = (bf16[112,1152]{1,0:T(8,128)(2,1)S(1)}, bf16[112,1152]{1,0:T(8,128)(2,1)S(1)}, u32[]{:S(2)}, u32[]{:S(2)}) collective-permute-start(bf16[112,1152]{1,0:T(8,128)(2,1)S(1)} %total.3.refs_0_), channel_id=1, source_target_pairs={{0,2},{2,0},{4,6},{6,4},{1,3},{3,1},{5,7},{7,5},{8,10},{10,8},{12,... | collective-permute-start | bytes 774152 | tf_op jit(solution)/shard_map/ppermute | solution.py:793
  212.3 0.9 copy-done.3
  213.2 0.9 copy-done.4
  214.1 1.6 copies.1
  215.7 4.5 %all-to-all-start.2 = ((bf16[4,3,2,2,32,768]{5,4,3,2,1,0:T(8,128)(2,1)}), bf16[4,3,2,2,32,768]{5,4,3,2,1,0:T(8,128)(2,1)}, u32[]{:S(2)}, u32[]{:S(2)}) async-start(bf16[4,3,2,2,32,768]{5,4,3,2,1,0:T(8,128)(2,1)} %copies.1), calls=%async_computation.5 | async-start | bytes 4718592 | tf_op jit(solution)/shard_map/all_to_all | solution.py:913
  220.3 2.0 collective-permute-start.19
  222.3 1.2 add.44.refs_0_
  223.5 2.4 collective-permute-start.22
  226.2 8.2 %collective-permute-done.19.refs_1_ = bf16[112,1152]{1,0:T(8,128)(2,1)S(1)} collective-permute-done((bf16[112,1152]{1,0:T(8,128)(2,1)S(1)}, bf16[112,1152]{1,0:T(8,128)(2,1)S(1)}, u32[]{:S(2)}, u32[]{:S(2)}) %collective-permute-start.19) | collective-permute-done | bytes 258080 | tf_op jit(solution)/shard_map/ppermute | solution.py:793
  234.4 0.8 add.45.refs_0_
  235.1 2.3 collective-permute-start.26
  237.4 17.7 %collective-permute-done.22.refs_3_ = bf16[96,1920]{1,0:T(8,128)(2,1)S(1)} collective-permute-done((bf16[96,1920]{1,0:T(8,128)(2,1)S(1)}, bf16[96,1920]{1,0:T(8,128)(2,1)S(1)}, u32[]{:S(2)}, u32[]{:S(2)}) %collective-permute-start.22) | collective-permute-done | bytes 368672 | tf_op jit(solution)/shard_map/ppermute | solution.py:785
  255.4 7.8 %collective-permute-done.21.refs_2_ = bf16[96,1920]{1,0:T(8,128)(2,1)S(1)} collective-permute-done((bf16[96,1920]{1,0:T(8,128)(2,1)S(1)}, bf16[96,1920]{1,0:T(8,128)(2,1)S(1)}, u32[]{:S(2)}, u32[]{:S(2)}) %collective-permute-start.21) | collective-permute-done | bytes 368672 | tf_op jit(solution)/shard_map/ppermute | solution.py:785
  263.2 1.2 stack.22.refs_0_
  264.5 10.5 %collective-permute-start.27 = (bf16[4,96,1920]{2,1,0:T(8,128)(2,1)}, bf16[4,96,1920]{2,1,0:T(8,128)(2,1)}, u32[]{:S(2)}, u32[]{:S(2)}) collective-permute-start(bf16[4,96,1920]{2,1,0:T(8,128)(2,1)} %stack.22.refs_0_), channel_id=1, source_target_pairs={{0,1},{1,0},{2,3},{3,2},{4,5},{5,4},{6,7},{7,6},{8,9},{9,8},{10,11... | collective-permute-start | bytes 4423688 | tf_op jit(solution)/shard_map/ppermute | solution.py:781
  274.9 0.7 add.46.tally_ref
  275.6 4.3 %finish_experts.1 = (f32[2,768,384]{2,1,0:T(8,128)}, f32[2,384,768]{2,1,0:T(8,128)}, s32[2]{0:T(128)}) custom-call(s32[4]{0:T(128)S(1)} %copy-done.1, f32[1,256]{1,0:T(1,128)S(1)} %add.46.tally_ref, bf16[4,3,2,2,32,768]{5,4,3,2,1,0:T(8,128)(2,1)} %all-to-all-done.2.refs_0_), custom_call_target="tpu_custom_call" | custom-call | flops 399999991808 | bytes 1048576 | tf_op jit(solution)/shard_map/finish_experts/pallas_call | solution.py:710
  280.0 1.4 stack.23.refs_2_
  281.5 2.6 collective-permute-done.28.refs_3_
  284.1 6.2 %join_weights.1 = (f32[2,384,2304]{2,1,0:T(8,128)}, f32[2,384,768]{2,1,0:T(8,128)}, f32[8,768]{1,0:T(8,128)S(1)}) custom-call(s32[4]{0:T(128)S(1)} %copy-done.1, bf16[4,96,1920]{2,1,0:T(8,128)(2,1)} %stack.22.refs_0_, bf16[4,96,1920]{2,1,0:T(8,128)(2,1)} %collective-permute-done.27.refs_1_, bf16[4,112,1152]{2,1,0:T(8,128)(2,1)S(1)} %stack.23.refs_2_, ...), custom_call_target="tpu_custom_call" | custom-call | flops 499999997952 | bytes 1048576 | tf_op jit(solution)/shard_map/join_weights/pallas_call | solution.py:751
  (113 shorter events, 5.2 us)
Async XLA Ops:
  7.2 130.1 %reduce-scatter.4.cloned.1.call-start = ((), (), s32[]{:S(2)}) async-start(), calls=%async_computation.6 | async-start | bytes 7077888 | tf_op jit(solution)/shard_map/reduce_scatter | solution.py:945
  7.8 3.6 %copy-start.5 = (f32[768]{0:T(1024)S(1)}, f32[768]{0:T(1024)}, u32[]{:S(2)}) copy-start(f32[768]{0:T(1024)} %shift_ref.2) | copy-start | bytes 9220
  7.8 3.6 %copy-start.9 = (f32[768]{0:T(1024)S(1)}, f32[768]{0:T(1024)}, u32[]{:S(2)}) copy-start(f32[768]{0:T(1024)} %refs_5_.3) | copy-start | bytes 9220
  10.7 9.2 %collective-permute-start = (f32[1,256]{1,0:T(1,128)}, f32[1,256]{1,0:T(1,128)}, u32[]{:S(2)}, u32[]{:S(2)}) collective-permute-start(f32[1,256]{1,0:T(1,128)} %get-tuple-element.108.refs_0_), channel_id=1, source_target_pairs={{0,1},{1,0},{2,3},{3,2},{4,5},{5,4},{6,7},{7,6},{8,9},{9,8},{10,11... | collective-permute-start | bytes 3080 | tf_op jit(solution)/shard_map/ppermute | solution.py:781
  11.5 8.5 %copy-start.13 = (f32[1,256]{1,0:T(1,128)S(1)}, f32[1,256]{1,0:T(1,128)}, u32[]{:S(2)}) copy-start(f32[1,256]{1,0:T(1,128)} %get-tuple-element.108.refs_0_) | copy-start | bytes 3076
  19.9 2.5 copy-start.22
  19.9 2.5 copy-start.27
  19.9 2.5 copy-start.29
  21.2 15.0 %collective-permute-start.1 = (f32[1,256]{1,0:T(1,128)}, f32[1,256]{1,0:T(1,128)}, u32[]{:S(2)}, u32[]{:S(2)}) collective-permute-start(f32[1,256]{1,0:T(1,128)} %add.35.refs_0_), channel_id=1, source_target_pairs={{0,8},{8,0},{16,24},{24,16},{1,9},{9,1},{17,25},{25,17},{2,10},{10... | collective-permute-start | bytes 3080 | tf_op jit(solution)/shard_map/ppermute | solution.py:785
  36.2 2.5 copy-start.6
  36.2 2.5 copy-start.7
  36.2 2.5 copy-start.24
  37.5 7.0 %collective-permute-start.2 = (f32[1,256]{1,0:T(1,128)}, f32[1,256]{1,0:T(1,128)}, u32[]{:S(2)}, u32[]{:S(2)}) collective-permute-start(f32[1,256]{1,0:T(1,128)} %add.36.refs_0_), channel_id=1, source_target_pairs={{0,16},{8,24},{16,0},{24,8},{1,17},{9,25},{17,1},{25,9},{2,18},{10... | collective-permute-start | bytes 3080 | tf_op jit(solution)/shard_map/ppermute | solution.py:785
  45.2 52.4 %copy-start.11 = (f32[1,256]{1,0:T(1,128)}, f32[1,256]{1,0:T(1,128)S(1)}, u32[]{:S(2)}) copy-start(f32[1,256]{1,0:T(1,128)S(1)} %add.37.refs_0_) | copy-start | bytes 3076
  56.1 43.4 %collective-permute-start.3 = (bf16[4,2,64,768]{3,2,1,0:T(8,128)(2,1)}, bf16[4,2,64,768]{3,2,1,0:T(8,128)(2,1)}, u32[]{:S(2)}, u32[]{:S(2)}) collective-permute-start(bf16[4,2,64,768]{3,2,1,0:T(8,128)(2,1)} %get-tuple-element.128), channel_id=1, source_target_pairs={{0,1},{1,0},{2,3},{3,2},{4,5},{5,4},{6,7},{7,6},{8,9},{9,8},{10,11... | collective-permute-start | bytes 2359304 | tf_op jit(solution)/shard_map/ppermute | solution.py:781
  56.8 42.7 %collective-permute-start.4 = (bf16[4,2,64,768]{3,2,1,0:T(8,128)(2,1)}, bf16[4,2,64,768]{3,2,1,0:T(8,128)(2,1)}, u32[]{:S(2)}, u32[]{:S(2)}) collective-permute-start(bf16[4,2,64,768]{3,2,1,0:T(8,128)(2,1)} %get-tuple-element.129), channel_id=1, source_target_pairs={{0,8},{8,0},{16,24},{24,16},{1,9},{9,1},{17,25},{25,17},{2,10},{10... | collective-permute-start | bytes 2359304 | tf_op jit(solution)/shard_map/ppermute | solution.py:785
  57.0 40.6 %collective-permute-start.5 = (bf16[4,2,64,768]{3,2,1,0:T(8,128)(2,1)}, bf16[4,2,64,768]{3,2,1,0:T(8,128)(2,1)}, u32[]{:S(2)}, u32[]{:S(2)}) collective-permute-start(bf16[4,2,64,768]{3,2,1,0:T(8,128)(2,1)} %get-tuple-element.130), channel_id=1, source_target_pairs={{0,9},{1,8},{8,1},{9,0},{16,25},{17,24},{24,17},{25,16},{2,11},{3,... | collective-permute-start | bytes 2359304 | tf_op jit(solution)/shard_map/ppermute | solution.py:789
  69.7 142.6 %reduce-scatter.6.cloned.1.call-start = ((), (), s32[]{:S(2)}) async-start(), calls=%async_computation.7 | async-start | bytes 983040 | tf_op jit(solution)/shard_map/reduce_scatter | solution.py:965
  69.9 11.3 %copy-start.8 = (f32[768]{0:T(1024)S(1)}, f32[768]{0:T(1024)}, u32[]{:S(2)}) copy-start(f32[768]{0:T(1024)} %refs_7_.1) | copy-start | bytes 9220
  80.8 44.8 %collective-permute-start.6 = (bf16[4,2,64,768]{3,2,1,0:T(8,128)(2,1)}, bf16[4,2,64,768]{3,2,1,0:T(8,128)(2,1)}, u32[]{:S(2)}, u32[]{:S(2)}) collective-permute-start(bf16[4,2,64,768]{3,2,1,0:T(8,128)(2,1)} %get-tuple-element.139), channel_id=1, source_target_pairs={{0,1},{1,0},{2,3},{3,2},{4,5},{5,4},{6,7},{7,6},{8,9},{9,8},{10,11... | collective-permute-start | bytes 2359304 | tf_op jit(solution)/shard_map/ppermute | solution.py:781
  81.0 44.6 %collective-permute-start.7 = (bf16[4,2,64,768]{3,2,1,0:T(8,128)(2,1)}, bf16[4,2,64,768]{3,2,1,0:T(8,128)(2,1)}, u32[]{:S(2)}, u32[]{:S(2)}) collective-permute-start(bf16[4,2,64,768]{3,2,1,0:T(8,128)(2,1)} %get-tuple-element.140), channel_id=1, source_target_pairs={{0,16},{8,24},{16,0},{24,8},{1,17},{9,25},{17,1},{25,9},{2,18},{10... | collective-permute-start | bytes 2359304 | tf_op jit(solution)/shard_map/ppermute | solution.py:785
  81.3 18.2 %copy-start.26 = (bf16[4,2,64,768]{3,2,1,0:T(8,128)(2,1)S(1)}, bf16[4,2,64,768]{3,2,1,0:T(8,128)(2,1)}, u32[]{:S(2)}) copy-start(bf16[4,2,64,768]{3,2,1,0:T(8,128)(2,1)} %get-tuple-element.127.a_ref) | copy-start | bytes 2359300
  97.7 6.3 %copy-start.14 = (s32[8]{0:T(128)}, s32[8]{0:T(128)S(1)}, u32[]{:S(2)}) copy-start(s32[8]{0:T(128)S(1)} %fusion.voice_ref) | copy-start | bytes 100
  97.7 27.9 %collective-permute-start.8 = (bf16[4,2,64,768]{3,2,1,0:T(8,128)(2,1)}, bf16[4,2,64,768]{3,2,1,0:T(8,128)(2,1)}, u32[]{:S(2)}, u32[]{:S(2)}) collective-permute-start(bf16[4,2,64,768]{3,2,1,0:T(8,128)(2,1)} %get-tuple-element.141), channel_id=1, source_target_pairs={{0,17},{1,16},{8,25},{9,24},{16,1},{17,0},{24,9},{25,8},{2,19},{3,... | collective-permute-start | bytes 2359304 | tf_op jit(solution)/shard_map/ppermute | solution.py:789
  99.5 4.8 %copy-start.23 = (f32[1024,128]{1,0:T(8,128)S(1)}, f32[1024,128]{1,0:T(8,128)}, u32[]{:S(2)}) copy-start(f32[1024,128]{1,0:T(8,128)} %get-tuple-element.110.seg_col_ref) | copy-start | bytes 1572868
  99.5 4.8 %copy-start.28 = (f32[1,1024]{1,0:T(1,128)S(1)}, f32[1,1024]{1,0:T(1,128)}, u32[]{:S(2)}) copy-start(f32[1,1024]{1,0:T(1,128)} %get-tuple-element.111.seg_row_ref) | copy-start | bytes 12292
  99.5 4.7 %copy-start.30 = (s32[3,4]{1,0:T(4,128)S(1)}, s32[3,4]{1,0:T(4,128)}, u32[]{:S(2)}) copy-start(s32[3,4]{1,0:T(4,128)} %get-tuple-element.104.lo_ref) | copy-start | bytes 148
  104.0 30.9 %collective-permute-start.9 = (bf16[4,2,2,32,768]{4,3,2,1,0:T(8,128)(2,1)}, bf16[4,2,2,32,768]{4,3,2,1,0:T(8,128)(2,1)}, u32[]{:S(2)}, u32[]{:S(2)}) collective-permute-start(bf16[4,2,2,32,768]{4,3,2,1,0:T(8,128)(2,1)} %get-tuple-element.152), channel_id=1, source_target_pairs={{0,16},{8,24},{16,0},{24,8},{1,17},{9,25},{17,1},{25,9},{2,18},{10... | collective-permute-start | bytes 2359304 | tf_op jit(solution)/shard_map/ppermute | solution.py:785
  116.0 9.5 %copy-start.17 = (bf16[3,1024,384]{2,1,0:T(8,128)(2,1)}, bf16[3,1024,384]{2,1,0:T(8,128)(2,1)S(1)}, u32[]{:S(2)}) copy-start(bf16[3,1024,384]{2,1,0:T(8,128)(2,1)S(1)} %attn_bwd.2.refs_1_.refs_0_) | copy-start | bytes 7077892
  116.1 9.6 %copy-start.15 = (s32[8]{0:T(128)S(1)}, s32[8]{0:T(128)}, u32[]{:S(2)}) copy-start(s32[8]{0:T(128)} %copy-done.14) | copy-start | bytes 100
  116.1 9.6 %copy-start.25 = (bf16[4,2,64,768]{3,2,1,0:T(8,128)(2,1)S(1)}, bf16[4,2,64,768]{3,2,1,0:T(8,128)(2,1)}, u32[]{:S(2)}) copy-start(bf16[4,2,64,768]{3,2,1,0:T(8,128)(2,1)} %get-tuple-element.138.a_ref) | copy-start | bytes 2359300
  125.6 14.2 %collective-permute-start.10 = (bf16[384,1920]{1,0:T(8,128)(2,1)}, bf16[384,1920]{1,0:T(8,128)(2,1)}, u32[]{:S(2)}, u32[]{:S(2)}) collective-permute-start(bf16[384,1920]{1,0:T(8,128)(2,1)} %get-tuple-element.148), channel_id=1, source_target_pairs={{0,1},{1,0},{2,3},{3,2},{4,5},{5,4},{6,7},{7,6},{8,9},{9,8},{10,11... | collective-permute-start | bytes 4423688 | tf_op jit(solution)/shard_map/ppermute | solution.py:781
  130.1 36.9 %collective-permute-start.11 = (bf16[4,2,2,32,768]{4,3,2,1,0:T(8,128)(2,1)}, bf16[4,2,2,32,768]{4,3,2,1,0:T(8,128)(2,1)}, u32[]{:S(2)}, u32[]{:S(2)}) collective-permute-start(bf16[4,2,2,32,768]{4,3,2,1,0:T(8,128)(2,1)} %get-tuple-element.161), channel_id=1, source_target_pairs={{0,8},{8,0},{16,24},{24,16},{1,9},{9,1},{17,25},{25,17},{2,10},{10... | collective-permute-start | bytes 2359304 | tf_op jit(solution)/shard_map/ppermute | solution.py:785
  137.3 1.1 copy-start.2
  138.4 1.4 copy-start.19
  142.6 33.1 %all-to-all-start = ((bf16[4,96,1920]{2,1,0:T(8,128)(2,1)}), bf16[4,96,1920]{2,1,0:T(8,128)(2,1)}, u32[]{:S(2)}, u32[]{:S(2)}) async-start(bf16[4,96,1920]{2,1,0:T(8,128)(2,1)} %bitcast.9), calls=%async_computation.1 | async-start | bytes 2949120 | tf_op jit(solution)/shard_map/all_to_all | solution.py:913
  147.0 65.3 %reduce-scatter.8.cloned.1.call-start = ((), (), s32[]{:S(2)}) async-start(), calls=%async_computation.8 | async-start | bytes 983040 | tf_op jit(solution)/shard_map/reduce_scatter | solution.py:965
  147.2 26.1 %collective-permute-start.12 = (bf16[2,2,2,32,768]{4,3,2,1,0:T(8,128)(2,1)}, bf16[2,2,2,32,768]{4,3,2,1,0:T(8,128)(2,1)}, u32[]{:S(2)}, u32[]{:S(2)}) collective-permute-start(bf16[2,2,2,32,768]{4,3,2,1,0:T(8,128)(2,1)} %get-tuple-element.163), channel_id=1, source_target_pairs={{0,16},{8,24},{16,0},{24,8},{1,17},{9,25},{17,1},{25,9},{2,18},{10... | collective-permute-start | bytes 1179656 | tf_op jit(solution)/shard_map/ppermute | solution.py:785
  160.3 6.0 %copy-start.18 = (bf16[3,1024,384]{2,1,0:T(8,128)(2,1)}, bf16[3,1024,384]{2,1,0:T(8,128)(2,1)S(1)}, u32[]{:S(2)}) copy-start(bf16[3,1024,384]{2,1,0:T(8,128)(2,1)S(1)} %attn_bwd.3.refs_1_) | copy-start | bytes 7077892
  166.3 2.9 copy-start.12
  166.3 21.1 %collective-permute-start.13 = (bf16[384,1152]{1,0:T(8,128)(2,1)}, bf16[384,1152]{1,0:T(8,128)(2,1)S(1)}, u32[]{:S(2)}, u32[]{:S(2)}) collective-permute-start(bf16[384,1152]{1,0:T(8,128)(2,1)} %get-tuple-element.159), channel_id=1, source_target_pairs={{0,1},{1,0},{2,3},{3,2},{4,5},{5,4},{6,7},{7,6},{8,9},{9,8},{10,11... | collective-permute-start | bytes 2654216 | tf_op jit(solution)/shard_map/ppermute | solution.py:781
  169.2 25.8 %collective-permute-start.15 = (f32[1,256]{1,0:T(1,128)S(1)}, f32[1,256]{1,0:T(1,128)S(1)}, u32[]{:S(2)}, u32[]{:S(2)}) collective-permute-start(f32[1,256]{1,0:T(1,128)S(1)} %copy-done.12), channel_id=1, source_target_pairs={{0,2},{2,0},{4,6},{6,4},{1,3},{3,1},{5,7},{7,5},{8,10},{10,8},{12,... | collective-permute-start | bytes 3080 | tf_op jit(solution)/shard_map/ppermute | solution.py:793
  174.5 23.2 %collective-permute-start.16 = (bf16[2,2,32,768]{3,2,1,0:T(8,128)(2,1)S(1)}, bf16[2,2,32,768]{3,2,1,0:T(8,128)(2,1)S(1)}, u32[]{:S(2)}, u32[]{:S(2)}) collective-permute-start(bf16[2,2,32,768]{3,2,1,0:T(8,128)(2,1)S(1)} %get-tuple-element.176), channel_id=1, source_target_pairs={{0,8},{8,0},{16,24},{24,16},{1,9},{9,1},{17,25},{25,17},{2,10},{10... | collective-permute-start | bytes 589832 | tf_op jit(solution)/shard_map/ppermute | solution.py:785
  175.7 1.7 copy-start.10
  177.3 10.0 %copy-start.16 = (bf16[384,1152]{1,0:T(8,128)(2,1)S(1)}, bf16[384,1152]{1,0:T(8,128)(2,1)}, u32[]{:S(2)}) copy-start(bf16[384,1152]{1,0:T(8,128)(2,1)} %get-tuple-element.169.mine_ref) | copy-start | bytes 2654212
  177.3 16.9 %collective-permute-start.14 = (bf16[96,1920]{1,0:T(8,128)(2,1)S(1)}, bf16[96,1920]{1,0:T(8,128)(2,1)S(1)}, u32[]{:S(2)}, u32[]{:S(2)}) collective-permute-start(bf16[96,1920]{1,0:T(8,128)(2,1)S(1)} %total.2.refs_0_), channel_id=1, source_target_pairs={{0,2},{2,0},{4,6},{6,4},{1,3},{3,1},{5,7},{7,5},{8,10},{10,8},{12,... | collective-permute-start | bytes 1105928 | tf_op jit(solution)/shard_map/ppermute | solution.py:793
  188.6 19.8 %all-to-all-start.1 = ((bf16[4,112,1152]{2,1,0:T(8,128)(2,1)}), bf16[4,112,1152]{2,1,0:T(8,128)(2,1)S(1)}, u32[]{:S(2)}, u32[]{:S(2)}) async-start(bf16[4,112,1152]{2,1,0:T(8,128)(2,1)} %merge_small.1), calls=%async_computation.2 | async-start | bytes 2064384 | tf_op jit(solution)/shard_map/all_to_all | solution.py:913
  195.6 2.2 copy-start.21
  195.6 79.3 %collective-permute-start.23 = (f32[1,256]{1,0:T(1,128)}, f32[1,256]{1,0:T(1,128)}, u32[]{:S(2)}, u32[]{:S(2)}) collective-permute-start(f32[1,256]{1,0:T(1,128)} %add.41.refs_0_), channel_id=1, source_target_pairs={{0,6},{6,0},{2,4},{4,2},{1,7},{7,1},{3,5},{5,3},{8,14},{14,8},{10,... | collective-permute-start | bytes 3080 | tf_op jit(solution)/shard_map/ppermute | solution.py:793
  197.7 24.6 %collective-permute-start.18 = (bf16[96,1920]{1,0:T(8,128)(2,1)}, bf16[96,1920]{1,0:T(8,128)(2,1)}, u32[]{:S(2)}, u32[]{:S(2)}) collective-permute-start(bf16[96,1920]{1,0:T(8,128)(2,1)} %add.40.refs_0_), channel_id=1, source_target_pairs={{0,6},{6,0},{2,4},{4,2},{1,7},{7,1},{3,5},{5,3},{8,14},{14,8},{10,... | collective-permute-start | bytes 1105928 | tf_op jit(solution)/shard_map/ppermute | solution.py:793
  208.5 11.7 %collective-permute-start.17 = (bf16[112,1152]{1,0:T(8,128)(2,1)S(1)}, bf16[112,1152]{1,0:T(8,128)(2,1)S(1)}, u32[]{:S(2)}, u32[]{:S(2)}) collective-permute-start(bf16[112,1152]{1,0:T(8,128)(2,1)S(1)} %total.3.refs_0_), channel_id=1, source_target_pairs={{0,2},{2,0},{4,6},{6,4},{1,3},{3,1},{5,7},{7,5},{8,10},{10,8},{12,... | collective-permute-start | bytes 774152 | tf_op jit(solution)/shard_map/ppermute | solution.py:793
  212.3 0.9 copy-start.3
  213.2 0.9 copy-start.4
  215.7 59.9 %all-to-all-start.2 = ((bf16[4,3,2,2,32,768]{5,4,3,2,1,0:T(8,128)(2,1)}), bf16[4,3,2,2,32,768]{5,4,3,2,1,0:T(8,128)(2,1)}, u32[]{:S(2)}, u32[]{:S(2)}) async-start(bf16[4,3,2,2,32,768]{5,4,3,2,1,0:T(8,128)(2,1)} %copies.1), calls=%async_computation.5 | async-start | bytes 4718592 | tf_op jit(solution)/shard_map/all_to_all | solution.py:913
  220.3 14.1 %collective-permute-start.19 = (bf16[112,1152]{1,0:T(8,128)(2,1)S(1)}, bf16[112,1152]{1,0:T(8,128)(2,1)S(1)}, u32[]{:S(2)}, u32[]{:S(2)}) collective-permute-start(bf16[112,1152]{1,0:T(8,128)(2,1)S(1)} %add.43.refs_0_), channel_id=1, source_target_pairs={{0,6},{6,0},{2,4},{4,2},{1,7},{7,1},{3,5},{5,3},{8,14},{14,8},{10,... | collective-permute-start | bytes 774152 | tf_op jit(solution)/shard_map/ppermute | solution.py:793
  223.5 31.6 %collective-permute-start.22 = (bf16[96,1920]{1,0:T(8,128)(2,1)S(1)}, bf16[96,1920]{1,0:T(8,128)(2,1)S(1)}, u32[]{:S(2)}, u32[]{:S(2)}) collective-permute-start(bf16[96,1920]{1,0:T(8,128)(2,1)S(1)} %add.44.refs_0_), channel_id=1, source_target_pairs={{0,24},{8,16},{16,8},{24,0},{1,25},{9,17},{17,9},{25,1},{2,26},{10... | collective-permute-start | bytes 1105928 | tf_op jit(solution)/shard_map/ppermute | solution.py:785
  225.9 37.4 %collective-permute-start.21 = (bf16[96,1920]{1,0:T(8,128)(2,1)S(1)}, bf16[96,1920]{1,0:T(8,128)(2,1)S(1)}, u32[]{:S(2)}, u32[]{:S(2)}) collective-permute-start(bf16[96,1920]{1,0:T(8,128)(2,1)S(1)} %add.44.refs_0_), channel_id=1, source_target_pairs={{0,16},{8,24},{16,0},{24,8},{1,17},{9,25},{17,1},{25,9},{2,18},{10... | collective-permute-start | bytes 1105928 | tf_op jit(solution)/shard_map/ppermute | solution.py:785
  226.1 37.1 %collective-permute-start.20 = (bf16[96,1920]{1,0:T(8,128)(2,1)S(1)}, bf16[96,1920]{1,0:T(8,128)(2,1)S(1)}, u32[]{:S(2)}, u32[]{:S(2)}) collective-permute-start(bf16[96,1920]{1,0:T(8,128)(2,1)S(1)} %add.44.refs_0_), channel_id=1, source_target_pairs={{0,8},{8,0},{16,24},{24,16},{1,9},{9,1},{17,25},{25,17},{2,10},{10... | collective-permute-start | bytes 1105928 | tf_op jit(solution)/shard_map/ppermute | solution.py:785
  235.1 44.8 %collective-permute-start.26 = (bf16[112,1152]{1,0:T(8,128)(2,1)}, bf16[112,1152]{1,0:T(8,128)(2,1)}, u32[]{:S(2)}, u32[]{:S(2)}) collective-permute-start(bf16[112,1152]{1,0:T(8,128)(2,1)} %add.45.refs_0_), channel_id=1, source_target_pairs={{0,24},{8,16},{16,8},{24,0},{1,25},{9,17},{17,9},{25,1},{2,26},{10... | collective-permute-start | bytes 774152 | tf_op jit(solution)/shard_map/ppermute | solution.py:785
  255.1 24.8 %collective-permute-start.25 = (bf16[112,1152]{1,0:T(8,128)(2,1)}, bf16[112,1152]{1,0:T(8,128)(2,1)}, u32[]{:S(2)}, u32[]{:S(2)}) collective-permute-start(bf16[112,1152]{1,0:T(8,128)(2,1)} %add.45.refs_0_), channel_id=1, source_target_pairs={{0,16},{8,24},{16,0},{24,8},{1,17},{9,25},{17,1},{25,9},{2,18},{10... | collective-permute-start | bytes 774152 | tf_op jit(solution)/shard_map/ppermute | solution.py:785
  263.2 16.7 %collective-permute-start.24 = (bf16[112,1152]{1,0:T(8,128)(2,1)}, bf16[112,1152]{1,0:T(8,128)(2,1)}, u32[]{:S(2)}, u32[]{:S(2)}) collective-permute-start(bf16[112,1152]{1,0:T(8,128)(2,1)} %add.45.refs_0_), channel_id=1, source_target_pairs={{0,8},{8,0},{16,24},{24,16},{1,9},{9,1},{17,25},{25,17},{2,10},{10... | collective-permute-start | bytes 774152 | tf_op jit(solution)/shard_map/ppermute | solution.py:785
  264.4 11.2 %copy-start.1 = (s32[4]{0:T(128)S(1)}, s32[4]{0:T(128)}, u32[]{:S(2)}) copy-start(s32[4]{0:T(128)} %pad_add_fusion.place_ref.c_ref) | copy-start | bytes 52
  264.5 17.0 %collective-permute-start.27 = (bf16[4,96,1920]{2,1,0:T(8,128)(2,1)}, bf16[4,96,1920]{2,1,0:T(8,128)(2,1)}, u32[]{:S(2)}, u32[]{:S(2)}) collective-permute-start(bf16[4,96,1920]{2,1,0:T(8,128)(2,1)} %stack.22.refs_0_), channel_id=1, source_target_pairs={{0,1},{1,0},{2,3},{3,2},{4,5},{5,4},{6,7},{7,6},{8,9},{9,8},{10,11... | collective-permute-start | bytes 4423688 | tf_op jit(solution)/shard_map/ppermute | solution.py:781
  281.4 2.7 collective-permute-start.28
  (2 other events, 1.4 us)
Sparse Core Ops, SparseCore 0:
  69.8 67.4 reduce-scatter.3
  139.6 20.7 reduce-scatter.5
  169.3 26.8 reduce-scatter.7

commit v2 on v1

--- a/solution.py
+++ b/solution.py
@@ -679,8 +679,7 @@
 
 
 def finish_kernel(axes, place_ref, tally_ref, *refs):
-    blocks, (gin_ref, gout_ref, counts_ref, hold_ref) = refs[:-4], refs[-4:]
-    spots = [(ref, k) for ref in blocks for k in range(ref.shape[1])]
+    near_ref, last_ref, gin_ref, gout_ref, counts_ref, hold_ref = refs
     d = gin_ref.shape[1]
     lane = lax.broadcasted_iota(jnp.int32, tally_ref.shape, 1)
     counts = [jnp.sum(jnp.where(lane == 128 + e, tally_ref[...], 0.0)) for e in range(2)]
@@ -688,14 +687,20 @@
         counts_ref[e] = counts[e].astype(jnp.int32)
     unit = hold_ref.shape[0]
     step = unit // 4
-    for p, ((ref, part), axis) in enumerate(zip(spots, axes)):
+    for p, axis in enumerate(axes):
         for e in range(2):
             factor = jnp.full((1, d), counts[0] + counts[1], f32) / (2.0 * counts[e])
             for j in range(2):
                 for k in range(4):
-                    to = 2 * (k & 1) + (k >> 1) if axis == X else k
-                    rows = slice(to * step, (to + 1) * step)
-                    hold_ref[rows, :] = ref[k, part, e, j].astype(f32) * factor
+                    x, y = k & 1, k >> 1
+                    if p < 2:
+                        x, y = place_ref[1] ^ x, place_ref[2] ^ y
+                        piece = near_ref[k, p, e, j]
+                    else:
+                        piece = last_ref[k, 0, e, j]
+                    to = 2 * x + y if axis == X else 2 * y + x
+                    rows = pl.ds(pl.multiple_of(to * step, step), step)
+                    hold_ref[rows, :] = piece.astype(f32) * factor
                 where = slice(p * unit, (p + 1) * unit)
                 if j == 0:
                     gin_ref[e, :, where] = hold_ref[...].T
@@ -1003,11 +1008,13 @@
     tally = line(add, tally, away_t)
     away_t = along_z(tally, FAR)
     half_a = line(add, keep_a, away_a)
+    around_ab = around(line(stack, half_a, half_b))
     result_out = line(lambda v: result_of(info, (hid_a, hid_b, hid_c), w_out, v, UNIT), resid)
     piece_2 = line(total, all_2)
     away_2 = along_z(piece_2, NEAR)
     PHASE[0] = "tail"
-    all_e = exchange(line(copies, half_a, half_b, half_c))
+    all_e = exchange(line(copies, half_c))
+    block_ab = line(stack, *around_ab)
     piece_2 = line(add, piece_2, away_2)
     away_2 = along_z(piece_2, FAR)
     piece_1 = line(add, piece_1, away_1)
@@ -1018,7 +1025,7 @@
     other_1 = swap_core(whole_1)
     tally = line(add, tally, away_t)
     grad_w_in, grad_w_out, all_counts = line(
-        lambda v: finish_experts((Y, X, Y), place, tie(tally, piece_2), (v,)), all_e
+        lambda v: finish_experts((Y, X, Y), place, tie(tally, piece_2), (block_ab, v)), all_e
     )
     whole_2 = line(stack, *around_2)
     other_2 = swap_core(whole_2)

time: 300 us -> 286 us (0.953)
  waiting for transfers between devices: 45.1 us -> 30.1 us
    ppermute x14 -> x17, waiting for transfers between devices: 31.9 us -> 15.6 us  [swap(): return lax.ppermute(v, 'dp', [(i, i ^ axis) for i in range(4)])]
    ppermute x7, starting transfers between devices: 12.8 us -> 7.43 us  [swap_core(): return lax.ppermute(v, 'core', [(0, 1), (1, 0)])]
    ppermute x14 -> x17, starting transfers between devices: 11.4 us -> 15.1 us  [swap(): return lax.ppermute(v, 'dp', [(i, i ^ axis) for i in range(4)])]
    pallas_call x18 -> x20, Pallas kernels: 20.5 us -> 20.1 us  [small(): pl.pallas_call(functools.partial(small_kernel, fn), in_specs=[resident()]...]
  transfers between devices with their start and end apart: 35 -> 38, of which waited for: 8 -> 8; matrix products, arithmetic and copies ran while one was open for 0% -> 0% of each run, Pallas kernels for 54% -> 57%
where the time goes in v2:
time: 286 us; the launch traced here: 281 us
  Pallas kernels  183 us (64%)
  starting transfers between devices  48.1 us (17%)
  waiting for transfers between devices  30.1 us (11%)
  between operations  14.2 us (5%)
  local copies, waits for them, and re-layouts  4.89 us (2%)
    pallas_call x3, Pallas kernels, expert_part(): pl.pallas_call(functools.partial(expert_kernel, axis), grid_spec=pltpu.Pr...  33 us
    pallas_call x2, Pallas kernels, attn_bwd(): pl.pallas_call(functools.partial(bwd_kernel, qb, win), out_shape=pltpu.VM...  23.4 us
    pallas_call x20, Pallas kernels, small(): pl.pallas_call(functools.partial(small_kernel, fn), in_specs=[resident()]...  20.1 us
    pallas_call x1, Pallas kernels, post_ffn(): pl.pallas_call(functools.partial(post_kernel, n, unit), grid_spec=pltpu.P...  16.4 us
    ppermute x17, waiting for transfers between devices, swap(): return lax.ppermute(v, 'dp', [(i, i ^ axis) for i in range(4)])  15.6 us
    pallas_call x2, Pallas kernels, weight_grads(): pl.pallas_call(weight_kernel, grid_spec=pltpu.PrefetchScalarGridSpec(num_...  15.5 us
    ppermute x17, starting transfers between devices, swap(): return lax.ppermute(v, 'dp', [(i, i ^ axis) for i in range(4)])  15.1 us
    pallas_call x1, Pallas kernels, attn_fwd(): pl.pallas_call(functools.partial(fwd_kernel, qb, win), out_shape=(pltpu.V...  13.8 us
  transfers between devices with their start and end apart: 38, of which 8 were waited for; matrix products, arithmetic and copies ran while one was open for 0% of the time, Pallas kernels for 57%

profile of v2, /device:TPU:9, one launch (start us, length us, event | category | flops | bytes accessed | tf_op | source)
XLA Modules:
  0.0 280.6 jit_solution(4651306987497094014)
XLA Ops:
  7.8 2.9 %prelude.1 = (s32[3,4]{1,0:T(4,128)}, s32[3]{0:T(128)}, f32[1024,128]{1,0:T(8,128)}, f32[1,1024]{1,0:T(1,128)}, f32[1024,128]{1,0:T(8,128)}, /*index=5*/f32[1,256]{1,0:T(1,128)}) custom-call(s32[4]{0:T(128)} %pad_add_fusion.place_ref.c_ref, s32[8,128]{1,0:T(8,128)} %bitcast.18, s32[8,128]{1,0:T(8,128)} %bitcast.19), custom_call_target="tpu_custom_call" | custom-call | flops 199999995904 | bytes 1048576 | tf_op jit(solution)/shard_map/prelude/pallas_call | solution.py:338
  11.5 8.5 %ln_qkv.1 = (bf16[768,1024]{1,0:T(8,128)(2,1)}, bf16[1024,2304]{1,0:T(8,128)(2,1)}) custom-call(bf16[1024,768]{1,0:T(8,128)(2,1)} %refs_2_, f32[768]{0:T(1024)S(1)} %copy-done.9, f32[768]{0:T(1024)S(1)} %copy-done.5, bf16[768,2304]{1,0:T(8,128)(2,1)} %refs_4_.1), custom_call_target="tpu_custom_call" | custom-call | flops 799999983616 | bytes 1048576 | tf_op jit(solution)/shard_map/ln_qkv/pallas_call | solution.py:278
  20.0 1.3 add.35.refs_0_
  21.2 1.2 collective-permute-start.1
  22.5 13.8 %attn_fwd.1 = (bf16[1024,768]{1,0:T(8,128)(2,1)S(1)}, bf16[768,1024]{1,0:T(8,128)(2,1)}, f32[6,2,1024]{2,1,0:T(2,128)S(1)}) custom-call(s32[3,4]{1,0:T(4,128)S(1)} %copy-done.31, bf16[1024,2304]{1,0:T(8,128)(2,1)} %get-tuple-element.110.q_ref.k_ref.v_ref, bf16[1024,2304]{1,0:T(8,128)(2,1)} %get-tuple-element.110.q_ref.k_ref.v_ref, ...), custom_call_target="tpu_custom_call" | custom-call | flops 1399999954944 | bytes 1048576 | tf_op jit(solution)/shard_map/attn_fwd/pallas_call | solution.py:124
  36.3 1.3 add.36.refs_0_
  37.6 1.2 collective-permute-start.2
  38.8 5.8 %proj_ln.1 = (f32[1024,768]{1,0:T(8,128)}, bf16[1024,768]{1,0:T(8,128)(2,1)S(1)}, bf16[1024,768]{1,0:T(8,128)(2,1)S(1)}) custom-call(bf16[1024,768]{1,0:T(8,128)(2,1)} %refs_2_, bf16[1024,768]{1,0:T(8,128)(2,1)S(1)} %get-tuple-element.115.mixed_ref, bf16[1024,768]{1,0:T(8,128)(2,1)} %refs_5_.2, f32[1024,128]{1,0:T(8,128)S(1)} %copy-done.26, ...), custom_call_target="tpu_custom_call" | custom-call | flops 699999977472 | bytes 1048576 | tf_op jit(solution)/shard_map/proj_ln/pallas_call | solution.py:368
  45.3 10.9 %expert_part.3 = (bf16[1024,1024]{1,0:T(8,128)(2,1)}, bf16[1024,1024]{1,0:T(8,128)(2,1)}, bf16[4,2,64,768]{3,2,1,0:T(8,128)(2,1)}, bf16[4,2,64,768]{3,2,1,0:T(8,...) custom-call(s32[3]{0:T(128)S(1)} %copy-done.22, s32[4]{0:T(128)S(1)} %copy-done, ...), custom_call_target="tpu_custom_call" | custom-call | flops 1100000002048 | bytes 1048576 | tf_op jit(solution)/shard_map/expert_part/pallas_call | solution.py:454
  57.1 1.4 collective-permute-start.5
  58.5 11.2 %expert_part.4 = (bf16[1024,1024]{1,0:T(8,128)(2,1)}, bf16[1024,1024]{1,0:T(8,128)(2,1)}, bf16[8,4,2,2,32,768]{5,4,3,2,1,0:T(8,128)(2,1)}) custom-call(s32[3]{0:T(128)S(1)} %copy-done.22, s32[4]{0:T(128)S(1)} %copy-done, bf16[1024,768]{1,0:T(8,128)(2,1)S(1)} %get-tuple-element.125.h2_ref, bf16[1024,768]{1,0:T(8,128)(2,1)S(1)} %get-tuple-element.121.cot_ref, ...), custom_call_target="tpu_custom_call" | custom-call | flops 1100000002048 | bytes 1048576 | tf_op jit(solution)/shard_map/expert_part/pallas_call | solution.py:454
  70.0 10.9 %expert_part.5 = (bf16[1024,1024]{1,0:T(8,128)(2,1)}, bf16[1024,1024]{1,0:T(8,128)(2,1)}, bf16[4,2,64,768]{3,2,1,0:T(8,128)(2,1)}, bf16[4,2,64,768]{3,2,1,0:T(8,...) custom-call(s32[3]{0:T(128)S(1)} %copy-done.22, s32[4]{0:T(128)S(1)} %copy-done, ...), custom_call_target="tpu_custom_call" | custom-call | flops 1100000002048 | bytes 1048576 | tf_op jit(solution)/shard_map/expert_part/pallas_call | solution.py:454
  81.3 16.4 %post_ffn.1 = (f32[1024,768]{1,0:T(8,128)}, bf16[1024,768]{1,0:T(8,128)(2,1)}, bf16[1024,768]{1,0:T(8,128)(2,1)}, f32[2,768]{1,0:T(2,128)S(1)}) custom-call(s32[3]{0:T(128)S(1)} %copy-done.22, bf16[1024,1024]{1,0:T(8,128)(2,1)} %get-tuple-element.132.refs_0_, bf16[1024,1024]{1,0:T(8,128)(2,1)} %get-tuple-element.134.refs_1_, ...), custom_call_target="tpu_custom_call" | custom-call | flops 999999995904 | bytes 1048576 | tf_op jit(solution)/shard_map/post_ffn/pallas_call | solution.py:506
  97.7 1.8 collective-permute-start.8
  99.6 4.5 %sum_sides.2 = (bf16[4,2,2,32,768]{4,3,2,1,0:T(8,128)(2,1)S(1)}, bf16[4,2,2,32,768]{4,3,2,1,0:T(8,128)(2,1)}) custom-call(s32[4]{0:T(128)S(1)} %copy-done, s32[8]{0:T(128)S(1)} %fusion.voice_ref, bf16[4,2,64,768]{3,2,1,0:T(8,128)(2,1)S(1)} %copy-done.28, bf16[4,2,64,768]{3,2,1,0:T(8,128)(2,1)} %collective-permute-done.3.b_ref, ...), custom_call_target="tpu_custom_call" | custom-call | flops 299999985664 | bytes 1048576 | tf_op jit(solution)/shard_map/sum_sides/pallas_call | solution.py:666
  104.3 11.7 %attn_bwd.2.refs_1_.refs_0_ = bf16[3,1024,384]{2,1,0:T(8,128)(2,1)S(1)} custom-call(s32[3,4]{1,0:T(4,128)S(1)} %copy-done.32, bf16[1024,2304]{1,0:T(8,128)(2,1)} %get-tuple-element.110.q_ref.k_ref.v_ref, bf16[1024,2304]{1,0:T(8,128)(2,1)} %get-tuple-element.110.q_ref.k_ref.v_ref, bf16[1024,2304]{1,0:T(8,128)(2,1)} %get-tuple-element.110.q_ref.k_ref.v_ref, ...), custom_call_target="tpu_custom_call" | custom-call | flops 1110000009216 | bytes 1048576 | tf_op jit(solution)/shard_map/attn_bwd/pallas_call | solution.py:218
  116.0 9.5 %weight_grads.2 = (bf16[384,1920]{1,0:T(8,128)(2,1)}, bf16[384,1920]{1,0:T(8,128)(2,1)}) custom-call(s32[4]{0:T(128)S(1)} %copy-done, bf16[768,1024]{1,0:T(8,128)(2,1)} %get-tuple-element.159.refs_0_, bf16[3,1024,384]{2,1,0:T(8,128)(2,1)S(1)} %attn_bwd.2.refs_1_.refs_0_, bf16[768,1024]{1,0:T(8,128)(2,1)} %get-tuple-element.145.ot_ref.refs_2_, ...), custom_call_target="tpu_custom_call" | custom-call | flops 599999971328 | bytes 1048576 | tf_op jit(solution)/shard_map/weight_grads/pallas_call | solution.py:589
  125.7 4.5 %sum_sides.3 = (bf16[4,2,2,32,768]{4,3,2,1,0:T(8,128)(2,1)S(1)}, bf16[4,2,2,32,768]{4,3,2,1,0:T(8,128)(2,1)}) custom-call(s32[4]{0:T(128)S(1)} %copy-done, s32[8]{0:T(128)S(1)} %copy-done.15, bf16[4,2,64,768]{3,2,1,0:T(8,128)(2,1)S(1)} %copy-done.27, bf16[4,2,64,768]{3,2,1,0:T(8,128)(2,1)} %collective-permute-done.6.b_ref, ...), custom_call_target="tpu_custom_call" | custom-call | flops 299999985664 | bytes 1048576 | tf_op jit(solution)/shard_map/sum_sides/pallas_call | solution.py:666
  130.6 4.3 %collective-permute-done.9.refs_1_ = bf16[4,2,2,32,768]{4,3,2,1,0:T(8,128)(2,1)} collective-permute-done((bf16[4,2,2,32,768]{4,3,2,1,0:T(8,128)(2,1)}, bf16[4,2,2,32,768]{4,3,2,1,0:T(8,128)(2,1)}, u32[]{:S(2)}, u32[]{:S(2)}) %collective-permute-start.9) | collective-permute-done | bytes 786464 | tf_op jit(solution)/shard_map/ppermute | solution.py:790
  134.9 2.2 add.38
  137.4 1.1 copy-done.2
  138.5 1.3 split.2
  139.9 2.8 %merge.1 = bf16[384,1920]{1,0:T(8,128)(2,1)} custom-call(bf16[384,1920]{1,0:T(8,128)(2,1)S(1)} %copy-done.21, bf16[384,1920]{1,0:T(8,128)(2,1)} %collective-permute-done.10.refs_1_), custom_call_target="tpu_custom_call" | custom-call | flops 99999997952 | bytes 1048576 | tf_op jit(solution)/shard_map/merge/pallas_call | solution.py:812
  142.7 4.4 %all-to-all-start = ((bf16[4,96,1920]{2,1,0:T(8,128)(2,1)}), bf16[4,96,1920]{2,1,0:T(8,128)(2,1)}, u32[]{:S(2)}, u32[]{:S(2)}) async-start(bf16[4,96,1920]{2,1,0:T(8,128)(2,1)} %bitcast.9), calls=%async_computation.1 | async-start | bytes 2949120 | tf_op jit(solution)/shard_map/all_to_all | solution.py:918
  147.3 1.2 collective-permute-start.12
  148.5 11.7 %attn_bwd.3.refs_1_ = bf16[3,1024,384]{2,1,0:T(8,128)(2,1)S(1)} custom-call(s32[3,4]{1,0:T(4,128)S(1)} %copy-done.32, bf16[1024,2304]{1,0:T(8,128)(2,1)} %get-tuple-element.110.q_ref.k_ref.v_ref, bf16[1024,2304]{1,0:T(8,128)(2,1)} %get-tuple-element.110.q_ref.k_ref.v_ref, bf16[1024,2304]{1,0:T(8,128)(2,1)} %get-tuple-element.110.q_ref.k_ref.v_ref, ...), custom_call_target="tpu_custom_call" | custom-call | flops 1110000009216 | bytes 1048576 | tf_op jit(solution)/shard_map/attn_bwd/pallas_call | solution.py:218
  160.2 6.0 %weight_grads.3 = (bf16[384,1152]{1,0:T(8,128)(2,1)}, bf16[384,1152]{1,0:T(8,128)(2,1)}) custom-call(s32[4]{0:T(128)S(1)} %copy-done, bf16[768,1024]{1,0:T(8,128)(2,1)} %get-tuple-element.159.refs_0_, bf16[3,1024,384]{2,1,0:T(8,128)(2,1)S(1)} %attn_bwd.3.refs_1_), custom_call_target="tpu_custom_call" | custom-call | flops 359999995904 | bytes 1048576 | tf_op jit(solution)/shard_map/weight_grads/pallas_call | solution.py:589
  166.2 0.9 collective-permute-start.13
  167.0 2.2 add.39
  169.3 2.0 collective-permute-start.15
  171.3 2.2 collective-permute-done.12.refs_1_
  173.5 1.1 split.3
  174.6 1.3 collective-permute-start.16
  175.8 1.6 total.2.refs_0_
  177.5 9.9 %input_grad.1 = (f32[1024,768]{1,0:T(8,128)}, f32[2,768]{1,0:T(2,128)S(1)}) custom-call(bf16[3,1024,384]{2,1,0:T(8,128)(2,1)} %copy-done.17, bf16[3,1024,384]{2,1,0:T(8,128)(2,1)} %copy-done.18, bf16[1024,768]{1,0:T(8,128)(2,1)} %refs_2_, f32[1024,768]{1,0:T(8,128)} %get-tuple-element.136.refs_3_, bf16[768,2304]{1,0:T(8,128)(2,1)} %refs_4_.1, f32[768]{0:T(1024)S(1)} %copy-done.10), custom_call_target="tpu_custom_call" | custom-call | flops 12000000000 | bytes 1048576 | tf_op jit(solution)/shard_map/input_grad/pallas_call | solution.py:627
  187.5 1.2 merge_small.1
  188.7 3.5 %all-to-all-start.1 = ((bf16[4,112,1152]{2,1,0:T(8,128)(2,1)}), bf16[4,112,1152]{2,1,0:T(8,128)(2,1)S(1)}, u32[]{:S(2)}, u32[]{:S(2)}) async-start(bf16[4,112,1152]{2,1,0:T(8,128)(2,1)} %merge_small.1), calls=%async_computation.3 | async-start | bytes 2064384 | tf_op jit(solution)/shard_map/all_to_all | solution.py:918
  192.2 2.0 collective-permute-done.14.refs_1_
  194.2 0.8 add.40.refs_0_
  195.6 2.1 collective-permute-start.26
  197.9 0.9 copy-done.3
  198.8 1.0 collective-permute-start.19
  199.8 1.0 collective-permute-start.18
  201.5 10.6 %result_of.1 = bf16[1024,768]{1,0:T(8,128)(2,1)} custom-call(s32[3]{0:T(128)S(1)} %copy-done.23, bf16[1024,1024]{1,0:T(8,128)(2,1)} %get-tuple-element.124.refs_0_, bf16[1024,1024]{1,0:T(8,128)(2,1)} %get-tuple-element.122.refs_1_, bf16[1024,1024]{1,0:T(8,128)(2,1)} %get-tuple-element.126.refs_2_, bf16[2,3072,768]{2,1,0:T(8,128)(2,1)} %refs_3_.3, ...), custom_call_target="tpu_custom_call" | custom-call | flops 9600000000 | bytes 1048576 | tf_op jit(solution)/shard_map/result_of/pallas_call | solution.py:539
  212.3 0.9 copy-done.4
  213.2 0.9 copies.1
  214.1 4.4 %all-to-all-start.2 = ((bf16[4,1,2,2,32,768]{5,4,3,2,1,0:T(8,128)(2,1)}), bf16[4,1,2,2,32,768]{5,4,3,2,1,0:T(8,128)(2,1)}, u32[]{:S(2)}, u32[]{:S(2)}) async-start(bf16[4,1,2,2,32,768]{5,4,3,2,1,0:T(8,128)(2,1)} %copies.1), calls=%async_computation.5 | async-start | bytes 1572864 | tf_op jit(solution)/shard_map/all_to_all | solution.py:918
  218.6 3.7 %collective-permute-start.20 = (bf16[112,1152]{1,0:T(8,128)(2,1)S(1)}, bf16[112,1152]{1,0:T(8,128)(2,1)S(1)}, u32[]{:S(2)}, u32[]{:S(2)}) collective-permute-start(bf16[112,1152]{1,0:T(8,128)(2,1)S(1)} %total.3.refs_0_), channel_id=1, source_target_pairs={{0,2},{2,0},{4,6},{6,4},{1,3},{3,1},{5,7},{7,5},{8,10},{10,8},{12,... | collective-permute-start | bytes 774152 | tf_op jit(solution)/shard_map/ppermute | solution.py:798
  222.4 1.1 copy-done.19
  223.5 3.1 %collective-permute-done.20.refs_1_ = bf16[112,1152]{1,0:T(8,128)(2,1)S(1)} collective-permute-done((bf16[112,1152]{1,0:T(8,128)(2,1)S(1)}, bf16[112,1152]{1,0:T(8,128)(2,1)S(1)}, u32[]{:S(2)}, u32[]{:S(2)}) %collective-permute-start.20) | collective-permute-done | bytes 258080 | tf_op jit(solution)/shard_map/ppermute | solution.py:798
  226.6 1.6 collective-permute-start.22
  228.3 1.2 add.44.refs_0_
  229.5 2.2 collective-permute-start.25
  232.2 6.9 %collective-permute-done.22.refs_1_ = bf16[112,1152]{1,0:T(8,128)(2,1)S(1)} collective-permute-done((bf16[112,1152]{1,0:T(8,128)(2,1)S(1)}, bf16[112,1152]{1,0:T(8,128)(2,1)S(1)}, u32[]{:S(2)}, u32[]{:S(2)}) %collective-permute-start.22) | collective-permute-done | bytes 258080 | tf_op jit(solution)/shard_map/ppermute | solution.py:798
  239.8 1.8 collective-permute-start.29
  241.8 9.0 %collective-permute-done.24.refs_2_ = bf16[96,1920]{1,0:T(8,128)(2,1)S(1)} collective-permute-done((bf16[96,1920]{1,0:T(8,128)(2,1)S(1)}, bf16[96,1920]{1,0:T(8,128)(2,1)S(1)}, u32[]{:S(2)}, u32[]{:S(2)}) %collective-permute-start.24) | collective-permute-done | bytes 368672 | tf_op jit(solution)/shard_map/ppermute | solution.py:790
  250.9 1.6 collective-permute-start.27
  252.4 1.3 stack.26.refs_0_
  253.7 4.1 %collective-permute-start.30 = (bf16[4,96,1920]{2,1,0:T(8,128)(2,1)}, bf16[4,96,1920]{2,1,0:T(8,128)(2,1)}, u32[]{:S(2)}, u32[]{:S(2)}) collective-permute-start(bf16[4,96,1920]{2,1,0:T(8,128)(2,1)} %stack.26.refs_0_), channel_id=1, source_target_pairs={{0,1},{1,0},{2,3},{3,2},{4,5},{5,4},{6,7},{7,6},{8,9},{9,8},{10,11... | collective-permute-start | bytes 4423688 | tf_op jit(solution)/shard_map/ppermute | solution.py:786
  258.5 4.2 %finish_experts.1 = (f32[2,768,384]{2,1,0:T(8,128)}, f32[2,384,768]{2,1,0:T(8,128)}, s32[2]{0:T(128)}) custom-call(s32[4]{0:T(128)S(1)} %copy-done.1, f32[1,256]{1,0:T(1,128)S(1)} %add.46.tally_ref, bf16[4,2,2,2,32,768]{5,4,3,2,1,0:T(8,128)(2,1)S(1)} %copy-done.20, bf16[4,1,2,2,32,768]{5,4,3,2,1,0:T(8,128)(2,1)} %all-to-all-done.2.refs_1_), custom_call_target="tpu_custom_call" | custom-call | flops 399999991808 | bytes 1048576 | tf_op jit(solution)/shard_map/finish_experts/pallas_call | solution.py:715
  262.8 1.4 stack.27.refs_2_
  264.2 0.8 collective-permute-start.31
  265.0 2.3 collective-permute-done.31.refs_3_
  267.2 6.2 %join_weights.1 = (f32[2,384,2304]{2,1,0:T(8,128)}, f32[2,384,768]{2,1,0:T(8,128)}, f32[8,768]{1,0:T(8,128)S(1)}) custom-call(s32[4]{0:T(128)S(1)} %copy-done.1, bf16[4,96,1920]{2,1,0:T(8,128)(2,1)} %stack.26.refs_0_, bf16[4,96,1920]{2,1,0:T(8,128)(2,1)} %collective-permute-done.30.refs_1_, bf16[4,112,1152]{2,1,0:T(8,128)(2,1)S(1)} %stack.27.refs_2_, ...), custom_call_target="tpu_custom_call" | custom-call | flops 499999997952 | bytes 1048576 | tf_op jit(solution)/shard_map/join_weights/pallas_call | solution.py:756
  (125 shorter events, 9.7 us)
Async XLA Ops:
  7.2 130.2 %reduce-scatter.4.cloned.1.call-start = ((), (), s32[]{:S(2)}) async-start(), calls=%async_computation.6 | async-start | bytes 7077888 | tf_op jit(solution)/shard_map/reduce_scatter | solution.py:950
  7.8 3.6 %copy-start.5 = (f32[768]{0:T(1024)S(1)}, f32[768]{0:T(1024)}, u32[]{:S(2)}) copy-start(f32[768]{0:T(1024)} %shift_ref.2) | copy-start | bytes 9220
  7.8 3.6 %copy-start.9 = (f32[768]{0:T(1024)S(1)}, f32[768]{0:T(1024)}, u32[]{:S(2)}) copy-start(f32[768]{0:T(1024)} %refs_5_.3) | copy-start | bytes 9220
  10.7 9.2 %collective-permute-start = (f32[1,256]{1,0:T(1,128)}, f32[1,256]{1,0:T(1,128)}, u32[]{:S(2)}, u32[]{:S(2)}) collective-permute-start(f32[1,256]{1,0:T(1,128)} %get-tuple-element.109.refs_0_), channel_id=1, source_target_pairs={{0,1},{1,0},{2,3},{3,2},{4,5},{5,4},{6,7},{7,6},{8,9},{9,8},{10,11... | collective-permute-start | bytes 3080 | tf_op jit(solution)/shard_map/ppermute | solution.py:786
  11.5 8.5 %copy-start.13 = (f32[1,256]{1,0:T(1,128)S(1)}, f32[1,256]{1,0:T(1,128)}, u32[]{:S(2)}) copy-start(f32[1,256]{1,0:T(1,128)} %get-tuple-element.109.refs_0_) | copy-start | bytes 3076
  19.9 2.5 copy-start.24
  19.9 2.5 copy-start.29
  19.9 2.5 copy-start.31
  21.2 15.0 %collective-permute-start.1 = (f32[1,256]{1,0:T(1,128)}, f32[1,256]{1,0:T(1,128)}, u32[]{:S(2)}, u32[]{:S(2)}) collective-permute-start(f32[1,256]{1,0:T(1,128)} %add.35.refs_0_), channel_id=1, source_target_pairs={{0,8},{8,0},{16,24},{24,16},{1,9},{9,1},{17,25},{25,17},{2,10},{10... | collective-permute-start | bytes 3080 | tf_op jit(solution)/shard_map/ppermute | solution.py:790
  36.2 2.6 copy-start.6
  36.2 2.6 copy-start.7
  36.3 2.6 copy-start.26
  37.6 7.0 %collective-permute-start.2 = (f32[1,256]{1,0:T(1,128)}, f32[1,256]{1,0:T(1,128)}, u32[]{:S(2)}, u32[]{:S(2)}) collective-permute-start(f32[1,256]{1,0:T(1,128)} %add.36.refs_0_), channel_id=1, source_target_pairs={{0,16},{8,24},{16,0},{24,8},{1,17},{9,25},{17,1},{25,9},{2,18},{10... | collective-permute-start | bytes 3080 | tf_op jit(solution)/shard_map/ppermute | solution.py:790
  45.3 52.4 %copy-start.11 = (f32[1,256]{1,0:T(1,128)}, f32[1,256]{1,0:T(1,128)S(1)}, u32[]{:S(2)}) copy-start(f32[1,256]{1,0:T(1,128)S(1)} %add.37.refs_0_) | copy-start | bytes 3076
  56.2 43.3 %collective-permute-start.3 = (bf16[4,2,64,768]{3,2,1,0:T(8,128)(2,1)}, bf16[4,2,64,768]{3,2,1,0:T(8,128)(2,1)}, u32[]{:S(2)}, u32[]{:S(2)}) collective-permute-start(bf16[4,2,64,768]{3,2,1,0:T(8,128)(2,1)} %get-tuple-element.129), channel_id=1, source_target_pairs={{0,1},{1,0},{2,3},{3,2},{4,5},{5,4},{6,7},{7,6},{8,9},{9,8},{10,11... | collective-permute-start | bytes 2359304 | tf_op jit(solution)/shard_map/ppermute | solution.py:786
  56.8 42.7 %collective-permute-start.4 = (bf16[4,2,64,768]{3,2,1,0:T(8,128)(2,1)}, bf16[4,2,64,768]{3,2,1,0:T(8,128)(2,1)}, u32[]{:S(2)}, u32[]{:S(2)}) collective-permute-start(bf16[4,2,64,768]{3,2,1,0:T(8,128)(2,1)} %get-tuple-element.130), channel_id=1, source_target_pairs={{0,8},{8,0},{16,24},{24,16},{1,9},{9,1},{17,25},{25,17},{2,10},{10... | collective-permute-start | bytes 2359304 | tf_op jit(solution)/shard_map/ppermute | solution.py:790
  57.1 40.6 %collective-permute-start.5 = (bf16[4,2,64,768]{3,2,1,0:T(8,128)(2,1)}, bf16[4,2,64,768]{3,2,1,0:T(8,128)(2,1)}, u32[]{:S(2)}, u32[]{:S(2)}) collective-permute-start(bf16[4,2,64,768]{3,2,1,0:T(8,128)(2,1)} %get-tuple-element.131), channel_id=1, source_target_pairs={{0,9},{1,8},{8,1},{9,0},{16,25},{17,24},{24,17},{25,16},{2,11},{3,... | collective-permute-start | bytes 2359304 | tf_op jit(solution)/shard_map/ppermute | solution.py:794
  69.8 128.1 %reduce-scatter.6.cloned.1.call-start = ((), (), s32[]{:S(2)}) async-start(), calls=%async_computation.7 | async-start | bytes 983040 | tf_op jit(solution)/shard_map/reduce_scatter | solution.py:970
  70.0 11.3 %copy-start.8 = (f32[768]{0:T(1024)S(1)}, f32[768]{0:T(1024)}, u32[]{:S(2)}) copy-start(f32[768]{0:T(1024)} %refs_7_.1) | copy-start | bytes 9220
  80.9 44.7 %collective-permute-start.6 = (bf16[4,2,64,768]{3,2,1,0:T(8,128)(2,1)}, bf16[4,2,64,768]{3,2,1,0:T(8,128)(2,1)}, u32[]{:S(2)}, u32[]{:S(2)}) collective-permute-start(bf16[4,2,64,768]{3,2,1,0:T(8,128)(2,1)} %get-tuple-element.140), channel_id=1, source_target_pairs={{0,1},{1,0},{2,3},{3,2},{4,5},{5,4},{6,7},{7,6},{8,9},{9,8},{10,11... | collective-permute-start | bytes 2359304 | tf_op jit(solution)/shard_map/ppermute | solution.py:786
  81.1 44.6 %collective-permute-start.7 = (bf16[4,2,64,768]{3,2,1,0:T(8,128)(2,1)}, bf16[4,2,64,768]{3,2,1,0:T(8,128)(2,1)}, u32[]{:S(2)}, u32[]{:S(2)}) collective-permute-start(bf16[4,2,64,768]{3,2,1,0:T(8,128)(2,1)} %get-tuple-element.141), channel_id=1, source_target_pairs={{0,16},{8,24},{16,0},{24,8},{1,17},{9,25},{17,1},{25,9},{2,18},{10... | collective-permute-start | bytes 2359304 | tf_op jit(solution)/shard_map/ppermute | solution.py:790
  81.3 18.2 %copy-start.28 = (bf16[4,2,64,768]{3,2,1,0:T(8,128)(2,1)S(1)}, bf16[4,2,64,768]{3,2,1,0:T(8,128)(2,1)}, u32[]{:S(2)}) copy-start(bf16[4,2,64,768]{3,2,1,0:T(8,128)(2,1)} %get-tuple-element.128.a_ref) | copy-start | bytes 2359300
  97.7 6.3 %copy-start.14 = (s32[8]{0:T(128)}, s32[8]{0:T(128)S(1)}, u32[]{:S(2)}) copy-start(s32[8]{0:T(128)S(1)} %fusion.voice_ref) | copy-start | bytes 100
  97.7 27.9 %collective-permute-start.8 = (bf16[4,2,64,768]{3,2,1,0:T(8,128)(2,1)}, bf16[4,2,64,768]{3,2,1,0:T(8,128)(2,1)}, u32[]{:S(2)}, u32[]{:S(2)}) collective-permute-start(bf16[4,2,64,768]{3,2,1,0:T(8,128)(2,1)} %get-tuple-element.142), channel_id=1, source_target_pairs={{0,17},{1,16},{8,25},{9,24},{16,1},{17,0},{24,9},{25,8},{2,19},{3,... | collective-permute-start | bytes 2359304 | tf_op jit(solution)/shard_map/ppermute | solution.py:794
  99.5 4.7 %copy-start.25 = (f32[1024,128]{1,0:T(8,128)S(1)}, f32[1024,128]{1,0:T(8,128)}, u32[]{:S(2)}) copy-start(f32[1024,128]{1,0:T(8,128)} %get-tuple-element.111.seg_col_ref) | copy-start | bytes 1572868
  99.5 4.7 %copy-start.30 = (f32[1,1024]{1,0:T(1,128)S(1)}, f32[1,1024]{1,0:T(1,128)}, u32[]{:S(2)}) copy-start(f32[1,1024]{1,0:T(1,128)} %get-tuple-element.112.seg_row_ref) | copy-start | bytes 12292
  99.6 4.7 %copy-start.32 = (s32[3,4]{1,0:T(4,128)S(1)}, s32[3,4]{1,0:T(4,128)}, u32[]{:S(2)}) copy-start(s32[3,4]{1,0:T(4,128)} %get-tuple-element.105.lo_ref) | copy-start | bytes 148
  104.0 30.9 %collective-permute-start.9 = (bf16[4,2,2,32,768]{4,3,2,1,0:T(8,128)(2,1)}, bf16[4,2,2,32,768]{4,3,2,1,0:T(8,128)(2,1)}, u32[]{:S(2)}, u32[]{:S(2)}) collective-permute-start(bf16[4,2,2,32,768]{4,3,2,1,0:T(8,128)(2,1)} %get-tuple-element.153), channel_id=1, source_target_pairs={{0,16},{8,24},{16,0},{24,8},{1,17},{9,25},{17,1},{25,9},{2,18},{10... | collective-permute-start | bytes 2359304 | tf_op jit(solution)/shard_map/ppermute | solution.py:790
  116.0 9.5 %copy-start.17 = (bf16[3,1024,384]{2,1,0:T(8,128)(2,1)}, bf16[3,1024,384]{2,1,0:T(8,128)(2,1)S(1)}, u32[]{:S(2)}) copy-start(bf16[3,1024,384]{2,1,0:T(8,128)(2,1)S(1)} %attn_bwd.2.refs_1_.refs_0_) | copy-start | bytes 7077892
  116.0 9.6 %copy-start.15 = (s32[8]{0:T(128)S(1)}, s32[8]{0:T(128)}, u32[]{:S(2)}) copy-start(s32[8]{0:T(128)} %copy-done.14) | copy-start | bytes 100
  116.0 9.6 %copy-start.27 = (bf16[4,2,64,768]{3,2,1,0:T(8,128)(2,1)S(1)}, bf16[4,2,64,768]{3,2,1,0:T(8,128)(2,1)}, u32[]{:S(2)}) copy-start(bf16[4,2,64,768]{3,2,1,0:T(8,128)(2,1)} %get-tuple-element.139.a_ref) | copy-start | bytes 2359300
  125.5 14.3 %collective-permute-start.10 = (bf16[384,1920]{1,0:T(8,128)(2,1)}, bf16[384,1920]{1,0:T(8,128)(2,1)}, u32[]{:S(2)}, u32[]{:S(2)}) collective-permute-start(bf16[384,1920]{1,0:T(8,128)(2,1)} %get-tuple-element.149), channel_id=1, source_target_pairs={{0,1},{1,0},{2,3},{3,2},{4,5},{5,4},{6,7},{7,6},{8,9},{9,8},{10,11... | collective-permute-start | bytes 4423688 | tf_op jit(solution)/shard_map/ppermute | solution.py:786
  130.1 36.9 %collective-permute-start.11 = (bf16[4,2,2,32,768]{4,3,2,1,0:T(8,128)(2,1)}, bf16[4,2,2,32,768]{4,3,2,1,0:T(8,128)(2,1)}, u32[]{:S(2)}, u32[]{:S(2)}) collective-permute-start(bf16[4,2,2,32,768]{4,3,2,1,0:T(8,128)(2,1)} %get-tuple-element.162), channel_id=1, source_target_pairs={{0,8},{8,0},{16,24},{24,16},{1,9},{9,1},{17,25},{25,17},{2,10},{10... | collective-permute-start | bytes 2359304 | tf_op jit(solution)/shard_map/ppermute | solution.py:790
  142.7 33.2 %all-to-all-start = ((bf16[4,96,1920]{2,1,0:T(8,128)(2,1)}), bf16[4,96,1920]{2,1,0:T(8,128)(2,1)}, u32[]{:S(2)}, u32[]{:S(2)}) async-start(bf16[4,96,1920]{2,1,0:T(8,128)(2,1)} %bitcast.9), calls=%async_computation.1 | async-start | bytes 2949120 | tf_op jit(solution)/shard_map/all_to_all | solution.py:918
  147.0 65.2 %reduce-scatter.8.cloned.1.call-start = ((), (), s32[]{:S(2)}) async-start(), calls=%async_computation.8 | async-start | bytes 983040 | tf_op jit(solution)/shard_map/reduce_scatter | solution.py:970
  147.3 26.2 %collective-permute-start.12 = (bf16[2,2,2,32,768]{4,3,2,1,0:T(8,128)(2,1)}, bf16[2,2,2,32,768]{4,3,2,1,0:T(8,128)(2,1)}, u32[]{:S(2)}, u32[]{:S(2)}) collective-permute-start(bf16[2,2,2,32,768]{4,3,2,1,0:T(8,128)(2,1)} %get-tuple-element.164), channel_id=1, source_target_pairs={{0,16},{8,24},{16,0},{24,8},{1,17},{9,25},{17,1},{25,9},{2,18},{10... | collective-permute-start | bytes 1179656 | tf_op jit(solution)/shard_map/ppermute | solution.py:790
  160.2 6.0 %copy-start.18 = (bf16[3,1024,384]{2,1,0:T(8,128)(2,1)}, bf16[3,1024,384]{2,1,0:T(8,128)(2,1)S(1)}, u32[]{:S(2)}) copy-start(bf16[3,1024,384]{2,1,0:T(8,128)(2,1)S(1)} %attn_bwd.3.refs_1_) | copy-start | bytes 7077892
  166.2 3.1 %copy-start.12 = (f32[1,256]{1,0:T(1,128)S(1)}, f32[1,256]{1,0:T(1,128)}, u32[]{:S(2)}) copy-start(f32[1,256]{1,0:T(1,128)} %copy-done.11) | copy-start | bytes 3076
  166.2 21.3 %collective-permute-start.13 = (bf16[384,1152]{1,0:T(8,128)(2,1)}, bf16[384,1152]{1,0:T(8,128)(2,1)S(1)}, u32[]{:S(2)}, u32[]{:S(2)}) collective-permute-start(bf16[384,1152]{1,0:T(8,128)(2,1)} %get-tuple-element.160), channel_id=1, source_target_pairs={{0,1},{1,0},{2,3},{3,2},{4,5},{5,4},{6,7},{7,6},{8,9},{9,8},{10,11... | collective-permute-start | bytes 2654216 | tf_op jit(solution)/shard_map/ppermute | solution.py:786
  169.3 25.7 %collective-permute-start.15 = (f32[1,256]{1,0:T(1,128)S(1)}, f32[1,256]{1,0:T(1,128)S(1)}, u32[]{:S(2)}, u32[]{:S(2)}) collective-permute-start(f32[1,256]{1,0:T(1,128)S(1)} %copy-done.12), channel_id=1, source_target_pairs={{0,2},{2,0},{4,6},{6,4},{1,3},{3,1},{5,7},{7,5},{8,10},{10,8},{12,... | collective-permute-start | bytes 3080 | tf_op jit(solution)/shard_map/ppermute | solution.py:798
  174.6 23.2 %collective-permute-start.16 = (bf16[2,2,32,768]{3,2,1,0:T(8,128)(2,1)S(1)}, bf16[2,2,32,768]{3,2,1,0:T(8,128)(2,1)S(1)}, u32[]{:S(2)}, u32[]{:S(2)}) collective-permute-start(bf16[2,2,32,768]{3,2,1,0:T(8,128)(2,1)S(1)} %get-tuple-element.177), channel_id=1, source_target_pairs={{0,8},{8,0},{16,24},{24,16},{1,9},{9,1},{17,25},{25,17},{2,10},{10... | collective-permute-start | bytes 589832 | tf_op jit(solution)/shard_map/ppermute | solution.py:790
  175.8 1.7 copy-start.10
  177.4 10.0 %copy-start.16 = (bf16[384,1152]{1,0:T(8,128)(2,1)S(1)}, bf16[384,1152]{1,0:T(8,128)(2,1)}, u32[]{:S(2)}) copy-start(bf16[384,1152]{1,0:T(8,128)(2,1)} %get-tuple-element.170.mine_ref) | copy-start | bytes 2654212
  177.4 16.7 %collective-permute-start.14 = (bf16[96,1920]{1,0:T(8,128)(2,1)S(1)}, bf16[96,1920]{1,0:T(8,128)(2,1)S(1)}, u32[]{:S(2)}, u32[]{:S(2)}) collective-permute-start(bf16[96,1920]{1,0:T(8,128)(2,1)S(1)} %total.2.refs_0_), channel_id=1, source_target_pairs={{0,2},{2,0},{4,6},{6,4},{1,3},{3,1},{5,7},{7,5},{8,10},{10,8},{12,... | collective-permute-start | bytes 1105928 | tf_op jit(solution)/shard_map/ppermute | solution.py:798
  188.7 23.4 %all-to-all-start.1 = ((bf16[4,112,1152]{2,1,0:T(8,128)(2,1)}), bf16[4,112,1152]{2,1,0:T(8,128)(2,1)S(1)}, u32[]{:S(2)}, u32[]{:S(2)}) async-start(bf16[4,112,1152]{2,1,0:T(8,128)(2,1)} %merge_small.1), calls=%async_computation.3 | async-start | bytes 2064384 | tf_op jit(solution)/shard_map/all_to_all | solution.py:918
  195.6 62.3 %collective-permute-start.26 = (f32[1,256]{1,0:T(1,128)}, f32[1,256]{1,0:T(1,128)}, u32[]{:S(2)}, u32[]{:S(2)}) collective-permute-start(f32[1,256]{1,0:T(1,128)} %add.41.refs_0_), channel_id=1, source_target_pairs={{0,6},{6,0},{2,4},{4,2},{1,7},{7,1},{3,5},{5,3},{8,14},{14,8},{10,... | collective-permute-start | bytes 3080 | tf_op jit(solution)/shard_map/ppermute | solution.py:798
  197.7 30.5 %collective-permute-start.21 = (bf16[96,1920]{1,0:T(8,128)(2,1)}, bf16[96,1920]{1,0:T(8,128)(2,1)}, u32[]{:S(2)}, u32[]{:S(2)}) collective-permute-start(bf16[96,1920]{1,0:T(8,128)(2,1)} %add.40.refs_0_), channel_id=1, source_target_pairs={{0,6},{6,0},{2,4},{4,2},{1,7},{7,1},{3,5},{5,3},{8,14},{14,8},{10,... | collective-permute-start | bytes 1105928 | tf_op jit(solution)/shard_map/ppermute | solution.py:798
  198.8 2.7 copy-start.23
  198.8 19.8 %collective-permute-start.19 = (bf16[2,2,2,32,768]{4,3,2,1,0:T(8,128)(2,1)S(1)}, bf16[2,2,2,32,768]{4,3,2,1,0:T(8,128)(2,1)S(1)}, u32[]{:S(2)}, u32[]{:S(2)}) collective-permute-start(bf16[2,2,2,32,768]{4,3,2,1,0:T(8,128)(2,1)S(1)} %stack.24.refs_0_), channel_id=1, source_target_pairs={{0,24},{8,16},{16,8},{24,0},{1,25},{9,17},{17,9},{25,1},{2,26},{10... | collective-permute-start | bytes 1179656 | tf_op jit(solution)/shard_map/ppermute | solution.py:790
  199.8 22.4 %collective-permute-start.18 = (bf16[2,2,2,32,768]{4,3,2,1,0:T(8,128)(2,1)S(1)}, bf16[2,2,2,32,768]{4,3,2,1,0:T(8,128)(2,1)S(1)}, u32[]{:S(2)}, u32[]{:S(2)}) collective-permute-start(bf16[2,2,2,32,768]{4,3,2,1,0:T(8,128)(2,1)S(1)} %stack.24.refs_0_), channel_id=1, source_target_pairs={{0,16},{8,24},{16,0},{24,8},{1,17},{9,25},{17,1},{25,9},{2,18},{10... | collective-permute-start | bytes 1179656 | tf_op jit(solution)/shard_map/ppermute | solution.py:790
  200.8 21.4 %collective-permute-start.17 = (bf16[2,2,2,32,768]{4,3,2,1,0:T(8,128)(2,1)S(1)}, bf16[2,2,2,32,768]{4,3,2,1,0:T(8,128)(2,1)S(1)}, u32[]{:S(2)}, u32[]{:S(2)}) collective-permute-start(bf16[2,2,2,32,768]{4,3,2,1,0:T(8,128)(2,1)S(1)} %stack.24.refs_0_), channel_id=1, source_target_pairs={{0,8},{8,0},{16,24},{24,16},{1,9},{9,1},{17,25},{25,17},{2,10},{10... | collective-permute-start | bytes 1179656 | tf_op jit(solution)/shard_map/ppermute | solution.py:790
  214.1 44.4 %all-to-all-start.2 = ((bf16[4,1,2,2,32,768]{5,4,3,2,1,0:T(8,128)(2,1)}), bf16[4,1,2,2,32,768]{5,4,3,2,1,0:T(8,128)(2,1)}, u32[]{:S(2)}, u32[]{:S(2)}) async-start(bf16[4,1,2,2,32,768]{5,4,3,2,1,0:T(8,128)(2,1)} %copies.1), calls=%async_computation.5 | async-start | bytes 1572864 | tf_op jit(solution)/shard_map/all_to_all | solution.py:918
  218.6 8.0 %collective-permute-start.20 = (bf16[112,1152]{1,0:T(8,128)(2,1)S(1)}, bf16[112,1152]{1,0:T(8,128)(2,1)S(1)}, u32[]{:S(2)}, u32[]{:S(2)}) collective-permute-start(bf16[112,1152]{1,0:T(8,128)(2,1)S(1)} %total.3.refs_0_), channel_id=1, source_target_pairs={{0,2},{2,0},{4,6},{6,4},{1,3},{3,1},{5,7},{7,5},{8,10},{10,8},{12,... | collective-permute-start | bytes 774152 | tf_op jit(solution)/shard_map/ppermute | solution.py:798
  226.6 12.4 %collective-permute-start.22 = (bf16[112,1152]{1,0:T(8,128)(2,1)S(1)}, bf16[112,1152]{1,0:T(8,128)(2,1)S(1)}, u32[]{:S(2)}, u32[]{:S(2)}) collective-permute-start(bf16[112,1152]{1,0:T(8,128)(2,1)S(1)} %add.43.refs_0_), channel_id=1, source_target_pairs={{0,6},{6,0},{2,4},{4,2},{1,7},{7,1},{3,5},{5,3},{8,14},{14,8},{10,... | collective-permute-start | bytes 774152 | tf_op jit(solution)/shard_map/ppermute | solution.py:798
  229.5 12.1 %collective-permute-start.25 = (bf16[96,1920]{1,0:T(8,128)(2,1)S(1)}, bf16[96,1920]{1,0:T(8,128)(2,1)S(1)}, u32[]{:S(2)}, u32[]{:S(2)}) collective-permute-start(bf16[96,1920]{1,0:T(8,128)(2,1)S(1)} %add.44.refs_0_), channel_id=1, source_target_pairs={{0,24},{8,16},{16,8},{24,0},{1,25},{9,17},{17,9},{25,1},{2,26},{10... | collective-permute-start | bytes 1105928 | tf_op jit(solution)/shard_map/ppermute | solution.py:790
  231.6 19.2 %collective-permute-start.24 = (bf16[96,1920]{1,0:T(8,128)(2,1)S(1)}, bf16[96,1920]{1,0:T(8,128)(2,1)S(1)}, u32[]{:S(2)}, u32[]{:S(2)}) collective-permute-start(bf16[96,1920]{1,0:T(8,128)(2,1)S(1)} %add.44.refs_0_), channel_id=1, source_target_pairs={{0,16},{8,24},{16,0},{24,8},{1,17},{9,25},{17,1},{25,9},{2,18},{10... | collective-permute-start | bytes 1105928 | tf_op jit(solution)/shard_map/ppermute | solution.py:790
  231.9 20.5 %collective-permute-start.23 = (bf16[96,1920]{1,0:T(8,128)(2,1)S(1)}, bf16[96,1920]{1,0:T(8,128)(2,1)S(1)}, u32[]{:S(2)}, u32[]{:S(2)}) collective-permute-start(bf16[96,1920]{1,0:T(8,128)(2,1)S(1)} %add.44.refs_0_), channel_id=1, source_target_pairs={{0,8},{8,0},{16,24},{24,16},{1,9},{9,1},{17,25},{25,17},{2,10},{10... | collective-permute-start | bytes 1105928 | tf_op jit(solution)/shard_map/ppermute | solution.py:790
  239.8 22.9 %collective-permute-start.29 = (bf16[112,1152]{1,0:T(8,128)(2,1)}, bf16[112,1152]{1,0:T(8,128)(2,1)}, u32[]{:S(2)}, u32[]{:S(2)}) collective-permute-start(bf16[112,1152]{1,0:T(8,128)(2,1)} %add.45.refs_0_), channel_id=1, source_target_pairs={{0,24},{8,16},{16,8},{24,0},{1,25},{9,17},{17,9},{25,1},{2,26},{10... | collective-permute-start | bytes 774152 | tf_op jit(solution)/shard_map/ppermute | solution.py:790
  241.6 21.1 %collective-permute-start.28 = (bf16[112,1152]{1,0:T(8,128)(2,1)}, bf16[112,1152]{1,0:T(8,128)(2,1)}, u32[]{:S(2)}, u32[]{:S(2)}) collective-permute-start(bf16[112,1152]{1,0:T(8,128)(2,1)} %add.45.refs_0_), channel_id=1, source_target_pairs={{0,16},{8,24},{16,0},{24,8},{1,17},{9,25},{17,1},{25,9},{2,18},{10... | collective-permute-start | bytes 774152 | tf_op jit(solution)/shard_map/ppermute | solution.py:790
  250.9 11.9 %collective-permute-start.27 = (bf16[112,1152]{1,0:T(8,128)(2,1)}, bf16[112,1152]{1,0:T(8,128)(2,1)}, u32[]{:S(2)}, u32[]{:S(2)}) collective-permute-start(bf16[112,1152]{1,0:T(8,128)(2,1)} %add.45.refs_0_), channel_id=1, source_target_pairs={{0,8},{8,0},{16,24},{24,16},{1,9},{9,1},{17,25},{25,17},{2,10},{10... | collective-permute-start | bytes 774152 | tf_op jit(solution)/shard_map/ppermute | solution.py:790
  253.7 4.8 %copy-start.1 = (s32[4]{0:T(128)S(1)}, s32[4]{0:T(128)}, u32[]{:S(2)}) copy-start(s32[4]{0:T(128)} %pad_add_fusion.place_ref.c_ref) | copy-start | bytes 52
  253.7 4.8 %copy-start.20 = (bf16[4,2,2,2,32,768]{5,4,3,2,1,0:T(8,128)(2,1)S(1)}, bf16[4,2,2,2,32,768]{5,4,3,2,1,0:T(8,128)(2,1)}, u32[]{:S(2)}) copy-start(bf16[4,2,2,2,32,768]{5,4,3,2,1,0:T(8,128)(2,1)} %copy-done.19) | copy-start | bytes 4718596
  253.7 13.5 %collective-permute-start.30 = (bf16[4,96,1920]{2,1,0:T(8,128)(2,1)}, bf16[4,96,1920]{2,1,0:T(8,128)(2,1)}, u32[]{:S(2)}, u32[]{:S(2)}) collective-permute-start(bf16[4,96,1920]{2,1,0:T(8,128)(2,1)} %stack.26.refs_0_), channel_id=1, source_target_pairs={{0,1},{1,0},{2,3},{3,2},{4,5},{5,4},{6,7},{7,6},{8,9},{9,8},{10,11... | collective-permute-start | bytes 4423688 | tf_op jit(solution)/shard_map/ppermute | solution.py:786
  264.2 3.0 %collective-permute-start.31 = (bf16[4,112,1152]{2,1,0:T(8,128)(2,1)S(1)}, bf16[4,112,1152]{2,1,0:T(8,128)(2,1)S(1)}, u32[]{:S(2)}, u32[]{:S(2)}) collective-permute-start(bf16[4,112,1152]{2,1,0:T(8,128)(2,1)S(1)} %stack.27.refs_2_), channel_id=1, source_target_pairs={{0,1},{1,0},{2,3},{3,2},{4,5},{5,4},{6,7},{7,6},{8,9},{9,8},{10,11... | collective-permute-start | bytes 3096584 | tf_op jit(solution)/shard_map/ppermute | solution.py:786
  (7 other events, 6.9 us)
Sparse Core Ops, SparseCore 0:
  69.9 67.4 reduce-scatter.3
  139.7 20.7 reduce-scatter.5
  169.4 26.5 reduce-scatter.7
